TPU v7x, 512 devices: a whole 4x4x16 slice. The times are simulated.
512 devices in a mesh: grid: 64 (over y_lo, z, core), dp: 8 (over y_hi, x).
Axes of the slice: x: 4, y: 4 (y_hi: 2, y_lo: 2; y = y_hi * 2 + y_lo), z: 16, core: 2. Of those that a mesh axis runs over, the one named last changes fastest.
Arguments:
- field: bfloat16 [65536, 1024], P('grid', 'dp'), may hold values from -6 to 6
- cotangent: bfloat16 [65536, 1024], P('grid', 'dp'), may hold values from -6 to 6
- mode_blocks: int32 [8], replicated, may hold values from 0 to 4095, as said below
- spectral: bfloat16 [2, 64, 64, 64], P(None, 'grid'), may hold values from -6 to 6
- w_in: bfloat16 [64, 256], replicated, may hold values from -0.75 to 0.75
- b_in: float32 [256], replicated, may hold values from -3 to 3
- w_out: bfloat16 [256, 64], replicated, may hold values from -0.375 to 0.375
- b_out: float32 [64], replicated, may hold values from -3 to 3
Outputs:
- output: bfloat16 [65536, 1024], P('grid', 'dp')
- field_grad: bfloat16 [65536, 1024], P('grid', 'dp')
- spectral_grad: float32 [2, 64, 64, 64], P(None, 'grid')
- w_in_grad: float32 [64, 256], replicated
- b_in_grad: float32 [256], replicated
- w_out_grad: float32 [256, 64], replicated
- b_out_grad: float32 [64], replicated
Inputs may be any that keep to these rules, and one draw needn't show every extreme that they name: `mode_blocks`: distinct block numbers; 0 and 4095 are always among them.
All inputs are finite; a program needn't handle non-finite values.
Results may differ from a plain program's by a relative error of at most 0.013.
Values may be sent and summed in bfloat16 or wider, within the bound.
No kernel may reach another device: no remote copies, remote signals or barrier semaphores. Data moves between devices by JAX's collectives and lax.ppermute only.
A program may use at most 64 MiB of HBM per device.

v0:
```python
import math

import jax
import jax.numpy as jnp
from jax import lax
from jax.sharding import PartitionSpec as P

NX = 65536
BLK = 8


def mode_list(mode_blocks, block_width):
    offsets = jnp.arange(block_width, dtype=jnp.int32)
    return (mode_blocks[:, None] * block_width + offsets[None, :]).reshape(-1)


def forward_table(modes, first_row, count, length):
    rows_here = first_row + jnp.arange(count, dtype=jnp.int32)
    product = modes[:, None] * rows_here[None, :] % length
    phase = product.astype(jnp.float32) * (2.0 * math.pi / length)
    scale = 1.0 / math.sqrt(length)
    table = jnp.stack([jnp.cos(phase) * scale, -jnp.sin(phase) * scale], axis=1)
    return table.reshape(2 * modes.shape[0], count).astype(jnp.bfloat16)


def inverse_table(forward):
    return (forward.astype(jnp.float32) * 2.0).astype(jnp.bfloat16).T


def gelu_grad(pre):
    _, pull = jax.vjp(jax.nn.gelu, pre)
    return pull(jnp.ones_like(pre))[0]


def mix(real, imag, weight_re, weight_im):
    best = lax.Precision.HIGHEST
    out_re = jnp.einsum("kbi,kio->kbo", real, weight_re, precision=best) - jnp.einsum(
        "kbi,kio->kbo", imag, weight_im, precision=best
    )
    out_im = jnp.einsum("kbi,kio->kbo", real, weight_im, precision=best) + jnp.einsum(
        "kbi,kio->kbo", imag, weight_re, precision=best
    )
    return (out_re, out_im)


def mix_grads(real, imag, grad_re, grad_im, weight_re, weight_im):
    best = lax.Precision.HIGHEST
    w_re = jnp.einsum("kbi,kbo->kio", real, grad_re, precision=best) + jnp.einsum(
        "kbi,kbo->kio", imag, grad_im, precision=best
    )
    w_im = jnp.einsum("kbi,kbo->kio", real, grad_im, precision=best) - jnp.einsum(
        "kbi,kbo->kio", imag, grad_re, precision=best
    )
    in_re = jnp.einsum("kbo,kio->kbi", grad_re, weight_re, precision=best) + jnp.einsum(
        "kbo,kio->kbi", grad_im, weight_im, precision=best
    )
    in_im = jnp.einsum("kbo,kio->kbi", grad_im, weight_re, precision=best) - jnp.einsum(
        "kbo,kio->kbi", grad_re, weight_im, precision=best
    )
    return (w_re, w_im, in_re, in_im)


def pointwise_pass(field, spec, cotangent, w_in, b_in, w_out, b_out):
    chans = w_in.shape[0]
    shape = field.shape
    spec_rows = spec.reshape(-1, chans)
    pre = jnp.dot(spec_rows, w_in, preferred_element_type=jnp.float32) + b_in
    hidden = jax.nn.gelu(pre).astype(jnp.bfloat16)
    out = jnp.dot(hidden, w_out, preferred_element_type=jnp.float32) + b_out
    result = (
        (field.reshape(-1, chans).astype(jnp.float32) + out).astype(jnp.bfloat16).reshape(shape)
    )
    upstream = cotangent.reshape(-1, chans)
    grad_w_out = jnp.einsum("nh,nc->hc", hidden, upstream, preferred_element_type=jnp.float32)
    grad_b_out = jnp.sum(upstream.astype(jnp.float32), axis=0)
    grad_hidden = jnp.einsum("nc,hc->nh", upstream, w_out, preferred_element_type=jnp.float32)
    grad_pre = (grad_hidden * gelu_grad(pre)).astype(jnp.bfloat16)
    grad_w_in = jnp.einsum("nc,nh->ch", spec_rows, grad_pre, preferred_element_type=jnp.float32)
    grad_b_in = jnp.sum(grad_pre.astype(jnp.float32), axis=0)
    grad_spec = (
        jnp.einsum("nh,ch->nc", grad_pre, w_in, preferred_element_type=jnp.float32)
        .astype(jnp.bfloat16)
        .reshape(shape)
    )
    return (result, grad_spec, (grad_w_in, grad_b_in, grad_w_out, grad_b_out))


def local(field, cotangent, mode_blocks, spectral, w_in, b_in, w_out, b_out):
    rows = field.shape[0]
    width = field.shape[1]
    chans = w_in.shape[0]
    ncol = width // chans
    own = spectral.shape[1]
    modes = mode_list(mode_blocks, BLK)
    columns_total = ncol * lax.axis_size("dp")
    first = lax.axis_index("grid") * rows
    forward_here = forward_table(modes, first, rows, NX)
    inverse_here = inverse_table(forward_here)
    weight_re = spectral[0].astype(jnp.float32)
    weight_im = spectral[1].astype(jnp.float32)
    part = forward_here
    modal = lax.psum_scatter(
        jnp.dot(part, field, preferred_element_type=jnp.float32).reshape(
            own * lax.axis_size("grid"), 2 * width
        ),
        "grid",
        scatter_dimension=0,
        tiled=True,
    ).reshape(own, 2, ncol, chans)
    real = modal[:, 0]
    imag = modal[:, 1]
    out_re, out_im = mix(real, imag, weight_re, weight_im)
    mixed = jnp.stack([out_re, out_im], axis=1).reshape(own, 2 * width).astype(jnp.bfloat16)
    piece = lax.all_gather(mixed, "grid", axis=0, tiled=True)
    count = piece.shape[0]
    part = inverse_here
    spec = jnp.dot(
        part, piece.reshape(2 * count, width), preferred_element_type=jnp.float32
    ).astype(jnp.bfloat16)
    output, grad_spec, sums = pointwise_pass(field, spec, cotangent, w_in, b_in, w_out, b_out)
    part = inverse_here
    grad_modal = lax.psum_scatter(
        jnp.einsum("rm,rw->mw", part, grad_spec, preferred_element_type=jnp.float32).reshape(
            own * lax.axis_size("grid"), 2 * width
        ),
        "grid",
        scatter_dimension=0,
        tiled=True,
    ).reshape(own, 2, ncol, chans)
    w_re, w_im, in_re, in_im = mix_grads(
        real, imag, grad_modal[:, 0], grad_modal[:, 1], weight_re, weight_im
    )
    grad_in = jnp.stack([in_re, in_im], axis=1).reshape(own, 2 * width).astype(jnp.bfloat16)
    piece = lax.all_gather(grad_in, "grid", axis=0, tiled=True)
    count = piece.shape[0]
    part = forward_here
    back = jnp.einsum(
        "mr,mw->rw", part, piece.reshape(2 * count, width), preferred_element_type=jnp.float32
    )
    field_grad = (cotangent.astype(jnp.float32) + back).astype(jnp.bfloat16)
    spectral_part = jnp.stack([w_re, w_im], axis=0)
    spectral_sum = lax.psum(spectral_part.astype(jnp.bfloat16), "dp").astype(jnp.float32)
    grad_w_in, grad_b_in, grad_w_out, grad_b_out = lax.psum(
        (sums[0], sums[1], sums[2], sums[3]), ("grid", "dp")
    )
    inv_cols = 1.0 / columns_total
    return (
        output,
        field_grad,
        spectral_sum * inv_cols,
        grad_w_in * inv_cols,
        grad_b_in * inv_cols,
        grad_w_out * inv_cols,
        grad_b_out * inv_cols,
    )


def solution(mesh):
    in_specs = (
        P("grid", "dp"),
        P("grid", "dp"),
        P(),
        P(None, "grid", None, None),
        P(),
        P(),
        P(),
        P(),
    )
    out_specs = (P("grid", "dp"), P("grid", "dp"), P(None, "grid", None, None), P(), P(), P(), P())
    return jax.shard_map(local, mesh=mesh, in_specs=in_specs, out_specs=out_specs, check_vma=False)
```

profile of v0, /device:TPU:1, one launch (start us, length us, event | category | flops | bytes accessed | tf_op | source)
XLA Modules:
  0.0 1456.2 jit_solution(12951280648803934894)
XLA Ops:
  7.3 0.7 broadcast_multiply_fusion.4
  8.1 1.2 cosine_multiply_fusion
  9.4 0.3 copy.27
  9.8 0.2 fusion.47
  10.0 0.6 reshape.368
  10.8 0.2 reshape.377
  11.0 0.3 convert_reduce_fusion.1
  11.3 0.2 reshape.384
  11.5 0.3 copy.26
  11.9 0.3 copy.28
  12.2 1.3 dynamic-slice
  13.5 363.8 %all-reduce.8.cloned.1.call-done = f32[64,256]{1,0:T(8,128)} async-done(((f32[64,256]{1,0:T(8,128)}), f32[64,256]{1,0:T(8,128)}) %all-reduce.8.cloned.1.call-update) | async-done | bytes 65552
  377.3 1.4 dynamic-slice_reduce_fusion.1
  379.4 61.0 %all-gather = bf16[64,1,256]{2,1,0:T(2,128)(2,1)S(1)} all-gather(bf16[1,1,256]{2,1,0:T(2,128)(2,1)S(1)} %reshape.385), channel_id=1, replica_groups=mesh['grid'=64,'dp'=8] {'grid'}, dimensions={0}, use_global_device_ids=true | all-gather | bytes 33280 | tf_op jit(solution)/shard_map/all_gather | solution.py:114
  440.3 0.2 reduce.1
  440.5 0.3 convolution_convert_fusion.1
  440.8 0.2 reshape.375
  441.1 0.9 multiply_convert_fusion
  442.0 1.5 convert_reduce_fusion
  443.5 0.9 fusion.49
  444.4 0.4 convolution_convert_fusion
  444.9 0.9 fusion.50
  445.8 0.3 copy.30
  446.1 0.3 reshape.378
  446.4 0.2 fusion.48
  446.6 101.6 %all-reduce.2 = (f32[256]{0:T(256)S(1)}, f32[64]{0:T(128)S(1)}) all-reduce(f32[256]{0:T(256)S(1)} %get-tuple-element.17, f32[64]{0:T(128)S(1)} %convert_reduce_fusion.1), channel_id=1, replica_groups=mesh['grid'=64,'dp'=8] {'grid','dp'}, use_global_device_ids=true, to_apply=%region_5.6 | all-reduce | flops 320 | bytes 2560 | tf_op jit(solution)/shard_map/psum | solution.py:143
  548.2 0.6 broadcast_multiply_fusion.2
  548.8 0.4 fusion.2
  549.3 0.5 broadcast_multiply_fusion.3
  549.8 0.6 reshape.379
  550.5 0.3 copy.29
  550.7 1.0 reshape.376
  551.7 437.2 %all-reduce.12.cloned.1.call-done = (f32[64,256]{1,0:T(8,128)}, f32[256,64]{0,1:T(8,128)}) async-done(((f32[64,256]{1,0:T(8,128)}, f32[256,64]{0,1:T(8,128)}), (f32[64,256]{1,0:T(8,128)}, f32[256,64]{0,1:T(8,128)})) %all-reduce.12.cloned.1.call-update) | async-done | bytes 131088 | tf_op jit(solution)/shard_map/psum | solution.py:143
  988.9 1.5 broadcast_multiply_fusion
  990.4 1.5 broadcast_multiply_fusion.1
  991.9 351.2 %all-reduce.10.cloned.1.call-done = f32[64,256]{1,0:T(8,128)} async-done(((f32[64,256]{1,0:T(8,128)}), f32[64,256]{1,0:T(8,128)}) %all-reduce.10.cloned.1.call-update) | async-done | bytes 65552
  1343.1 1.4 dynamic-slice_reduce_fusion
  1344.5 0.2 fusion.46
  1344.8 0.2 fusion.45
  1345.1 0.1 fusion.30
  1345.3 0.3 fusion.13
  1345.6 0.2 fusion.12
  1345.8 34.1 %psum.35 = bf16[2,1,64,64]{3,2,1,0:T(8,128)(2,1)S(1)} all-reduce(bf16[2,1,64,64]{3,2,1,0:T(8,128)(2,1)S(1)} %pad_maximum_fusion), channel_id=1, replica_groups=mesh['grid'=64,'dp'=8] {'dp'}, use_global_device_ids=true, to_apply=%region_2.3 | all-reduce | flops 8192 | bytes 32768 | tf_op jit(solution)/shard_map/psum | solution.py:142
  1380.0 0.6 convert_multiply_fusion
  1380.7 0.1 fusion.18
  1381.0 67.5 %all-gather.1 = bf16[64,1,256]{2,1,0:T(2,128)(2,1)S(1)} all-gather(bf16[1,1,256]{2,1,0:T(2,128)(2,1)S(1)} %reshape.387), channel_id=1, replica_groups=mesh['grid'=64,'dp'=8] {'grid'}, dimensions={0}, use_global_device_ids=true | all-gather | bytes 33280 | tf_op jit(solution)/shard_map/all_gather | solution.py:134
  1448.5 0.2 reduce.3
  1448.7 1.0 fusion.9
  (41 shorter events, 1.8 us)
Async XLA Ops:
  7.2 433.9 %copy-start = (bf16[64,256]{1,0:T(8,128)(2,1)S(1)}, bf16[64,256]{1,0:T(8,128)(2,1)}, u32[]{:S(2)}) copy-start(bf16[64,256]{1,0:T(8,128)(2,1)} %param.12) | copy-start | bytes 98308
  7.2 2.6 copy-start.2
  7.2 3.6 copy-start.1
  7.2 370.1 %all-reduce.8.cloned.1.call-start = ((), (), s32[]{:S(2)}) async-start(), calls=%async_computation | async-start | bytes 131072
  10.7 978.2 %all-reduce.12.cloned.1.call-start = ((), (), s32[]{:S(2)}) async-start(), calls=%async_computation.2 | async-start | bytes 262144 | tf_op jit(solution)/shard_map/psum | solution.py:143
  11.3 367.4 %copy-start.3 = (bf16[2,1,64,64]{3,2,1,0:T(8,128)(2,1)S(1)}, bf16[2,1,64,64]{3,2,1,0:T(8,128)(2,1)}, u32[]{:S(2)}) copy-start(bf16[2,1,64,64]{3,2,1,0:T(8,128)(2,1)} %param.11) | copy-start | bytes 49156
  11.5 429.6 %copy-start.6 = (f32[256]{0:T(256)S(1)}, f32[256]{0:T(256)}, u32[]{:S(2)}) copy-start(f32[256]{0:T(256)} %param.13) | copy-start | bytes 3076
  441.1 0.9 copy-start.4
  444.9 104.0 %copy-start.5 = (f32[64]{0:T(128)S(1)}, f32[64]{0:T(128)}, u32[]{:S(2)}) copy-start(f32[64]{0:T(128)} %param.15) | copy-start | bytes 772
  548.8 794.3 %all-reduce.10.cloned.1.call-start = ((), (), s32[]{:S(2)}) async-start(), calls=%async_computation.1 | async-start | bytes 131072
Sparse Core Ops, SparseCore 0:
  11.5 365.7 all-reduce.7
  548.9 439.9 all-reduce.11
  992.4 350.6 all-reduce.9
where the time goes:
time: 1460 us
  waiting for transfers between devices  1150 us (79%)
  blocking collectives  264 us (18%)
    unnamed x5, waiting for transfers between devices  715 us
    psum x1, waiting for transfers between devices, local(): lax.psum((sums[0], sums[1], sums[2], sums[3]), ('grid', 'dp'))  437 us
    psum x1, blocking collectives, local(): lax.psum((sums[0], sums[1], sums[2], sums[3]), ('grid', 'dp'))  102 us
    all_gather x1, blocking collectives, local(): piece = lax.all_gather(grad_in, 'grid', axis=0, tiled=True)  67.5 us
    all_gather x1, blocking collectives, local(): piece = lax.all_gather(mixed, 'grid', axis=0, tiled=True)  61 us
    psum x1, blocking collectives, local(): lax.psum(spectral_part.astype(jnp.bfloat16), 'dp').astype(jnp.float32)  34.1 us
  transfers between devices with their start and end apart: 3, of which 3 were waited for; matrix products, arithmetic and copies ran while one was open for 1% of the time, Pallas kernels for 0%

commit v1 on v0

v1 whole, which is shorter than its diff:
```python
import math

import jax
import jax.numpy as jnp
from jax import lax
from jax.sharding import PartitionSpec as P

NX = 65536
BLK = 8


def mode_list(mode_blocks, block_width):
    offsets = jnp.arange(block_width, dtype=jnp.int32)
    return (mode_blocks[:, None] * block_width + offsets[None, :]).reshape(-1)


def forward_table(modes, first_row, count, length):
    rows_here = first_row + jnp.arange(count, dtype=jnp.int32)
    product = modes[:, None] * rows_here[None, :] % length
    phase = product.astype(jnp.float32) * (2.0 * math.pi / length)
    scale = 1.0 / math.sqrt(length)
    table = jnp.stack([jnp.cos(phase) * scale, -jnp.sin(phase) * scale], axis=1)
    return table.reshape(2 * modes.shape[0], count).astype(jnp.bfloat16)


def gelu_grad(pre):
    _, pull = jax.vjp(jax.nn.gelu, pre)
    return pull(jnp.ones_like(pre))[0]


def exchange(x, axis):
    return lax.all_to_all(x, axis, 0, 0, tiled=True)


def complex_mix(real, imag, weight_re, weight_im):
    best = lax.Precision.HIGHEST
    left = jnp.concatenate([real, imag], axis=0)
    by_re = jnp.dot(left, weight_re, precision=best)
    by_im = jnp.dot(left, weight_im, precision=best)
    n = real.shape[0]
    return by_re[:n] - by_im[n:], by_im[:n] + by_re[n:]


def complex_outer(real, imag, grad_re, grad_im):
    best = lax.Precision.HIGHEST
    w_re = jnp.dot(real.T, grad_re, precision=best) + jnp.dot(imag.T, grad_im, precision=best)
    w_im = jnp.dot(real.T, grad_im, precision=best) - jnp.dot(imag.T, grad_re, precision=best)
    return w_re, w_im


def local(field, cotangent, mode_blocks, spectral, w_in, b_in, w_out, b_out):
    rows, width = field.shape
    chans, hid = w_in.shape
    ncol = width // chans
    grid = lax.axis_size("grid")
    dp = lax.axis_size("dp")
    modes = mode_list(mode_blocks, BLK)
    first = lax.axis_index("grid") * rows
    table = forward_table(modes, first, rows, NX)
    twice = (table.astype(jnp.float32) * 2.0).astype(jnp.bfloat16)
    weight_re = spectral[0, 0].astype(jnp.float32)
    weight_im = spectral[1, 0].astype(jnp.float32)

    modal = jnp.dot(table, field, preferred_element_type=jnp.float32)
    modal = jnp.sum(exchange(modal.reshape(grid, 2, width), "grid"), axis=0)
    real = modal[0].reshape(ncol, chans)
    imag = modal[1].reshape(ncol, chans)
    out_re, out_im = complex_mix(real, imag, weight_re, weight_im)
    mixed = jnp.stack([out_re.reshape(width), out_im.reshape(width)]).astype(jnp.bfloat16)
    piece = exchange(jnp.broadcast_to(mixed[None], (grid, 2, width)), "grid").reshape(2 * grid, width)

    spec = jnp.einsum("mr,mw->rw", twice, piece, preferred_element_type=jnp.float32).astype(jnp.bfloat16)
    spec_rows = spec.reshape(-1, chans)
    pre = jnp.dot(spec_rows, w_in, preferred_element_type=jnp.float32) + b_in
    hidden = jax.nn.gelu(pre).astype(jnp.bfloat16)
    out = jnp.dot(hidden, w_out, preferred_element_type=jnp.float32) + b_out
    output = (field.astype(jnp.float32) + out.reshape(field.shape)).astype(jnp.bfloat16)
    upstream = cotangent.reshape(-1, chans)
    grad_w_out = jnp.einsum("nh,nc->hc", hidden, upstream, preferred_element_type=jnp.float32)
    grad_b_out = jnp.sum(upstream.astype(jnp.float32), axis=0)
    grad_hidden = jnp.einsum("nc,hc->nh", upstream, w_out, preferred_element_type=jnp.float32)
    grad_pre = (grad_hidden * gelu_grad(pre)).astype(jnp.bfloat16)
    grad_w_in = jnp.einsum("nc,nh->ch", spec_rows, grad_pre, preferred_element_type=jnp.float32)
    grad_b_in = jnp.sum(grad_pre.astype(jnp.float32), axis=0)
    grad_spec = (
        jnp.einsum("nh,ch->nc", grad_pre, w_in, preferred_element_type=jnp.float32)
        .astype(jnp.bfloat16)
        .reshape(field.shape)
    )
    grad_modal = jnp.dot(twice, grad_spec, preferred_element_type=jnp.float32)

    biases = jnp.concatenate([grad_b_in, grad_b_out]).reshape(grid, 1, -1)
    biases = jnp.pad(biases, ((0, 0), (0, 0), (0, width - biases.shape[2])))
    parts = jnp.concatenate(
        [
            grad_modal.reshape(grid, 2, width),
            grad_w_in.reshape(grid, -1, width),
            grad_w_out.reshape(grid, -1, width),
            biases,
        ],
        axis=1,
    )
    sums = jnp.sum(exchange(parts, "grid"), axis=0)
    d_re = sums[0].reshape(ncol, chans)
    d_im = sums[1].reshape(ncol, chans)
    w_re, w_im = complex_outer(real, imag, d_re, d_im)
    in_re, in_im = complex_mix(d_re, d_im, weight_re.T, -weight_im.T)

    feed = sums[2:]
    high = lax.reduce_precision(feed, 8, 7)
    low = feed - high
    share = jnp.concatenate(
        [
            w_re.reshape(-1, width).astype(jnp.bfloat16),
            w_im.reshape(-1, width).astype(jnp.bfloat16),
            high.astype(jnp.bfloat16),
            low.astype(jnp.bfloat16),
        ],
        axis=0,
    )
    shares = exchange(jnp.broadcast_to(share[None], (dp,) + share.shape), "dp")
    total = jnp.sum(shares.astype(jnp.float32), axis=0)
    inv_cols = 1.0 / (ncol * dp)
    nspec = 2 * chans * chans // width
    spectral_grad = (total[:nspec] * inv_cols).reshape(2, 1, chans, chans)
    nfeed = feed.shape[0]
    feed = (total[nspec : nspec + nfeed] + total[nspec + nfeed :]) * inv_cols

    own = jnp.concatenate(
        [jnp.stack([in_re.reshape(width), in_im.reshape(width)]), feed], axis=0
    ).astype(jnp.bfloat16)
    every = exchange(jnp.broadcast_to(own[None], (grid,) + own.shape), "grid")
    grad_in = every[:, :2].reshape(2 * grid, width)
    back = jnp.einsum("mr,mw->rw", table, grad_in, preferred_element_type=jnp.float32)
    field_grad = (cotangent.astype(jnp.float32) + back).astype(jnp.bfloat16)
    nrow = chans * hid // (grid * width)
    feeds = every[:, 2:].astype(jnp.float32)
    w_in_grad = feeds[:, :nrow].reshape(chans, hid)
    w_out_grad = feeds[:, nrow : 2 * nrow].reshape(hid, chans)
    flat = feeds[:, 2 * nrow, : (hid + chans) // grid].reshape(-1)
    return (output, field_grad, spectral_grad, w_in_grad, flat[:hid], w_out_grad, flat[hid:])


def solution(mesh):
    in_specs = (
        P("grid", "dp"),
        P("grid", "dp"),
        P(),
        P(None, "grid", None, None),
        P(),
        P(),
        P(),
        P(),
    )
    out_specs = (P("grid", "dp"), P("grid", "dp"), P(None, "grid", None, None), P(), P(), P(), P())
    return jax.shard_map(local, mesh=mesh, in_specs=in_specs, out_specs=out_specs, check_vma=False)
```

time: 1460 us -> 141 us (0.10)
  waiting for transfers between devices: 1150 us -> 71.3 us
  blocking collectives: 264 us -> 0 us
  starting transfers between devices: 0.12 us -> 38.4 us
    unnamed x5 -> x0, waiting for transfers between devices: 715 us -> none
    psum x1 -> x0, waiting for transfers between devices: 437 us -> none  [local(): lax.psum((sums[0], sums[1], sums[2], sums[3]), ('grid', 'dp'))]
    psum x2 -> x0, blocking collectives: 136 us -> none  [the longest x1 102 us: local(): lax.psum((sums[0], sums[1], sums[2], sums[3]), ('grid', 'dp'))]
    all_gather x2 -> x0, blocking collectives: 128 us -> none  [the longest x1 67.5 us: local(): piece = lax.all_gather(grad_in, 'grid', axis=0, tiled=True)]
    all_to_all x0 -> x5, waiting for transfers between devices: none -> 71.3 us  [exchange(): return lax.all_to_all(x, axis, 0, 0, tiled=True)]
    all_to_all x0 -> x5, starting transfers between devices: none -> 38.4 us  [exchange(): return lax.all_to_all(x, axis, 0, 0, tiled=True)]
  transfers between devices with their start and end apart: 3 -> 5, of which waited for: 3 -> 5; matrix products, arithmetic and copies ran while one was open for 1% -> 3% of each run, Pallas kernels for 0% -> 0%
where the time goes in v1:
time: 141 us; the launch traced here: 140 us
  waiting for transfers between devices  71.3 us (51%)
  starting transfers between devices  38.4 us (27%)
  local copies, waits for them, and re-layouts  11.9 us (8%)
  matrix products  11.4 us (8%)
  other arithmetic  6.33 us (4%)
    all_to_all x5, waiting for transfers between devices, exchange(): return lax.all_to_all(x, axis, 0, 0, tiled=True)  71.3 us
    all_to_all x5, starting transfers between devices, exchange(): return lax.all_to_all(x, axis, 0, 0, tiled=True)  38.4 us
    dot_general x1, matrix products, local(): jnp.einsum('nc,hc->nh', upstream, w_out, preferred_element_type=jnp.float32)  3.36 us
    convert_element_type x1, other arithmetic, local(): grad_pre = (grad_hidden * gelu_grad(pre)).astype(jnp.bfloat16)  2.92 us
  transfers between devices with their start and end apart: 5, of which 5 were waited for; matrix products, arithmetic and copies ran while one was open for 3% of the time, Pallas kernels for 0%

profile of v1, /device:TPU:1, one launch (start us, length us, event | category | flops | bytes accessed | tf_op | source)
XLA Modules:
  0.0 140.4 jit_solution(14302567793977667854)
XLA Ops:
  0.7 0.7 broadcast_multiply_fusion
  1.5 1.2 multiply_convert_fusion.3
  2.8 1.2 fusion.27
  4.0 0.7 copy.57
  4.7 18.2 %all-to-all-start = ((f32[64,2,128]{2,1,0:T(2,128)}), f32[64,2,128]{2,1,0:T(2,128)S(1)}, u32[]{:S(2)}, u32[]{:S(2)}) async-start(f32[64,2,128]{2,1,0:T(2,128)} %copy.57), calls=%async_computation | async-start | bytes 131072 | tf_op jit(solution)/shard_map/all_to_all | solution.py:32
  22.8 1.2 reshape.255
  24.0 13.4 %all-to-all-done = f32[64,2,128]{2,1,0:T(2,128)S(1)} async-done(((f32[64,2,128]{2,1,0:T(2,128)}), f32[64,2,128]{2,1,0:T(2,128)S(1)}, u32[]{:S(2)}, u32[]{:S(2)}) %all-to-all-start) | async-done | bytes 65568 | tf_op jit(solution)/shard_map/all_to_all | solution.py:32
  37.7 0.8 fusion.36
  38.9 0.6 broadcast_in_dim.6
  39.5 4.4 %all-to-all-start.1 = ((bf16[64,2,128]{2,1,0:T(2,128)(2,1)}), bf16[64,2,128]{2,1,0:T(2,128)(2,1)S(1)}, u32[]{:S(2)}, u32[]{:S(2)}) async-start(bf16[64,2,128]{2,1,0:T(2,128)(2,1)} %broadcast_in_dim.6), calls=%async_computation.1 | async-start | bytes 65536 | tf_op jit(solution)/shard_map/all_to_all | solution.py:32
  44.0 0.3 convert_reduce_fusion.1
  44.2 13.0 %all-to-all-done.1 = bf16[64,2,128]{2,1,0:T(2,128)(2,1)S(1)} async-done(((bf16[64,2,128]{2,1,0:T(2,128)(2,1)}), bf16[64,2,128]{2,1,0:T(2,128)(2,1)S(1)}, u32[]{:S(2)}, u32[]{:S(2)}) %all-to-all-start.1) | async-done | bytes 32800 | tf_op jit(solution)/shard_map/all_to_all | solution.py:32
  57.3 0.3 fusion.19
  57.5 0.2 reshape.253
  57.8 0.5 convolution_add_fusion
  58.3 3.4 %convert_reduce_fusion = (f32[256]{0:T(256)S(1)}, bf16[2048,256]{0,1:T(8,128)(2,1)}, bf16[2048,256]{0,1:T(8,128)(2,1)S(1)}, f32[2048,256]{0,1:T(8,128)}) fusion(f32[2048,256]{0,1:T(8,128)S(1)} %convolution_add_fusion, bf16[2048,64]{1,0:T(8,128)(2,1)S(1)} %reshape.255, bf16[256,64]{0,1:T(8,128)(2,1)S(1)} %copy-done), kind=kOutput, calls=%fused_computation.25 | convolution fusion | flops 79167232 | bytes 6587392 | tf_op jit(solution)/shard_map/nc,hc->nh/dot_general | solution.py:81
  61.6 1.0 copy-done.1
  62.6 0.4 fusion.57
  63.2 2.9 %fusion.15 = bf16[256,2048]{1,0:T(8,128)(2,1)S(1)} fusion(f32[2048,256]{0,1:T(8,128)S(1)} %convolution_add_fusion, f32[2048,256]{0,1:T(8,128)} %get-tuple-element.59), kind=kLoop, calls=%fused_computation.22 | loop fusion | flops 9961472 | bytes 5242880 | tf_op jit(solution)/shard_map/convert_element_type | solution.py:82
  66.1 0.5 fusion.22
  66.7 1.5 %convolution_convert_fusion = bf16[2048,64]{0,1:T(8,128)(2,1)S(1)} fusion(bf16[64,256]{1,0:T(8,128)(2,1)S(1)} %copy-done.5, bf16[2048,256]{0,1:T(8,128)(2,1)} %get-tuple-element.47), kind=kOutput, calls=%fused_computation.6 | convolution fusion | flops 67239936 | bytes 1343488 | tf_op jit(solution)/shard_map/nh,ch->nc/dot_general | solution.py:86
  68.3 0.3 copy.60
  68.5 0.3 reshape.264
  68.8 0.2 fusion.29
  69.1 0.8 copy.64
  69.9 4.6 %all-to-all-start.2 = ((f32[64,7,128]{2,1,0:T(8,128)}), f32[64,7,128]{2,1,0:T(8,128)S(1)}, u32[]{:S(2)}, u32[]{:S(2)}) async-start(f32[64,7,128]{2,1,0:T(8,128)} %copy.64), calls=%async_computation.2 | async-start | bytes 524288 | tf_op jit(solution)/shard_map/all_to_all | solution.py:32
  74.6 0.3 convolution_add_fusion.1
  74.9 0.3 copy.59
  75.2 0.2 reshape.254
  75.5 21.5 %all-to-all-done.2 = f32[64,7,128]{2,1,0:T(8,128)S(1)} async-done(((f32[64,7,128]{2,1,0:T(8,128)}), f32[64,7,128]{2,1,0:T(8,128)S(1)}, u32[]{:S(2)}, u32[]{:S(2)}) %all-to-all-start.2) | async-done | bytes 229408 | tf_op jit(solution)/shard_map/all_to_all | solution.py:32
  97.3 0.1 fusion.38
  97.5 0.3 fusion.59
  97.8 0.2 fusion.58
  98.0 0.2 fusion.21
  98.3 0.2 fusion.20
  98.7 0.7 broadcast_in_dim.7
  99.4 6.4 %all-to-all-start.3 = ((bf16[8,74,128]{2,1,0:T(8,128)(2,1)}), bf16[8,74,128]{2,1,0:T(8,128)(2,1)S(1)}, u32[]{:S(2)}, u32[]{:S(2)}) async-start(bf16[8,74,128]{2,1,0:T(8,128)(2,1)} %broadcast_in_dim.7), calls=%async_computation.3 | async-start | bytes 327680 | tf_op jit(solution)/shard_map/all_to_all | solution.py:32
  105.9 7.7 %all-to-all-done.3 = bf16[8,74,128]{2,1,0:T(8,128)(2,1)S(1)} async-done(((bf16[8,74,128]{2,1,0:T(8,128)(2,1)}), bf16[8,74,128]{2,1,0:T(8,128)(2,1)S(1)}, u32[]{:S(2)}, u32[]{:S(2)}) %all-to-all-start.3) | async-done | bytes 151584 | tf_op jit(solution)/shard_map/all_to_all | solution.py:32
  113.8 0.7 broadcast_in_dim.8
  114.4 4.8 %all-to-all-start.4 = ((bf16[64,7,128]{2,1,0:T(8,128)(2,1)}), bf16[64,7,128]{2,1,0:T(8,128)(2,1)S(1)}, u32[]{:S(2)}, u32[]{:S(2)}) async-start(bf16[64,7,128]{2,1,0:T(8,128)(2,1)} %broadcast_in_dim.8), calls=%async_computation.4 | async-start | bytes 262144 | tf_op jit(solution)/shard_map/all_to_all | solution.py:32
  119.3 0.8 add_convert_fusion
  120.0 0.7 reshape.259
  120.8 15.8 %all-to-all-done.4 = bf16[64,7,128]{2,1,0:T(8,128)(2,1)S(1)} async-done(((bf16[64,7,128]{2,1,0:T(8,128)(2,1)}), bf16[64,7,128]{2,1,0:T(8,128)(2,1)S(1)}, u32[]{:S(2)}, u32[]{:S(2)}) %all-to-all-start.4) | async-done | bytes 114720 | tf_op jit(solution)/shard_map/all_to_all | solution.py:32
  136.8 0.5 slice.99
  137.4 0.6 slice.97
  138.0 1.0 fusion.18
  138.9 0.6 copy.80
  139.7 0.7 copy.68
  (60 shorter events, 2.4 us)
Async XLA Ops:
  0.6 57.6 %copy-start = (bf16[256,64]{0,1:T(8,128)(2,1)S(1)}, bf16[256,64]{0,1:T(8,128)(2,1)}, u32[]{:S(2)}) copy-start(bf16[256,64]{0,1:T(8,128)(2,1)} %param.14) | copy-start | bytes 98308
  0.6 37.9 %copy-start.8 = (bf16[2,1,64,64]{3,2,1,0:T(8,128)(2,1)S(1)}, bf16[2,1,64,64]{3,2,1,0:T(8,128)(2,1)}, u32[]{:S(2)}) copy-start(bf16[2,1,64,64]{3,2,1,0:T(8,128)(2,1)} %param.11) | copy-start | bytes 49156
  1.5 56.3 %copy-start.5 = (bf16[64,256]{1,0:T(8,128)(2,1)S(1)}, bf16[64,256]{1,0:T(8,128)(2,1)}, u32[]{:S(2)}) copy-start(bf16[64,256]{1,0:T(8,128)(2,1)} %param.12) | copy-start | bytes 98308
  1.5 56.3 %copy-start.9 = (f32[256]{0:T(256)S(1)}, f32[256]{0:T(256)}, u32[]{:S(2)}) copy-start(f32[256]{0:T(256)} %param.13) | copy-start | bytes 3076
  2.8 54.5 %copy-start.6 = (bf16[64,1,1024]{2,0,1:T(8,128)(2,1)}, bf16[64,1,1024]{2,0,1:T(8,128)(2,1)S(1)}, u32[]{:S(2)}) copy-start(bf16[64,1,1024]{2,0,1:T(8,128)(2,1)S(1)} %get-tuple-element.52) | copy-start | bytes 393220
  4.7 32.8 %all-to-all-start = ((f32[64,2,128]{2,1,0:T(2,128)}), f32[64,2,128]{2,1,0:T(2,128)S(1)}, u32[]{:S(2)}, u32[]{:S(2)}) async-start(f32[64,2,128]{2,1,0:T(2,128)} %copy.57), calls=%async_computation | async-start | bytes 131072 | tf_op jit(solution)/shard_map/all_to_all | solution.py:32
  39.5 17.7 %all-to-all-start.1 = ((bf16[64,2,128]{2,1,0:T(2,128)(2,1)}), bf16[64,2,128]{2,1,0:T(2,128)(2,1)S(1)}, u32[]{:S(2)}, u32[]{:S(2)}) async-start(bf16[64,2,128]{2,1,0:T(2,128)(2,1)} %broadcast_in_dim.6), calls=%async_computation.1 | async-start | bytes 65536 | tf_op jit(solution)/shard_map/all_to_all | solution.py:32
  61.6 1.0 copy-start.1
  66.1 2.7 %copy-start.7 = (bf16[64,1,1024]{2,0,1:T(8,128)(2,1)S(1)}, bf16[64,1,1024]{2,0,1:T(8,128)(2,1)}, u32[]{:S(2)}) copy-start(bf16[64,1,1024]{2,0,1:T(8,128)(2,1)} %copy-done.6) | copy-start | bytes 393220
  68.2 6.3 %copy-start.2 = (bf16[2048,256]{0,1:T(8,128)(2,1)S(1)}, bf16[2048,256]{0,1:T(8,128)(2,1)}, u32[]{:S(2)}) copy-start(bf16[2048,256]{0,1:T(8,128)(2,1)} %copy-done.1) | copy-start | bytes 3145732
  68.3 6.3 %copy-start.10 = (f32[64]{0:T(128)S(1)}, f32[64]{0:T(128)}, u32[]{:S(2)}) copy-start(f32[64]{0:T(128)} %param.15) | copy-start | bytes 772
  69.9 27.0 %all-to-all-start.2 = ((f32[64,7,128]{2,1,0:T(8,128)}), f32[64,7,128]{2,1,0:T(8,128)S(1)}, u32[]{:S(2)}, u32[]{:S(2)}) async-start(f32[64,7,128]{2,1,0:T(8,128)} %copy.64), calls=%async_computation.2 | async-start | bytes 524288 | tf_op jit(solution)/shard_map/all_to_all | solution.py:32
  74.9 44.4 %copy-start.4 = (bf16[1024,128]{1,0:T(8,128)(2,1)S(1)}, bf16[1024,128]{1,0:T(8,128)(2,1)}, u32[]{:S(2)}) copy-start(bf16[1024,128]{1,0:T(8,128)(2,1)} %param.8) | copy-start | bytes 786436
  75.5 62.5 %copy-start.3 = (bf16[1024,128]{1,0:T(8,128)(2,1)S(1)}, bf16[1024,128]{1,0:T(8,128)(2,1)}, u32[]{:S(2)}) copy-start(bf16[1024,128]{1,0:T(8,128)(2,1)} %param.9) | copy-start | bytes 786436
  99.4 14.3 %all-to-all-start.3 = ((bf16[8,74,128]{2,1,0:T(8,128)(2,1)}), bf16[8,74,128]{2,1,0:T(8,128)(2,1)S(1)}, u32[]{:S(2)}, u32[]{:S(2)}) async-start(bf16[8,74,128]{2,1,0:T(8,128)(2,1)} %broadcast_in_dim.7), calls=%async_computation.3 | async-start | bytes 327680 | tf_op jit(solution)/shard_map/all_to_all | solution.py:32
  114.4 22.1 %all-to-all-start.4 = ((bf16[64,7,128]{2,1,0:T(8,128)(2,1)}), bf16[64,7,128]{2,1,0:T(8,128)(2,1)S(1)}, u32[]{:S(2)}, u32[]{:S(2)}) async-start(bf16[64,7,128]{2,1,0:T(8,128)(2,1)} %broadcast_in_dim.8), calls=%async_computation.4 | async-start | bytes 262144 | tf_op jit(solution)/shard_map/all_to_all | solution.py:32

commit v2 on v1

v2 whole, which is shorter than its diff:
```python
import functools
import math

import jax
import jax.numpy as jnp
from jax import lax
from jax.experimental import pallas as pl
from jax.experimental.pallas import tpu as pltpu
from jax.sharding import PartitionSpec as P

NX = 65536
BLK = 8
LANES = 128
TILE = 8
F32 = jnp.float32
BF16 = jnp.bfloat16
VMEM = pl.BlockSpec(memory_space=pltpu.VMEM)
SMEM = pl.BlockSpec(memory_space=pltpu.SMEM)


def call(kernel, name, outs, specs, scratch=()):
    return pl.pallas_call(
        kernel,
        name=name,
        out_shape=[jax.ShapeDtypeStruct(shape, dtype) for shape, dtype in outs],
        in_specs=specs,
        out_specs=[VMEM] * len(outs),
        scratch_shapes=list(scratch),
        compiler_params=pltpu.CompilerParams(vmem_limit_bytes=48 << 20),
    )


def dot(a, b):
    return jnp.dot(a, b, preferred_element_type=F32)


def row_id(shape):
    return lax.broadcasted_iota(jnp.int32, shape, 0)


def every(ref, start, count, step):
    return ref[pl.ds(start, count, stride=step), :]


def cos_sin(turn):
    quarter = NX // 4
    quad = (turn + quarter // 2) >> (quarter.bit_length() - 1)
    rest = (turn - quad * quarter).astype(F32) * (2.0 * math.pi / NX)
    sq = rest * rest
    sin = rest * (1.0 + sq * (-1 / 6 + sq * (1 / 120 + sq * (-1 / 5040 + sq * (1 / 362880)))))
    cos = 1.0 + sq * (
        -1 / 2 + sq * (1 / 24 + sq * (-1 / 720 + sq * (1 / 40320 + sq * (-1 / 3628800))))
    )
    odd = (quad & 1) == 1
    c = jnp.where(odd, sin, cos)
    s = jnp.where(odd, cos, sin)
    return jnp.where(((quad + 1) & 2) != 0, -c, c), jnp.where((quad & 2) != 0, -s, s)


def modal_kernel(blocks_ref, first_ref, field_ref, modal_ref, table_ref):
    kblocks = blocks_ref.shape[0]
    count = kblocks * BLK
    rows = field_ref.shape[0]
    base = jnp.concatenate(
        [jnp.full((BLK, LANES), blocks_ref[b] * BLK, jnp.int32) for b in range(kblocks)], axis=0
    )
    modes = base + row_id((count, LANES)) % BLK
    lane = lax.broadcasted_iota(jnp.int32, (count, LANES), 1)
    scale = 1.0 / math.sqrt(NX)
    near_c, near_s = cos_sin((modes * lane) & (NX - 1))
    near_c, near_s = near_c * scale, near_s * scale
    far_c, far_s = cos_sin((modes * (first_ref[0] + lane * LANES)) & (NX - 1))
    for a in range(rows // LANES):
        ca = jnp.broadcast_to(far_c[:, a : a + 1], (count, LANES))
        sa = jnp.broadcast_to(far_s[:, a : a + 1], (count, LANES))
        span = pl.ds(a * LANES, LANES)
        table_ref[:count, span] = (near_c * ca - near_s * sa).astype(BF16)
        table_ref[count:, span] = (-(near_s * ca + near_c * sa)).astype(BF16)
    modal = dot(table_ref[...], field_ref[...])
    modal_ref[pl.ds(0, count, stride=2), :] = modal[:count]
    modal_ref[pl.ds(1, count, stride=2), :] = modal[count:]


def complex_rows(x, weights, sign):
    high = x.astype(BF16).astype(F32)
    rest = x - high
    mid = rest.astype(BF16).astype(F32)
    low = rest - mid
    row = row_id(x.shape)
    left = jnp.where(row < 2, high, jnp.where(row < 4, mid, jnp.where(row < 6, low, 0.0)))
    y = dot(left.astype(BF16), weights)
    y = y + pltpu.roll(y, 4, 0)
    y = y + pltpu.roll(y, 2, 0)
    by_re = y[:, :LANES]
    by_im = pltpu.roll(y[:, LANES:], 1, 0)
    return by_re + jnp.where(row % 2 == 0, sign, -sign) * by_im


def mix_kernel(recv_ref, weights_ref, out_ref, sum_ref):
    x = jnp.sum(recv_ref[...].reshape(-1, TILE, LANES), axis=0)
    x = x + pltpu.roll(x, 4, 0)
    x = x + pltpu.roll(x, 2, 0)
    sum_ref[...] = x
    mixed = complex_rows(x, weights_ref[...], -1.0)
    out_ref[...] = jnp.concatenate([mixed] * (out_ref.shape[0] // TILE), axis=0).astype(BF16)


def gelu_pair(pre):
    k = math.sqrt(2.0 / math.pi)
    sq = pre * pre
    t = jnp.tanh(pre * (k + (0.044715 * k) * sq))
    half = 0.5 * pre
    up = 1.0 + t
    return half * up, up * (0.5 + half * (1.0 - t) * (k + (3 * 0.044715 * k) * sq))


def cells_kernel(
    chunk,
    piece_ref,
    table_ref,
    table_t_ref,
    field_ref,
    cot_ref,
    cot_t_ref,
    win_ref,
    win_t_ref,
    bin_ref,
    wout_ref,
    wout_t_ref,
    bout_ref,
    out_ref,
    parts_ref,
    wide_ref,
    hidden_ref,
    gpre_ref,
    gspec_ref,
):
    rows = field_ref.shape[0]
    count = table_ref.shape[0] // 2
    hid = bin_ref.shape[1] // 2
    chans = LANES // 2
    wide_ref[...] = piece_ref[...].astype(F32)
    mixed = jnp.concatenate([every(wide_ref, 0, count, 2), every(wide_ref, 1, count, 2)], axis=0)
    mixed_t = mixed.T.astype(BF16)
    mixed = mixed.astype(BF16)
    for i in range(rows // chunk):
        span = pl.ds(i * chunk, chunk)
        spec = (2.0 * dot(table_t_ref[span, :], mixed)).astype(BF16)
        pre = dot(spec, win_ref[...]) + bin_ref[...]
        gate, slope = gelu_pair(pre)
        hidden = gate.astype(BF16)
        hidden_ref[span, :] = hidden
        gpre = (dot(cot_ref[span, :], wout_t_ref[...]) * slope).astype(BF16)
        gpre_ref[span, :] = gpre
        gspec_ref[span, :] = dot(gpre, win_t_ref[...]).astype(BF16)
        out = dot(hidden, wout_ref[...]) + bout_ref[...]
        out_ref[span, :] = (field_ref[span, :].astype(F32) + out).astype(BF16)
    spec_t = (2.0 * dot(mixed_t, table_ref[...])).astype(BF16)
    ones = jnp.ones((2 * TILE, rows), BF16)
    by_in = dot(jnp.concatenate([spec_t, ones], axis=0), gpre_ref[...])
    by_out = dot(cot_t_ref[...], hidden_ref[...])
    grad_modal = 2.0 * dot(table_ref[...], gspec_ref[...])
    sums_out = dot(ones, cot_ref[...])
    g_in = by_in[:chans, :hid] + by_in[chans:LANES, hid:]
    g_out = by_out[:chans, :hid] + by_out[chans:, hid:]
    b_in = by_in[LANES : LANES + 1, :hid] + by_in[LANES : LANES + 1, hid:]
    b_out = (sums_out + pltpu.roll(sums_out, chans, 1))[:1]
    row = row_id((count, LANES))
    bias = jnp.where(
        row == 0,
        b_in[:, :LANES],
        jnp.where(row == 1, b_in[:, LANES:], jnp.where(row == 2, b_out, 0.0)),
    )
    for r, block in enumerate(
        (
            grad_modal[:count],
            grad_modal[count:],
            g_in[:, :LANES],
            g_in[:, LANES:],
            g_out[:, :LANES],
            g_out[:, LANES:],
            bias,
            jnp.zeros((count, LANES), F32),
        )
    ):
        parts_ref[pl.ds(r, count, stride=TILE), :] = block


def share_kernel(recv_ref, modal_ref, share_ref, sum_ref):
    x = jnp.sum(recv_ref[...].astype(F32).reshape(-1, TILE, LANES), axis=0)
    sum_ref[...] = x
    both = jnp.concatenate([x, modal_ref[...]], axis=0)
    share_ref[...] = jnp.concatenate([both] * (share_ref.shape[0] // (2 * TILE)), axis=0)


def grad_in_kernel(sum_ref, weights_ref, out_ref):
    x = jnp.where(row_id((TILE, LANES)) < 2, sum_ref[...], 0.0)
    x = x + pltpu.roll(x, 4, 0)
    x = x + pltpu.roll(x, 2, 0)
    out_ref[...] = complex_rows(x, weights_ref[...], 1.0)


def total_kernel(scale, shares_ref, grad_in_ref, out_ref):
    x = jnp.sum(shares_ref[...].reshape(-1, 2 * TILE, LANES), axis=0)[:TILE]
    own = jnp.where(row_id((TILE, LANES)) < 2, grad_in_ref[...], x * scale)
    out_ref[...] = jnp.concatenate([own] * (out_ref.shape[0] // TILE), axis=0).astype(BF16)


def spectral_kernel(scale, shares_ref, out_ref):
    n = shares_ref.shape[0] // (2 * TILE)
    d_re, d_im, u_re, u_im = (every(shares_ref, r, n, 2 * TILE) for r in (0, 1, TILE, TILE + 1))
    left = jnp.concatenate([u_re, u_im], axis=0)
    right = jnp.concatenate(
        [jnp.concatenate([d_re, d_im], axis=0), jnp.concatenate([d_im, -d_re], axis=0)], axis=1
    )
    outer = lax.dot_general(
        left,
        right,
        (((0,), (0,)), ((), ())),
        precision=lax.Precision.HIGHEST,
        preferred_element_type=F32,
    )
    c = LANES // 2
    out_ref[0] = (outer[:c, :c] + outer[c:, c : 2 * c]) * scale
    out_ref[1] = (outer[:c, 2 * c : 3 * c] + outer[c:, 3 * c :]) * scale


def final_kernel(recv_ref, table_t_ref, cot_ref, fgrad_ref, win_ref, wout_ref, bin_ref, bout_ref, wide_ref):
    count = table_t_ref.shape[1] // 2
    wide_ref[...] = recv_ref[...].astype(F32)
    rows = [every(wide_ref, r, count, TILE) for r in range(TILE - 1)]
    grad_in = jnp.concatenate(rows[:2], axis=0).astype(BF16)
    back = dot(table_t_ref[...], grad_in)
    fgrad_ref[...] = (cot_ref[...].astype(F32) + back).astype(BF16)
    win_ref[:, :LANES] = rows[2]
    win_ref[:, LANES:] = rows[3]
    wout_ref[:LANES, :] = rows[4].T
    wout_ref[LANES:, :] = rows[5].T
    bin_ref[:, :LANES] = rows[6][0:1]
    bin_ref[:, LANES:] = rows[6][1:2]
    bout_ref[...] = rows[6][2:3, : bout_ref.shape[1]]


def exchange(x, axis):
    return lax.all_to_all(x, axis, 0, 0, tiled=True)


def exchange_pairs(x, axis):
    n = x.shape[0] // 2
    return exchange(x.reshape(n, 2, LANES), axis).reshape(2 * n, LANES)


def twice_diag(x):
    zero = jnp.zeros_like(x)
    return jnp.concatenate(
        [jnp.concatenate([x, zero], axis=1), jnp.concatenate([zero, x], axis=1)], axis=0
    )


def local(field, cotangent, mode_blocks, spectral, w_in, b_in, w_out, b_out):
    rows, width = field.shape
    chans, hid = w_in.shape
    ncol = width // chans
    grid = lax.axis_size("grid")
    dp = lax.axis_size("dp")
    inv_cols = 1.0 / (ncol * dp)
    count = mode_blocks.shape[0] * BLK
    first = (lax.axis_index("grid") * rows).reshape(1).astype(jnp.int32)
    s_re, s_im = spectral[0, 0], spectral[1, 0]
    mix_weights = jnp.concatenate([twice_diag(s_re), twice_diag(s_im)], axis=1)
    back_weights = jnp.concatenate([twice_diag(s_re.T), twice_diag(s_im.T)], axis=1)
    w_in_two, w_out_two = twice_diag(w_in), twice_diag(w_out)
    w_in_back, w_out_back = twice_diag(w_in.T), twice_diag(w_out.T)
    b_in_two = jnp.concatenate([b_in, b_in]).reshape(1, 2 * hid)
    b_out_two = jnp.concatenate([b_out, b_out]).reshape(1, width)

    modal, table = call(
        modal_kernel,
        "modal",
        [((2 * count, width), F32), ((2 * count, rows), BF16)],
        [SMEM, SMEM, VMEM],
    )(mode_blocks, first, field)
    table_t = table.T
    mixed, modal_sum = call(
        mix_kernel, "mix", [((2 * grid, width), BF16), ((TILE, width), F32)], [VMEM] * 2
    )(exchange_pairs(modal, "grid"), mix_weights)
    piece = exchange_pairs(mixed, "grid")

    output, parts = call(
        functools.partial(cells_kernel, 256),
        "cells",
        [((rows, width), BF16), ((TILE * grid, width), F32)],
        [VMEM] * 12,
        [
            pltpu.VMEM((2 * count, width), F32),
            pltpu.VMEM((rows, 2 * hid), BF16),
            pltpu.VMEM((rows, 2 * hid), BF16),
            pltpu.VMEM((rows, width), BF16),
        ],
    )(
        piece,
        table,
        table_t,
        field,
        cotangent,
        cotangent.T,
        w_in_two,
        w_in_back,
        b_in_two,
        w_out_two,
        w_out_back,
        b_out_two,
    )
    share, sums = call(
        share_kernel, "share", [((2 * TILE * dp, width), F32), ((TILE, width), F32)], [VMEM] * 2
    )(exchange(parts, "grid"), modal_sum)
    (grad_in,) = call(grad_in_kernel, "grad_in", [((TILE, width), F32)], [VMEM] * 2)(
        sums, back_weights
    )
    shares = exchange(share, "dp")
    (own,) = call(
        functools.partial(total_kernel, inv_cols), "total", [((TILE * grid, width), BF16)], [VMEM] * 2
    )(shares, grad_in)
    (spectral_grad,) = call(
        functools.partial(spectral_kernel, inv_cols), "spectral", [((2, chans, chans), F32)], [VMEM]
    )(shares)
    field_grad, w_in_grad, w_out_grad, b_in_grad, b_out_grad = call(
        final_kernel,
        "final",
        [
            ((rows, width), BF16),
            ((chans, hid), F32),
            ((hid, chans), F32),
            ((1, hid), F32),
            ((1, chans), F32),
        ],
        [VMEM] * 3,
        [pltpu.VMEM((TILE * grid, width), F32)],
    )(exchange(own, "grid"), table_t, cotangent)
    return (
        output,
        field_grad,
        spectral_grad.reshape(2, 1, chans, chans),
        w_in_grad,
        b_in_grad.reshape(hid),
        w_out_grad,
        b_out_grad.reshape(chans),
    )


def solution(mesh):
    in_specs = (
        P("grid", "dp"),
        P("grid", "dp"),
        P(),
        P(None, "grid", None, None),
        P(),
        P(),
        P(),
        P(),
    )
    out_specs = (P("grid", "dp"), P("grid", "dp"), P(None, "grid", None, None), P(), P(), P(), P())
    return jax.shard_map(local, mesh=mesh, in_specs=in_specs, out_specs=out_specs, check_vma=False)
```

time: 141 us -> 124 us (0.88)
  blocking collectives: 0 us -> 26.2 us
  waiting for transfers between devices: 71.3 us -> 47.8 us
  matrix products: 11.4 us -> 0 us
  Pallas kernels: 0 us -> 9.45 us
  local copies, waits for them, and re-layouts: 11.9 us -> 4.58 us
  other arithmetic: 6.33 us -> 0.39 us
  starting transfers between devices: 38.4 us -> 34.7 us
    all_to_all x0 -> x1, blocking collectives: none -> 26.2 us  [exchange(): return lax.all_to_all(x, axis, 0, 0, tiled=True)]
    all_to_all x5 -> x4, waiting for transfers between devices: 71.3 us -> 47.8 us  [exchange(): return lax.all_to_all(x, axis, 0, 0, tiled=True)]
    dot_general x18 -> x0, matrix products: 11.4 us -> none  [the longest x1 3.36 us: local(): jnp.einsum('nc,hc->nh', upstream, w_out, preferred_element_type=jnp.float32)]
    pallas_call x0 -> x8, Pallas kernels: none -> 9.45 us  [the longest x1 3.52 us: local(): call(functools.partial(cells_kernel, 256), 'cells', [((rows, width), BF16...]
    all_to_all x5 -> x4, starting transfers between devices: 38.4 us -> 34.7 us  [exchange(): return lax.all_to_all(x, axis, 0, 0, tiled=True)]
    convert_element_type x4 -> x0, other arithmetic: 3.71 us -> none  [the longest x1 2.92 us: local(): grad_pre = (grad_hidden * gelu_grad(pre)).astype(jnp.bfloat16)]
    reshape x9 -> x0, local copies, waits for them, and re-layouts: 2.98 us -> none  [the longest x1 1.19 us: local(): upstream = cotangent.reshape(-1, chans)]
    broadcast_in_dim x3 -> x0, local copies, waits for them, and re-layouts: 2 us -> none  [the longest x1 0.69 us: local(): shares = exchange(jnp.broadcast_to(share[None], (dp,) + share.shape), 'dp')]
  transfers between devices with their start and end apart: 5 -> 4, of which waited for: 5 -> 4; matrix products, arithmetic and copies ran while one was open for 3% -> 1% of each run, Pallas kernels for 0% -> 1%
where the time goes in v2:
time: 124 us
  waiting for transfers between devices  47.8 us (39%)
  starting transfers between devices  34.7 us (28%)
  blocking collectives  26.2 us (21%)
  Pallas kernels  9.45 us (8%)
  local copies, waits for them, and re-layouts  4.58 us (4%)
    all_to_all x4, waiting for transfers between devices, exchange(): return lax.all_to_all(x, axis, 0, 0, tiled=True)  47.8 us
    all_to_all x4, starting transfers between devices, exchange(): return lax.all_to_all(x, axis, 0, 0, tiled=True)  34.7 us
    all_to_all x1, blocking collectives, exchange(): return lax.all_to_all(x, axis, 0, 0, tiled=True)  26.2 us
    unnamed x24, local copies, waits for them, and re-layouts  4.3 us
    pallas_call x1, Pallas kernels, local(): call(functools.partial(cells_kernel, 256), 'cells', [((rows, width), BF16...  3.52 us
  transfers between devices with their start and end apart: 4, of which 4 were waited for; matrix products, arithmetic and copies ran while one was open for 1% of the time, Pallas kernels for 1%

profile of v2, /device:TPU:1, one launch (start us, length us, event | category | flops | bytes accessed | tf_op | source)
XLA Modules:
  0.0 123.8 jit_solution(5668668069261857270)
XLA Ops:
  0.6 0.0 copy-start.3
  0.6 0.6 copy-done.3
  1.3 0.0 copy-start.1
  1.3 0.9 copy-done.1
  2.2 1.7 %modal.1 = (f32[128,128]{1,0:T(8,128)}, bf16[128,1024]{1,0:T(8,128)(2,1)S(1)}) custom-call(s32[8]{0:T(128)S(1)} %copy-done.3, s32[1]{0:T(128)} %bitcast.first_ref, bf16[1024,128]{1,0:T(8,128)(2,1)S(1)} %copy-done.1), custom_call_target="tpu_custom_call" | custom-call | tf_op jit(solution)/shard_map/modal/pallas_call | solution.py:277
  3.9 0.0 copy-start.6
  3.9 18.3 %all-to-all-start = ((f32[64,2,128]{2,1,0:T(2,128)}), f32[64,2,128]{2,1,0:T(2,128)S(1)}, u32[]{:S(2)}, u32[]{:S(2)}) async-start(f32[64,2,128]{2,1,0:T(2,128)} %bitcast.1), calls=%async_computation | async-start | bytes 131072 | tf_op jit(solution)/shard_map/all_to_all | solution.py:245
  22.2 0.0 copy-done.6
  22.2 0.1 copy.25
  22.3 0.1 copy.26
  22.4 0.1 fusion.40
  22.5 0.0 copy-start.7
  22.5 0.0 copy-start.4
  22.6 0.0 copy-start.5
  22.6 0.1 copy.17.weights_ref
  22.7 0.5 copy-done.7
  23.2 0.1 copy-done.4
  23.3 0.0 copy-done.5
  23.3 13.5 %all-to-all-done = f32[64,2,128]{2,1,0:T(2,128)S(1)} async-done(((f32[64,2,128]{2,1,0:T(2,128)}), f32[64,2,128]{2,1,0:T(2,128)S(1)}, u32[]{:S(2)}, u32[]{:S(2)}) %all-to-all-start) | async-done | bytes 65568 | tf_op jit(solution)/shard_map/all_to_all | solution.py:245
  36.8 0.8 mix.1
  37.6 0.0 copy-start.8
  37.6 4.6 %all-to-all-start.1 = ((bf16[64,2,128]{2,1,0:T(2,128)(2,1)}), bf16[64,2,128]{2,1,0:T(2,128)(2,1)S(1)}, u32[]{:S(2)}, u32[]{:S(2)}) async-start(bf16[64,2,128]{2,1,0:T(2,128)(2,1)} %bitcast.5), calls=%async_computation.1 | async-start | bytes 65536 | tf_op jit(solution)/shard_map/all_to_all | solution.py:245
  42.1 0.0 copy-done.8
  42.1 0.1 maximum_bitcast_fusion.bout_ref
  42.2 0.1 copy.20
  42.3 0.1 copy.21
  42.5 0.0 copy-start
  42.5 0.2 copy.18
  42.6 0.8 copy-done
  43.4 0.1 copy.19
  43.6 0.0 copy-start.2
  43.6 0.1 fusion.10
  43.7 11.7 %all-to-all-done.1 = bf16[64,2,128]{2,1,0:T(2,128)(2,1)S(1)} async-done(((bf16[64,2,128]{2,1,0:T(2,128)(2,1)}), bf16[64,2,128]{2,1,0:T(2,128)(2,1)S(1)}, u32[]{:S(2)}, u32[]{:S(2)}) %all-to-all-start.1) | async-done | bytes 32800 | tf_op jit(solution)/shard_map/all_to_all | solution.py:245
  55.4 0.0 copy-done.2
  55.4 3.5 %cells.1 = (bf16[1024,128]{1,0:T(8,128)(2,1)}, f32[512,128]{1,0:T(8,128)S(1)}) custom-call(bf16[128,128]{1,0:T(8,128)(2,1)S(1)} %bitcast.38, bf16[128,1024]{1,0:T(8,128)(2,1)S(1)} %get-tuple-element.22.table_ref, bf16[1024,128]{1,0:T(8,128)(2,1)S(1)} %bitcast.29, bf16[1024,128]{1,0:T(8,128)(2,1)S(1)} %copy-done.2, bf16[1024,128]{1,0:T(8,128)(2,1)S(1)} %copy-done, ...), custom_call_target="tpu_custom_call" | custom-call | tf_op jit(solution)/shard_map/cells/pallas_call | solution.py:289
  59.0 26.2 %all_to_all.43 = f32[64,8,128]{2,1,0:T(8,128)S(1)} all-to-all(f32[64,8,128]{2,1,0:T(8,128)S(1)} %bitcast.36), channel_id=1, replica_groups=mesh['grid'=64,'dp'=8] {'grid'}, dimensions={0} | all-to-all | bytes 524288 | tf_op jit(solution)/shard_map/all_to_all | solution.py:245
  85.1 0.7 share.1
  85.8 6.4 %all-to-all-start.3 = ((f32[8,16,128]{2,1,0:T(8,128)}), f32[8,16,128]{2,1,0:T(8,128)S(1)}, u32[]{:S(2)}, u32[]{:S(2)}) async-start(f32[8,16,128]{2,1,0:T(8,128)} %bitcast.15), calls=%async_computation.3 | async-start | bytes 131072 | tf_op jit(solution)/shard_map/all_to_all | solution.py:245
  92.2 0.1 fusion.37.weights_ref
  92.3 0.1 grad_in.1.grad_in_ref
  92.4 6.5 %all-to-all-done.3 = f32[8,16,128]{2,1,0:T(8,128)S(1)} async-done(((f32[8,16,128]{2,1,0:T(8,128)}), f32[8,16,128]{2,1,0:T(8,128)S(1)}, u32[]{:S(2)}, u32[]{:S(2)}) %all-to-all-start.3) | async-done | bytes 65568 | tf_op jit(solution)/shard_map/all_to_all | solution.py:245
  98.9 0.7 total.1
  99.6 5.5 %all-to-all-start.4 = ((bf16[64,8,128]{2,1,0:T(8,128)(2,1)}), bf16[64,8,128]{2,1,0:T(8,128)(2,1)S(1)}, u32[]{:S(2)}, u32[]{:S(2)}) async-start(bf16[64,8,128]{2,1,0:T(8,128)(2,1)} %bitcast.21), calls=%async_computation.4 | async-start | bytes 262144 | tf_op jit(solution)/shard_map/all_to_all | solution.py:245
  105.0 1.0 spectral.1
  106.1 16.1 %all-to-all-done.4 = bf16[64,8,128]{2,1,0:T(8,128)(2,1)S(1)} async-done(((bf16[64,8,128]{2,1,0:T(8,128)(2,1)}), bf16[64,8,128]{2,1,0:T(8,128)(2,1)S(1)}, u32[]{:S(2)}, u32[]{:S(2)}) %all-to-all-start.4) | async-done | bytes 131104 | tf_op jit(solution)/shard_map/all_to_all | solution.py:245
  122.2 1.0 final.1
  123.1 0.7 copy.24
  (3 shorter events, 0.0 us)
Async XLA Ops:
  0.6 0.7 copy-start.3
  1.3 0.9 copy-start.1
  3.9 18.3 %copy-start.6 = (bf16[2,1,64,64]{3,2,1,0:T(8,128)(2,1)S(1)}, bf16[2,1,64,64]{3,2,1,0:T(8,128)(2,1)}, u32[]{:S(2)}) copy-start(bf16[2,1,64,64]{3,2,1,0:T(8,128)(2,1)} %param.11) | copy-start | bytes 49156
  3.9 32.9 %all-to-all-start = ((f32[64,2,128]{2,1,0:T(2,128)}), f32[64,2,128]{2,1,0:T(2,128)S(1)}, u32[]{:S(2)}, u32[]{:S(2)}) async-start(f32[64,2,128]{2,1,0:T(2,128)} %bitcast.1), calls=%async_computation | async-start | bytes 131072 | tf_op jit(solution)/shard_map/all_to_all | solution.py:245
  22.5 0.7 copy-start.7
  22.5 0.8 copy-start.4
  22.6 0.8 copy-start.5
  37.6 4.6 %copy-start.8 = (f32[64]{0:T(128)S(1)}, f32[64]{0:T(128)}, u32[]{:S(2)}) copy-start(f32[64]{0:T(128)} %param.15) | copy-start | bytes 772
  37.6 17.9 %all-to-all-start.1 = ((bf16[64,2,128]{2,1,0:T(2,128)(2,1)}), bf16[64,2,128]{2,1,0:T(2,128)(2,1)S(1)}, u32[]{:S(2)}, u32[]{:S(2)}) async-start(bf16[64,2,128]{2,1,0:T(2,128)(2,1)} %bitcast.5), calls=%async_computation.1 | async-start | bytes 65536 | tf_op jit(solution)/shard_map/all_to_all | solution.py:245
  42.5 1.0 copy-start
  43.6 11.9 %copy-start.2 = (bf16[1024,128]{1,0:T(8,128)(2,1)S(1)}, bf16[1024,128]{1,0:T(8,128)(2,1)}, u32[]{:S(2)}) copy-start(bf16[1024,128]{1,0:T(8,128)(2,1)} %field_ref.3) | copy-start | bytes 786436
  85.8 13.1 %all-to-all-start.3 = ((f32[8,16,128]{2,1,0:T(8,128)}), f32[8,16,128]{2,1,0:T(8,128)S(1)}, u32[]{:S(2)}, u32[]{:S(2)}) async-start(f32[8,16,128]{2,1,0:T(8,128)} %bitcast.15), calls=%async_computation.3 | async-start | bytes 131072 | tf_op jit(solution)/shard_map/all_to_all | solution.py:245
  99.6 22.6 %all-to-all-start.4 = ((bf16[64,8,128]{2,1,0:T(8,128)(2,1)}), bf16[64,8,128]{2,1,0:T(8,128)(2,1)S(1)}, u32[]{:S(2)}, u32[]{:S(2)}) async-start(bf16[64,8,128]{2,1,0:T(8,128)(2,1)} %bitcast.21), calls=%async_computation.4 | async-start | bytes 262144 | tf_op jit(solution)/shard_map/all_to_all | solution.py:245

commit v3 on v2

--- a/solution.py
+++ b/solution.py
@@ -15,16 +15,17 @@
 F32 = jnp.float32
 BF16 = jnp.bfloat16
 VMEM = pl.BlockSpec(memory_space=pltpu.VMEM)
-SMEM = pl.BlockSpec(memory_space=pltpu.SMEM)
+HBM = pl.BlockSpec(memory_space=pltpu.HBM)
+PARTS = 10
 
 
 def call(kernel, name, outs, specs, scratch=()):
     return pl.pallas_call(
         kernel,
         name=name,
-        out_shape=[jax.ShapeDtypeStruct(shape, dtype) for shape, dtype in outs],
+        out_shape=[jax.ShapeDtypeStruct(o[0], o[1]) for o in outs],
         in_specs=specs,
-        out_specs=[VMEM] * len(outs),
+        out_specs=[o[2] if len(o) > 2 else VMEM for o in outs],
         scratch_shapes=list(scratch),
         compiler_params=pltpu.CompilerParams(vmem_limit_bytes=48 << 20),
     )
@@ -57,10 +58,18 @@
     return jnp.where(((quad + 1) & 2) != 0, -c, c), jnp.where((quad & 2) != 0, -s, s)
 
 
-def modal_kernel(blocks_ref, first_ref, field_ref, modal_ref, table_ref):
+def modal_kernel(
+    blocks_hbm, field_hbm, modal_ref, table_ref, blocks_ref, field_ref, blocks_sem, field_sem
+):
+    blocks_copy = pltpu.make_async_copy(blocks_hbm, blocks_ref, blocks_sem)
+    blocks_copy.start()
+    field_copy = pltpu.make_async_copy(field_hbm, field_ref, field_sem)
+    field_copy.start()
+    blocks_copy.wait()
     kblocks = blocks_ref.shape[0]
     count = kblocks * BLK
     rows = field_ref.shape[0]
+    first = lax.axis_index("grid") * rows
     base = jnp.concatenate(
         [jnp.full((BLK, LANES), blocks_ref[b] * BLK, jnp.int32) for b in range(kblocks)], axis=0
     )
@@ -69,26 +78,28 @@
     scale = 1.0 / math.sqrt(NX)
     near_c, near_s = cos_sin((modes * lane) & (NX - 1))
     near_c, near_s = near_c * scale, near_s * scale
-    far_c, far_s = cos_sin((modes * (first_ref[0] + lane * LANES)) & (NX - 1))
+    far_c, far_s = cos_sin((modes * (first + lane * LANES)) & (NX - 1))
     for a in range(rows // LANES):
         ca = jnp.broadcast_to(far_c[:, a : a + 1], (count, LANES))
         sa = jnp.broadcast_to(far_s[:, a : a + 1], (count, LANES))
         span = pl.ds(a * LANES, LANES)
         table_ref[:count, span] = (near_c * ca - near_s * sa).astype(BF16)
         table_ref[count:, span] = (-(near_s * ca + near_c * sa)).astype(BF16)
+    field_copy.wait()
     modal = dot(table_ref[...], field_ref[...])
     modal_ref[pl.ds(0, count, stride=2), :] = modal[:count]
     modal_ref[pl.ds(1, count, stride=2), :] = modal[count:]
 
 
-def complex_rows(x, weights, sign):
+def complex_rows(x, weights, axis, sign):
     high = x.astype(BF16).astype(F32)
     rest = x - high
     mid = rest.astype(BF16).astype(F32)
     low = rest - mid
     row = row_id(x.shape)
     left = jnp.where(row < 2, high, jnp.where(row < 4, mid, jnp.where(row < 6, low, 0.0)))
-    y = dot(left.astype(BF16), weights)
+    dims = (((1,), (axis,)), ((), ()))
+    y = lax.dot_general(left.astype(BF16), weights, dims, preferred_element_type=F32)
     y = y + pltpu.roll(y, 4, 0)
     y = y + pltpu.roll(y, 2, 0)
     by_re = y[:, :LANES]
@@ -101,7 +112,7 @@
     x = x + pltpu.roll(x, 4, 0)
     x = x + pltpu.roll(x, 2, 0)
     sum_ref[...] = x
-    mixed = complex_rows(x, weights_ref[...], -1.0)
+    mixed = complex_rows(x, weights_ref[...], 0, -1.0)
     out_ref[...] = jnp.concatenate([mixed] * (out_ref.shape[0] // TILE), axis=0).astype(BF16)
 
 
@@ -128,12 +139,15 @@
     wout_ref,
     wout_t_ref,
     bout_ref,
-    out_ref,
+    out_hbm,
     parts_ref,
     wide_ref,
     hidden_ref,
     gpre_ref,
     gspec_ref,
+    out_ref,
+    sums_ref,
+    out_sems,
 ):
     rows = field_ref.shape[0]
     count = table_ref.shape[0] // 2
@@ -143,6 +157,7 @@
     mixed = jnp.concatenate([every(wide_ref, 0, count, 2), every(wide_ref, 1, count, 2)], axis=0)
     mixed_t = mixed.T.astype(BF16)
     mixed = mixed.astype(BF16)
+    copies = []
     for i in range(rows // chunk):
         span = pl.ds(i * chunk, chunk)
         spec = (2.0 * dot(table_t_ref[span, :], mixed)).astype(BF16)
@@ -155,6 +170,8 @@
         gspec_ref[span, :] = dot(gpre, win_t_ref[...]).astype(BF16)
         out = dot(hidden, wout_ref[...]) + bout_ref[...]
         out_ref[span, :] = (field_ref[span, :].astype(F32) + out).astype(BF16)
+        copies.append(pltpu.make_async_copy(out_ref.at[span], out_hbm.at[span], out_sems.at[i]))
+        copies[-1].start()
     spec_t = (2.0 * dot(mixed_t, table_ref[...])).astype(BF16)
     ones = jnp.ones((2 * TILE, rows), BF16)
     by_in = dot(jnp.concatenate([spec_t, ones], axis=0), gpre_ref[...])
@@ -173,31 +190,34 @@
     )
     for r, block in enumerate(
         (
-            grad_modal[:count],
-            grad_modal[count:],
+            *split(grad_modal[:count]),
+            *split(grad_modal[count:]),
             g_in[:, :LANES],
             g_in[:, LANES:],
             g_out[:, :LANES],
             g_out[:, LANES:],
-            bias,
-            jnp.zeros((count, LANES), F32),
+            *split(bias),
         )
     ):
-        parts_ref[pl.ds(r, count, stride=TILE), :] = block
-
-
-def share_kernel(recv_ref, modal_ref, share_ref, sum_ref):
-    x = jnp.sum(recv_ref[...].astype(F32).reshape(-1, TILE, LANES), axis=0)
-    sum_ref[...] = x
-    both = jnp.concatenate([x, modal_ref[...]], axis=0)
+        sums_ref[pl.ds(r, count, stride=PARTS), :] = block
+    parts_ref[...] = sums_ref[...].astype(BF16)
+    for copy in copies:
+        copy.wait()
+
+
+def split(x):
+    high = x.astype(BF16).astype(F32)
+    return high, x - high
+
+
+def share_kernel(recv_ref, modal_ref, weights_ref, share_ref, grad_in_ref):
+    x = jnp.sum(recv_ref[...].astype(F32).reshape(-1, 4 * PARTS, LANES), axis=0)
+    x = (x[:PARTS] + x[PARTS : 2 * PARTS]) + (x[2 * PARTS : 3 * PARTS] + x[3 * PARTS :])
+    d_re, d_im, bias = x[0:1] + x[1:2], x[2:3] + x[3:4], x[8:9] + x[9:10]
+    both = jnp.concatenate([d_re, d_im, x[4:8], bias, jnp.zeros_like(bias), modal_ref[...]], axis=0)
     share_ref[...] = jnp.concatenate([both] * (share_ref.shape[0] // (2 * TILE)), axis=0)
-
-
-def grad_in_kernel(sum_ref, weights_ref, out_ref):
-    x = jnp.where(row_id((TILE, LANES)) < 2, sum_ref[...], 0.0)
-    x = x + pltpu.roll(x, 4, 0)
-    x = x + pltpu.roll(x, 2, 0)
-    out_ref[...] = complex_rows(x, weights_ref[...], 1.0)
+    grad = jnp.concatenate([d_re, d_im] * (TILE // 2), axis=0)
+    grad_in_ref[...] = complex_rows(grad, weights_ref[...], 1, 1.0)
 
 
 def total_kernel(scale, shares_ref, grad_in_ref, out_ref):
@@ -225,20 +245,40 @@
     out_ref[1] = (outer[:c, 2 * c : 3 * c] + outer[c:, 3 * c :]) * scale
 
 
-def final_kernel(recv_ref, table_t_ref, cot_ref, fgrad_ref, win_ref, wout_ref, bin_ref, bout_ref, wide_ref):
+def final_kernel(
+    chunk,
+    recv_ref,
+    table_t_ref,
+    cot_ref,
+    fgrad_hbm,
+    win_ref,
+    wout_ref,
+    bin_ref,
+    bout_ref,
+    wide_ref,
+    fgrad_ref,
+    sems,
+):
     count = table_t_ref.shape[1] // 2
     wide_ref[...] = recv_ref[...].astype(F32)
     rows = [every(wide_ref, r, count, TILE) for r in range(TILE - 1)]
     grad_in = jnp.concatenate(rows[:2], axis=0).astype(BF16)
-    back = dot(table_t_ref[...], grad_in)
-    fgrad_ref[...] = (cot_ref[...].astype(F32) + back).astype(BF16)
+    copies = []
+    for i in range(table_t_ref.shape[0] // chunk):
+        span = pl.ds(i * chunk, chunk)
+        back = dot(table_t_ref[span, :], grad_in)
+        fgrad_ref[span, :] = (cot_ref[span, :].astype(F32) + back).astype(BF16)
+        copies.append(pltpu.make_async_copy(fgrad_ref.at[span], fgrad_hbm.at[span], sems.at[i]))
+        copies[-1].start()
     win_ref[:, :LANES] = rows[2]
     win_ref[:, LANES:] = rows[3]
-    wout_ref[:LANES, :] = rows[4].T
-    wout_ref[LANES:, :] = rows[5].T
+    wout_ref[:, :LANES] = rows[4]
+    wout_ref[:, LANES:] = rows[5]
     bin_ref[:, :LANES] = rows[6][0:1]
     bin_ref[:, LANES:] = rows[6][1:2]
     bout_ref[...] = rows[6][2:3, : bout_ref.shape[1]]
+    for copy in copies:
+        copy.wait()
 
 
 def exchange(x, axis):
@@ -265,10 +305,9 @@
     dp = lax.axis_size("dp")
     inv_cols = 1.0 / (ncol * dp)
     count = mode_blocks.shape[0] * BLK
-    first = (lax.axis_index("grid") * rows).reshape(1).astype(jnp.int32)
     s_re, s_im = spectral[0, 0], spectral[1, 0]
     mix_weights = jnp.concatenate([twice_diag(s_re), twice_diag(s_im)], axis=1)
-    back_weights = jnp.concatenate([twice_diag(s_re.T), twice_diag(s_im.T)], axis=1)
+    back_weights = jnp.concatenate([twice_diag(s_re), twice_diag(s_im)], axis=0)
     w_in_two, w_out_two = twice_diag(w_in), twice_diag(w_out)
     w_in_back, w_out_back = twice_diag(w_in.T), twice_diag(w_out.T)
     b_in_two = jnp.concatenate([b_in, b_in]).reshape(1, 2 * hid)
@@ -278,24 +317,54 @@
         modal_kernel,
         "modal",
         [((2 * count, width), F32), ((2 * count, rows), BF16)],
-        [SMEM, SMEM, VMEM],
-    )(mode_blocks, first, field)
-    table_t = table.T
+        [HBM, HBM],
+        [
+            pltpu.SMEM(mode_blocks.shape, jnp.int32),
+            pltpu.VMEM((rows, width), BF16),
+            pltpu.SemaphoreType.DMA,
+            pltpu.SemaphoreType.DMA,
+        ],
+    )(
+        pltpu.with_memory_space_constraint(mode_blocks, pltpu.HBM),
+        pltpu.with_memory_space_constraint(field, pltpu.HBM),
+    )
+    recv, ready = lax.optimization_barrier(
+        (
+            exchange_pairs(modal, "grid"),
+            (
+                table.T,
+                cotangent.T,
+                mix_weights,
+                back_weights,
+                w_in_two,
+                w_in_back,
+                b_in_two,
+                w_out_two,
+                w_out_back,
+                b_out_two,
+            ),
+        )
+    )
+    table_t, cotangent_t, mix_weights, back_weights = ready[:4]
+    w_in_two, w_in_back, b_in_two, w_out_two, w_out_back, b_out_two = ready[4:]
     mixed, modal_sum = call(
         mix_kernel, "mix", [((2 * grid, width), BF16), ((TILE, width), F32)], [VMEM] * 2
-    )(exchange_pairs(modal, "grid"), mix_weights)
+    )(recv, mix_weights)
     piece = exchange_pairs(mixed, "grid")
 
     output, parts = call(
         functools.partial(cells_kernel, 256),
         "cells",
-        [((rows, width), BF16), ((TILE * grid, width), F32)],
+        [((rows, width), BF16, HBM), ((PARTS * grid, width), BF16)],
         [VMEM] * 12,
         [
             pltpu.VMEM((2 * count, width), F32),
             pltpu.VMEM((rows, 2 * hid), BF16),
             pltpu.VMEM((rows, 2 * hid), BF16),
             pltpu.VMEM((rows, width), BF16),
+            pltpu.VMEM((rows, width), BF16),
+            pltpu.VMEM((PARTS * grid, width), F32),
+            pltpu.SemaphoreType.DMA((rows // 256,)),
         ],
     )(
         piece,
@@ -303,7 +372,7 @@
         table_t,
         field,
         cotangent,
-        cotangent.T,
+        cotangent_t,
         w_in_two,
         w_in_back,
         b_in_two,
@@ -311,12 +380,9 @@
         w_out_back,
         b_out_two,
     )
-    share, sums = call(
-        share_kernel, "share", [((2 * TILE * dp, width), F32), ((TILE, width), F32)], [VMEM] * 2
-    )(exchange(parts, "grid"), modal_sum)
-    (grad_in,) = call(grad_in_kernel, "grad_in", [((TILE, width), F32)], [VMEM] * 2)(
-        sums, back_weights
-    )
+    share, grad_in = call(
+        share_kernel, "share", [((2 * TILE * dp, width), F32), ((TILE, width), F32)], [VMEM] * 3
+    )(exchange_pairs(parts, "grid"), modal_sum, back_weights)
     shares = exchange(share, "dp")
     (own,) = call(
         functools.partial(total_kernel, inv_cols), "total", [((TILE * grid, width), BF16)], [VMEM] * 2
@@ -325,17 +391,21 @@
         functools.partial(spectral_kernel, inv_cols), "spectral", [((2, chans, chans), F32)], [VMEM]
     )(shares)
     field_grad, w_in_grad, w_out_grad, b_in_grad, b_out_grad = call(
-        final_kernel,
+        functools.partial(final_kernel, 256),
         "final",
         [
-            ((rows, width), BF16),
+            ((rows, width), BF16, HBM),
             ((chans, hid), F32),
-            ((hid, chans), F32),
+            ((chans, hid), F32),
             ((1, hid), F32),
             ((1, chans), F32),
         ],
         [VMEM] * 3,
-        [pltpu.VMEM((TILE * grid, width), F32)],
+        [
+            pltpu.VMEM((TILE * grid, width), F32),
+            pltpu.VMEM((rows, width), BF16),
+            pltpu.SemaphoreType.DMA((rows // 256,)),
+        ],
     )(exchange(own, "grid"), table_t, cotangent)
     return (
         output,
@@ -343,7 +413,7 @@
         spectral_grad.reshape(2, 1, chans, chans),
         w_in_grad,
         b_in_grad.reshape(hid),
-        w_out_grad,
+        w_out_grad.T,
         b_out_grad.reshape(chans),
     )
 

time: 124 us -> 117 us (0.944)
  blocking collectives: 26.2 us -> 52.1 us
  waiting for transfers between devices: 47.8 us -> 27.9 us
  starting transfers between devices: 34.7 us -> 24 us
  local copies, waits for them, and re-layouts: 4.58 us -> 2.58 us
    all_to_all x1 -> x3, blocking collectives: 26.2 us -> 52.1 us  [exchange(): return lax.all_to_all(x, axis, 0, 0, tiled=True)]
    all_to_all x4 -> x2, waiting for transfers between devices: 47.8 us -> 27.9 us  [exchange(): return lax.all_to_all(x, axis, 0, 0, tiled=True)]
    all_to_all x4 -> x2, starting transfers between devices: 34.7 us -> 24 us  [exchange(): return lax.all_to_all(x, axis, 0, 0, tiled=True)]
    unnamed x24 -> x17, local copies, waits for them, and re-layouts: 4.3 us -> 2.33 us
  transfers between devices with their start and end apart: 4 -> 2, of which waited for: 4 -> 2; matrix products, arithmetic and copies ran while one was open for 1% -> 1% of each run, Pallas kernels for 1% -> 1%
where the time goes in v3:
time: 117 us
  blocking collectives  52.1 us (45%)
  waiting for transfers between devices  27.9 us (24%)
  starting transfers between devices  24 us (21%)
  Pallas kernels  8.94 us (8%)
  local copies, waits for them, and re-layouts  2.58 us (2%)
    all_to_all x3, blocking collectives, exchange(): return lax.all_to_all(x, axis, 0, 0, tiled=True)  52.1 us
    all_to_all x2, waiting for transfers between devices, exchange(): return lax.all_to_all(x, axis, 0, 0, tiled=True)  27.9 us
    all_to_all x2, starting transfers between devices, exchange(): return lax.all_to_all(x, axis, 0, 0, tiled=True)  24 us
    pallas_call x1, Pallas kernels, local(): call(functools.partial(cells_kernel, 256), 'cells', [((rows, width), BF16...  3.5 us
  transfers between devices with their start and end apart: 2, of which 2 were waited for; matrix products, arithmetic and copies ran while one was open for 1% of the time, Pallas kernels for 1%

profile of v3, /device:TPU:1, one launch (start us, length us, event | category | flops | bytes accessed | tf_op | source)
XLA Modules:
  0.0 116.5 jit_solution(11190626129170478850)
XLA Ops:
  0.6 1.8 %modal.1 = (f32[128,128]{1,0:T(8,128)}, bf16[128,1024]{1,0:T(8,128)(2,1)S(1)}) custom-call(s32[8]{0:T(128)} %blocks_hbm.1, bf16[1024,128]{1,0:T(8,128)(2,1)} %field_ref.1), custom_call_target="tpu_custom_call" | custom-call | tf_op jit(solution)/shard_map/modal/pallas_call | solution.py:316
  2.5 0.0 copy-start.4
  2.5 18.2 %all-to-all-start = ((f32[64,2,128]{2,1,0:T(2,128)}), f32[64,2,128]{2,1,0:T(2,128)S(1)}, u32[]{:S(2)}, u32[]{:S(2)}) async-start(f32[64,2,128]{2,1,0:T(2,128)} %bitcast), calls=%async_computation | async-start | bytes 131072 | tf_op jit(solution)/shard_map/all_to_all | solution.py:285
  20.7 0.0 copy-done.4
  20.7 0.0 copy-start
  20.7 0.1 fusion.12
  20.8 0.0 copy-start.5
  20.8 0.0 copy-start.2
  20.8 0.6 copy-done.5
  21.5 0.0 copy-start.6
  21.5 0.6 copy-done.6
  22.1 0.1 maximum_bitcast_fusion.bout_ref
  22.2 0.0 copy-done.2
  22.2 0.0 copy-start.3
  22.2 0.1 copy.17
  22.3 0.6 copy-done.3
  23.0 0.1 copy.18
  23.1 0.0 copy-done
  23.1 0.1 copy.16
  23.2 0.2 copy.15
  23.4 0.0 copy-start.1
  23.4 0.1 fusion.10
  23.6 11.7 %all-to-all-done = f32[64,2,128]{2,1,0:T(2,128)S(1)} async-done(((f32[64,2,128]{2,1,0:T(2,128)}), f32[64,2,128]{2,1,0:T(2,128)S(1)}, u32[]{:S(2)}, u32[]{:S(2)}) %all-to-all-start) | async-done | bytes 65568 | tf_op jit(solution)/shard_map/all_to_all | solution.py:285
  35.2 0.2 mix.1
  35.4 17.0 %all_to_all.37 = bf16[64,2,128]{2,1,0:T(2,128)(2,1)S(1)} all-to-all(bf16[64,2,128]{2,1,0:T(2,128)(2,1)S(1)} %bitcast.38), channel_id=1, replica_groups=mesh['grid'=64,'dp'=8] {'grid'}, dimensions={0} | all-to-all | bytes 65536 | tf_op jit(solution)/shard_map/all_to_all | solution.py:285
  52.4 0.0 copy-done.1
  52.4 3.5 %cells.1 = (bf16[1024,128]{1,0:T(8,128)(2,1)}, bf16[640,128]{1,0:T(8,128)(2,1)S(1)}) custom-call(bf16[128,128]{1,0:T(8,128)(2,1)S(1)} %bitcast.36, bf16[128,1024]{1,0:T(8,128)(2,1)S(1)} %get-tuple-element.32.table_ref, bf16[1024,128]{1,0:T(8,128)(2,1)S(1)} %bitcast.27, bf16[1024,128]{1,0:T(8,128)(2,1)S(1)} %copy-done.1, bf16[1024,128]{1,0:T(8,128)(2,1)S(1)} %copy-done, ...), custom_call_target="tpu_custom_call" | custom-call | tf_op jit(solution)/shard_map/cells/pallas_call | solution.py:355
  55.9 22.3 %all_to_all.38 = bf16[320,2,128]{2,1,0:T(2,128)(2,1)S(1)} all-to-all(bf16[320,2,128]{2,1,0:T(2,128)(2,1)S(1)} %bitcast.35), channel_id=1, replica_groups=mesh['grid'=64,'dp'=8] {'grid'}, dimensions={0} | all-to-all | bytes 327680 | tf_op jit(solution)/shard_map/all_to_all | solution.py:285
  78.2 0.2 share.1
  78.4 12.9 %all_to_all.39 = f32[8,16,128]{2,1,0:T(8,128)S(1)} all-to-all(f32[8,16,128]{2,1,0:T(8,128)S(1)} %bitcast.37), channel_id=1, replica_groups=mesh['grid'=64,'dp'=8] {'dp'}, dimensions={0} | all-to-all | bytes 131072 | tf_op jit(solution)/shard_map/all_to_all | solution.py:285
  91.2 0.7 total.1
  91.9 5.8 %all-to-all-start.4 = ((bf16[64,8,128]{2,1,0:T(8,128)(2,1)}), bf16[64,8,128]{2,1,0:T(8,128)(2,1)S(1)}, u32[]{:S(2)}, u32[]{:S(2)}) async-start(bf16[64,8,128]{2,1,0:T(8,128)(2,1)} %bitcast.16), calls=%async_computation.4 | async-start | bytes 262144 | tf_op jit(solution)/shard_map/all_to_all | solution.py:285
  97.7 1.0 spectral.1
  98.7 16.2 %all-to-all-done.4 = bf16[64,8,128]{2,1,0:T(8,128)(2,1)S(1)} async-done(((bf16[64,8,128]{2,1,0:T(8,128)(2,1)}), bf16[64,8,128]{2,1,0:T(8,128)(2,1)S(1)}, u32[]{:S(2)}, u32[]{:S(2)}) %all-to-all-start.4) | async-done | bytes 131104 | tf_op jit(solution)/shard_map/all_to_all | solution.py:285
  114.9 1.6 %final.1 = (bf16[1024,128]{1,0:T(8,128)(2,1)}, f32[64,256]{1,0:T(8,128)}, f32[64,256]{1,0:T(8,128)}, f32[1,256]{1,0:T(1,128)}, f32[1,64]{1,0:T(1,128)}) custom-call(bf16[512,128]{1,0:T(8,128)(2,1)S(1)} %bitcast.33, bf16[1024,128]{1,0:T(8,128)(2,1)S(1)} %bitcast.28, bf16[1024,128]{1,0:T(8,128)(2,1)S(1)} %copy-done), custom_call_target="tpu_custom_call" | custom-call | tf_op jit(solution)/shard_map/final/pallas_call | solution.py:393
  (5 shorter events, 0.0 us)
Async XLA Ops:
  2.5 18.2 %copy-start.4 = (bf16[2,1,64,64]{3,2,1,0:T(8,128)(2,1)S(1)}, bf16[2,1,64,64]{3,2,1,0:T(8,128)(2,1)}, u32[]{:S(2)}) copy-start(bf16[2,1,64,64]{3,2,1,0:T(8,128)(2,1)} %param.11) | copy-start | bytes 49156
  2.5 32.8 %all-to-all-start = ((f32[64,2,128]{2,1,0:T(2,128)}), f32[64,2,128]{2,1,0:T(2,128)S(1)}, u32[]{:S(2)}, u32[]{:S(2)}) async-start(f32[64,2,128]{2,1,0:T(2,128)} %bitcast), calls=%async_computation | async-start | bytes 131072 | tf_op jit(solution)/shard_map/all_to_all | solution.py:285
  20.7 2.4 %copy-start = (bf16[1024,128]{1,0:T(8,128)(2,1)S(1)}, bf16[1024,128]{1,0:T(8,128)(2,1)}, u32[]{:S(2)}) copy-start(bf16[1024,128]{1,0:T(8,128)(2,1)} %cot_ref.3) | copy-start | bytes 786436
  20.8 0.7 copy-start.5
  20.8 1.4 %copy-start.2 = (bf16[64,256]{1,0:T(8,128)(2,1)S(1)}, bf16[64,256]{1,0:T(8,128)(2,1)}, u32[]{:S(2)}) copy-start(bf16[64,256]{1,0:T(8,128)(2,1)} %param.12) | copy-start | bytes 98308
  21.5 0.7 copy-start.6
  22.2 0.8 copy-start.3
  23.4 29.0 %copy-start.1 = (bf16[1024,128]{1,0:T(8,128)(2,1)S(1)}, bf16[1024,128]{1,0:T(8,128)(2,1)}, u32[]{:S(2)}) copy-start(bf16[1024,128]{1,0:T(8,128)(2,1)} %field_ref.1) | copy-start | bytes 786436
  91.9 23.0 %all-to-all-start.4 = ((bf16[64,8,128]{2,1,0:T(8,128)(2,1)}), bf16[64,8,128]{2,1,0:T(8,128)(2,1)S(1)}, u32[]{:S(2)}, u32[]{:S(2)}) async-start(bf16[64,8,128]{2,1,0:T(8,128)(2,1)} %bitcast.16), calls=%async_computation.4 | async-start | bytes 262144 | tf_op jit(solution)/shard_map/all_to_all | solution.py:285

commit v4 on v3

--- a/solution.py
+++ b/solution.py
@@ -129,7 +129,7 @@
     chunk,
     piece_ref,
     table_ref,
-    table_t_ref,
+    table_tt_ref,
     field_ref,
     cot_ref,
     cot_t_ref,
@@ -144,7 +144,6 @@
     wide_ref,
     hidden_ref,
     gpre_ref,
-    gspec_ref,
     out_ref,
     sums_ref,
     out_sems,
@@ -153,34 +152,34 @@
     count = table_ref.shape[0] // 2
     hid = bin_ref.shape[1] // 2
     chans = LANES // 2
-    wide_ref[...] = piece_ref[...].astype(F32)
+    wide_ref[...] = 2.0 * piece_ref[...].astype(F32)
     mixed = jnp.concatenate([every(wide_ref, 0, count, 2), every(wide_ref, 1, count, 2)], axis=0)
-    mixed_t = mixed.T.astype(BF16)
-    mixed = mixed.astype(BF16)
+    right = stack_parts(dot(mixed.astype(BF16), win_ref[...]))
     copies = []
     for i in range(rows // chunk):
         span = pl.ds(i * chunk, chunk)
-        spec = (2.0 * dot(table_t_ref[span, :], mixed)).astype(BF16)
-        pre = dot(spec, win_ref[...]) + bin_ref[...]
+        pre = dot(table_tt_ref[span, :], right) + bin_ref[...]
         gate, slope = gelu_pair(pre)
         hidden = gate.astype(BF16)
         hidden_ref[span, :] = hidden
-        gpre = (dot(cot_ref[span, :], wout_t_ref[...]) * slope).astype(BF16)
-        gpre_ref[span, :] = gpre
-        gspec_ref[span, :] = dot(gpre, win_t_ref[...]).astype(BF16)
+        gpre_ref[span, :] = (dot(cot_ref[span, :], wout_t_ref[...]) * slope).astype(BF16)
         out = dot(hidden, wout_ref[...]) + bout_ref[...]
         out_ref[span, :] = (field_ref[span, :].astype(F32) + out).astype(BF16)
         copies.append(pltpu.make_async_copy(out_ref.at[span], out_hbm.at[span], out_sems.at[i]))
         copies[-1].start()
-    spec_t = (2.0 * dot(mixed_t, table_ref[...])).astype(BF16)
     ones = jnp.ones((2 * TILE, rows), BF16)
-    by_in = dot(jnp.concatenate([spec_t, ones], axis=0), gpre_ref[...])
+    t = dot(jnp.concatenate([table_ref[...], ones], axis=0), gpre_ref[...])
     by_out = dot(cot_t_ref[...], hidden_ref[...])
-    grad_modal = 2.0 * dot(table_ref[...], gspec_ref[...])
     sums_out = dot(ones, cot_ref[...])
-    g_in = by_in[:chans, :hid] + by_in[chans:LANES, hid:]
+    b_in = t[2 * count : 2 * count + 1]
+    t_parts = stack_parts(t[: 2 * count])
+    grad_modal = dot(t_parts, win_t_ref[...])
+    grad_modal = 2.0 * (grad_modal[: 2 * count] + grad_modal[2 * count :])
+    mixed_t = mixed.T.astype(BF16)
+    by_in = dot(jnp.concatenate([mixed_t, mixed_t], axis=1), t_parts)
+    g_in = by_in[:chans, :hid] + by_in[chans:, hid:]
     g_out = by_out[:chans, :hid] + by_out[chans:, hid:]
-    b_in = by_in[LANES : LANES + 1, :hid] + by_in[LANES : LANES + 1, hid:]
+    b_in = b_in[:, :hid] + b_in[:, hid:]
     b_out = (sums_out + pltpu.roll(sums_out, chans, 1))[:1]
     row = row_id((count, LANES))
     bias = jnp.where(
@@ -205,6 +204,11 @@
         copy.wait()
 
 
+def stack_parts(x):
+    high, low = split(x)
+    return jnp.concatenate([high, low], axis=0).astype(BF16)
+
+
 def split(x):
     high = x.astype(BF16).astype(F32)
     return high, x - high
@@ -226,50 +230,26 @@
     out_ref[...] = jnp.concatenate([own] * (out_ref.shape[0] // TILE), axis=0).astype(BF16)
 
 
-def spectral_kernel(scale, shares_ref, out_ref):
-    n = shares_ref.shape[0] // (2 * TILE)
-    d_re, d_im, u_re, u_im = (every(shares_ref, r, n, 2 * TILE) for r in (0, 1, TILE, TILE + 1))
-    left = jnp.concatenate([u_re, u_im], axis=0)
-    right = jnp.concatenate(
-        [jnp.concatenate([d_re, d_im], axis=0), jnp.concatenate([d_im, -d_re], axis=0)], axis=1
-    )
-    outer = lax.dot_general(
-        left,
-        right,
-        (((0,), (0,)), ((), ())),
-        precision=lax.Precision.HIGHEST,
-        preferred_element_type=F32,
-    )
-    c = LANES // 2
-    out_ref[0] = (outer[:c, :c] + outer[c:, c : 2 * c]) * scale
-    out_ref[1] = (outer[:c, 2 * c : 3 * c] + outer[c:, 3 * c :]) * scale
-
-
 def final_kernel(
-    chunk,
+    scale,
     recv_ref,
-    table_t_ref,
+    shares_ref,
+    table_tt_ref,
     cot_ref,
-    fgrad_hbm,
+    fgrad_ref,
+    spectral_ref,
     win_ref,
     wout_ref,
     bin_ref,
     bout_ref,
     wide_ref,
-    fgrad_ref,
-    sems,
 ):
-    count = table_t_ref.shape[1] // 2
+    count = table_tt_ref.shape[1] // 4
     wide_ref[...] = recv_ref[...].astype(F32)
     rows = [every(wide_ref, r, count, TILE) for r in range(TILE - 1)]
     grad_in = jnp.concatenate(rows[:2], axis=0).astype(BF16)
-    copies = []
-    for i in range(table_t_ref.shape[0] // chunk):
-        span = pl.ds(i * chunk, chunk)
-        back = dot(table_t_ref[span, :], grad_in)
-        fgrad_ref[span, :] = (cot_ref[span, :].astype(F32) + back).astype(BF16)
-        copies.append(pltpu.make_async_copy(fgrad_ref.at[span], fgrad_hbm.at[span], sems.at[i]))
-        copies[-1].start()
+    back = dot(table_tt_ref[:, : 2 * count], grad_in)
+    fgrad_ref[...] = (cot_ref[...].astype(F32) + back).astype(BF16)
     win_ref[:, :LANES] = rows[2]
     win_ref[:, LANES:] = rows[3]
     wout_ref[:, :LANES] = rows[4]
@@ -277,8 +257,24 @@
     bin_ref[:, :LANES] = rows[6][0:1]
     bin_ref[:, LANES:] = rows[6][1:2]
     bout_ref[...] = rows[6][2:3, : bout_ref.shape[1]]
-    for copy in copies:
-        copy.wait()
+    spectral_sums(scale, shares_ref, spectral_ref)
+
+
+def spectral_sums(scale, shares_ref, out_ref):
+    n = shares_ref.shape[0] // (2 * TILE)
+    d_re, d_im, u_re, u_im = (every(shares_ref, r, n, 2 * TILE) for r in (0, 1, TILE, TILE + 1))
+    left_high, left_low = split(jnp.concatenate([u_re, u_im], axis=0))
+    right_high, right_low = split(
+        jnp.concatenate(
+            [jnp.concatenate([d_re, d_im], axis=0), jnp.concatenate([d_im, -d_re], axis=0)], axis=1
+        )
+    )
+    left = jnp.concatenate([left_high, left_high, left_low], axis=0).astype(BF16)
+    right = jnp.concatenate([right_high, right_low, right_high], axis=0).astype(BF16)
+    outer = lax.dot_general(left, right, (((0,), (0,)), ((), ())), preferred_element_type=F32)
+    c = LANES // 2
+    out_ref[0] = (outer[:c, :c] + outer[c:, c : 2 * c]) * scale
+    out_ref[1] = (outer[:c, 2 * c : 3 * c] + outer[c:, 3 * c :]) * scale
 
 
 def exchange(x, axis):
@@ -332,7 +328,7 @@
         (
             exchange_pairs(modal, "grid"),
             (
-                table.T,
+                jnp.concatenate([table.T, table.T], axis=1),
                 cotangent.T,
                 mix_weights,
                 back_weights,
@@ -345,7 +341,7 @@
             ),
         )
     )
-    table_t, cotangent_t, mix_weights, back_weights = ready[:4]
+    table_tt, cotangent_t, mix_weights, back_weights = ready[:4]
     w_in_two, w_in_back, b_in_two, w_out_two, w_out_back, b_out_two = ready[4:]
     mixed, modal_sum = call(
         mix_kernel, "mix", [((2 * grid, width), BF16), ((TILE, width), F32)], [VMEM] * 2
@@ -362,14 +358,13 @@
             pltpu.VMEM((rows, 2 * hid), BF16),
             pltpu.VMEM((rows, 2 * hid), BF16),
             pltpu.VMEM((rows, width), BF16),
-            pltpu.VMEM((rows, width), BF16),
             pltpu.VMEM((PARTS * grid, width), F32),
             pltpu.SemaphoreType.DMA((rows // 256,)),
         ],
     )(
         piece,
         table,
-        table_t,
+        table_tt,
         field,
         cotangent,
         cotangent_t,
@@ -387,26 +382,20 @@
     (own,) = call(
         functools.partial(total_kernel, inv_cols), "total", [((TILE * grid, width), BF16)], [VMEM] * 2
     )(shares, grad_in)
-    (spectral_grad,) = call(
-        functools.partial(spectral_kernel, inv_cols), "spectral", [((2, chans, chans), F32)], [VMEM]
-    )(shares)
-    field_grad, w_in_grad, w_out_grad, b_in_grad, b_out_grad = call(
-        functools.partial(final_kernel, 256),
+    field_grad, spectral_grad, w_in_grad, w_out_grad, b_in_grad, b_out_grad = call(
+        functools.partial(final_kernel, inv_cols),
         "final",
         [
-            ((rows, width), BF16, HBM),
+            ((rows, width), BF16),
+            ((2, chans, chans), F32),
             ((chans, hid), F32),
             ((chans, hid), F32),
             ((1, hid), F32),
             ((1, chans), F32),
         ],
-        [VMEM] * 3,
-        [
-            pltpu.VMEM((TILE * grid, width), F32),
-            pltpu.VMEM((rows, width), BF16),
-            pltpu.SemaphoreType.DMA((rows // 256,)),
-        ],
-    )(exchange(own, "grid"), table_t, cotangent)
+        [VMEM] * 4,
+        [pltpu.VMEM((TILE * grid, width), F32)],
+    )(exchange(own, "grid"), shares, table_tt, cotangent)
     return (
         output,
         field_grad,

time: 117 us -> 114 us (0.974)
  blocking collectives: 52.1 us -> 74.3 us
  waiting for transfers between devices: 27.9 us -> 12.2 us
  starting transfers between devices: 24 us -> 18.2 us
  Pallas kernels: 8.94 us -> 5.88 us
    all_to_all x3 -> x4, blocking collectives: 52.1 us -> 74.3 us  [exchange(): return lax.all_to_all(x, axis, 0, 0, tiled=True)]
    all_to_all x2 -> x1, waiting for transfers between devices: 27.9 us -> 12.2 us  [exchange(): return lax.all_to_all(x, axis, 0, 0, tiled=True)]
    all_to_all x2 -> x1, starting transfers between devices: 24 us -> 18.2 us  [exchange(): return lax.all_to_all(x, axis, 0, 0, tiled=True)]
    pallas_call x2 -> x1, Pallas kernels: 2.62 us -> 1.03 us  [local(): call(functools.partial(final_kernel, inv_cols), 'final', [((rows, width),...]
  transfers between devices with their start and end apart: 2 -> 1, of which waited for: 2 -> 1; matrix products, arithmetic and copies ran while one was open for 1% -> 1% of each run, Pallas kernels for 1% -> 0%
where the time goes in v4:
time: 114 us
  blocking collectives  74.3 us (65%)
  starting transfers between devices  18.2 us (16%)
  waiting for transfers between devices  12.2 us (11%)
  Pallas kernels  5.88 us (5%)
  local copies, waits for them, and re-layouts  2.02 us (2%)
    all_to_all x4, blocking collectives, exchange(): return lax.all_to_all(x, axis, 0, 0, tiled=True)  74.3 us
    all_to_all x1, starting transfers between devices, exchange(): return lax.all_to_all(x, axis, 0, 0, tiled=True)  18.2 us
    all_to_all x1, waiting for transfers between devices, exchange(): return lax.all_to_all(x, axis, 0, 0, tiled=True)  12.2 us
    pallas_call x1, Pallas kernels, local(): call(functools.partial(cells_kernel, 256), 'cells', [((rows, width), BF16...  2.68 us
  transfers between devices with their start and end apart: 1, of which 1 were waited for; matrix products, arithmetic and copies ran while one was open for 1% of the time, Pallas kernels for 0%

profile of v4, /device:TPU:1, one launch (start us, length us, event | category | flops | bytes accessed | tf_op | source)
XLA Modules:
  0.0 113.6 jit_solution(1128041598319763488)
XLA Ops:
  0.6 1.8 %modal.1 = (f32[128,128]{1,0:T(8,128)}, bf16[128,1024]{1,0:T(8,128)(2,1)S(1)}) custom-call(s32[8]{0:T(128)} %blocks_hbm.1, bf16[1024,128]{1,0:T(8,128)(2,1)} %field_ref.1), custom_call_target="tpu_custom_call" | custom-call | tf_op jit(solution)/shard_map/modal/pallas_call | solution.py:312
  2.5 0.0 copy-start.4
  2.5 18.2 %all-to-all-start = ((f32[64,2,128]{2,1,0:T(2,128)}), f32[64,2,128]{2,1,0:T(2,128)S(1)}, u32[]{:S(2)}, u32[]{:S(2)}) async-start(f32[64,2,128]{2,1,0:T(2,128)} %bitcast), calls=%async_computation | async-start | bytes 131072 | tf_op jit(solution)/shard_map/all_to_all | solution.py:281
  20.6 0.0 copy-done.4
  20.7 0.1 fusion.12
  20.8 0.0 copy-start.5
  20.8 0.0 copy-start.2
  20.8 0.0 copy-start.3
  20.8 0.6 copy-done.5
  21.5 0.1 copy-done.2
  21.5 0.0 copy-done.3
  21.6 0.0 copy-start.6
  21.6 0.0 copy-start
  21.6 0.6 copy-done.6
  22.2 0.1 maximum_bitcast_fusion.bout_ref
  22.3 0.1 copy.17
  22.4 0.1 copy.18
  22.5 0.0 copy-done
  22.5 0.1 copy.16
  22.7 0.2 copy.15
  22.9 0.1 fusion.10
  23.0 0.0 copy-start.1
  23.0 12.2 %all-to-all-done = f32[64,2,128]{2,1,0:T(2,128)S(1)} async-done(((f32[64,2,128]{2,1,0:T(2,128)}), f32[64,2,128]{2,1,0:T(2,128)S(1)}, u32[]{:S(2)}, u32[]{:S(2)}) %all-to-all-start) | async-done | bytes 65568 | tf_op jit(solution)/shard_map/all_to_all | solution.py:281
  35.2 0.2 mix.1
  35.4 17.0 %all_to_all.37 = bf16[64,2,128]{2,1,0:T(2,128)(2,1)S(1)} all-to-all(bf16[64,2,128]{2,1,0:T(2,128)(2,1)S(1)} %bitcast.37), channel_id=1, replica_groups=mesh['grid'=64,'dp'=8] {'grid'}, dimensions={0} | all-to-all | bytes 65536 | tf_op jit(solution)/shard_map/all_to_all | solution.py:281
  52.4 0.0 copy-done.1
  52.4 2.7 %cells.1 = (bf16[1024,128]{1,0:T(8,128)(2,1)}, bf16[640,128]{1,0:T(8,128)(2,1)S(1)}) custom-call(bf16[128,128]{1,0:T(8,128)(2,1)S(1)} %bitcast.35, bf16[128,1024]{1,0:T(8,128)(2,1)S(1)} %get-tuple-element.33.table_ref, bf16[1024,256]{1,0:T(8,128)(2,1)S(1)} %pad_maximum_fusion.table_tt_ref, bf16[1024,128]{1,0:T(8,128)(2,1)S(1)} %copy-done.1, ...), custom_call_target="tpu_custom_call" | custom-call | tf_op jit(solution)/shard_map/cells/pallas_call | solution.py:351
  55.1 22.3 %all_to_all.38 = bf16[320,2,128]{2,1,0:T(2,128)(2,1)S(1)} all-to-all(bf16[320,2,128]{2,1,0:T(2,128)(2,1)S(1)} %bitcast.34), channel_id=1, replica_groups=mesh['grid'=64,'dp'=8] {'grid'}, dimensions={0} | all-to-all | bytes 327680 | tf_op jit(solution)/shard_map/all_to_all | solution.py:281
  77.4 0.2 share.1
  77.5 12.8 %all_to_all.39 = f32[8,16,128]{2,1,0:T(8,128)S(1)} all-to-all(f32[8,16,128]{2,1,0:T(8,128)S(1)} %bitcast.36), channel_id=1, replica_groups=mesh['grid'=64,'dp'=8] {'dp'}, dimensions={0} | all-to-all | bytes 131072 | tf_op jit(solution)/shard_map/all_to_all | solution.py:281
  90.4 22.2 %all_to_all.40 = bf16[64,8,128]{2,1,0:T(8,128)(2,1)S(1)} all-to-all(bf16[64,8,128]{2,1,0:T(8,128)(2,1)S(1)} %bitcast.32), channel_id=1, replica_groups=mesh['grid'=64,'dp'=8] {'grid'}, dimensions={0} | all-to-all | bytes 262144 | tf_op jit(solution)/shard_map/all_to_all | solution.py:281
  112.6 1.0 final.1
  (7 shorter events, 0.1 us)
Async XLA Ops:
  2.5 18.2 %copy-start.4 = (bf16[2,1,64,64]{3,2,1,0:T(8,128)(2,1)S(1)}, bf16[2,1,64,64]{3,2,1,0:T(8,128)(2,1)}, u32[]{:S(2)}) copy-start(bf16[2,1,64,64]{3,2,1,0:T(8,128)(2,1)} %param.11) | copy-start | bytes 49156
  2.5 32.8 %all-to-all-start = ((f32[64,2,128]{2,1,0:T(2,128)}), f32[64,2,128]{2,1,0:T(2,128)S(1)}, u32[]{:S(2)}, u32[]{:S(2)}) async-start(f32[64,2,128]{2,1,0:T(2,128)} %bitcast), calls=%async_computation | async-start | bytes 131072 | tf_op jit(solution)/shard_map/all_to_all | solution.py:281
  20.8 0.7 copy-start.5
  20.8 0.8 copy-start.2
  20.8 0.8 copy-start.3
  21.6 0.7 copy-start.6
  21.6 1.0 copy-start
  23.0 29.4 %copy-start.1 = (bf16[1024,128]{1,0:T(8,128)(2,1)S(1)}, bf16[1024,128]{1,0:T(8,128)(2,1)}, u32[]{:S(2)}) copy-start(bf16[1024,128]{1,0:T(8,128)(2,1)} %field_ref.1) | copy-start | bytes 786436

commit v5 on v4

--- a/solution.py
+++ b/solution.py
@@ -16,7 +16,6 @@
 BF16 = jnp.bfloat16
 VMEM = pl.BlockSpec(memory_space=pltpu.VMEM)
 HBM = pl.BlockSpec(memory_space=pltpu.HBM)
-PARTS = 10
 
 
 def call(kernel, name, outs, specs, scratch=()):
@@ -59,7 +58,7 @@
 
 
 def modal_kernel(
-    blocks_hbm, field_hbm, modal_ref, table_ref, blocks_ref, field_ref, blocks_sem, field_sem
+    blocks_hbm, field_hbm, modal_ref, table_ref, blocks_ref, field_ref, wide_ref, blocks_sem, field_sem
 ):
     blocks_copy = pltpu.make_async_copy(blocks_hbm, blocks_ref, blocks_sem)
     blocks_copy.start()
@@ -87,8 +86,9 @@
         table_ref[count:, span] = (-(near_s * ca + near_c * sa)).astype(BF16)
     field_copy.wait()
     modal = dot(table_ref[...], field_ref[...])
-    modal_ref[pl.ds(0, count, stride=2), :] = modal[:count]
-    modal_ref[pl.ds(1, count, stride=2), :] = modal[count:]
+    wide_ref[pl.ds(0, count, stride=2), :] = modal[:count]
+    wide_ref[pl.ds(1, count, stride=2), :] = modal[count:]
+    modal_ref[...] = wide_ref[...].astype(BF16)
 
 
 def complex_rows(x, weights, axis, sign):
@@ -108,7 +108,7 @@
 
 
 def mix_kernel(recv_ref, weights_ref, out_ref, sum_ref):
-    x = jnp.sum(recv_ref[...].reshape(-1, TILE, LANES), axis=0)
+    x = jnp.sum(recv_ref[...].astype(F32).reshape(-1, TILE, LANES), axis=0)
     x = x + pltpu.roll(x, 4, 0)
     x = x + pltpu.roll(x, 2, 0)
     sum_ref[...] = x
@@ -189,8 +189,8 @@
     )
     for r, block in enumerate(
         (
-            *split(grad_modal[:count]),
-            *split(grad_modal[count:]),
+            grad_modal[:count],
+            grad_modal[count:],
             g_in[:, :LANES],
             g_in[:, LANES:],
             g_out[:, :LANES],
@@ -198,7 +198,7 @@
             *split(bias),
         )
     ):
-        sums_ref[pl.ds(r, count, stride=PARTS), :] = block
+        sums_ref[pl.ds(r, count, stride=TILE), :] = block
     parts_ref[...] = sums_ref[...].astype(BF16)
     for copy in copies:
         copy.wait()
@@ -215,12 +215,11 @@
 
 
 def share_kernel(recv_ref, modal_ref, weights_ref, share_ref, grad_in_ref):
-    x = jnp.sum(recv_ref[...].astype(F32).reshape(-1, 4 * PARTS, LANES), axis=0)
-    x = (x[:PARTS] + x[PARTS : 2 * PARTS]) + (x[2 * PARTS : 3 * PARTS] + x[3 * PARTS :])
-    d_re, d_im, bias = x[0:1] + x[1:2], x[2:3] + x[3:4], x[8:9] + x[9:10]
-    both = jnp.concatenate([d_re, d_im, x[4:8], bias, jnp.zeros_like(bias), modal_ref[...]], axis=0)
+    x = jnp.sum(recv_ref[...].astype(F32).reshape(-1, TILE, LANES), axis=0)
+    x = jnp.where(row_id(x.shape) == 6, x + pltpu.roll(x, TILE - 1, 0), x)
+    both = jnp.concatenate([x, modal_ref[...]], axis=0)
     share_ref[...] = jnp.concatenate([both] * (share_ref.shape[0] // (2 * TILE)), axis=0)
-    grad = jnp.concatenate([d_re, d_im] * (TILE // 2), axis=0)
+    grad = jnp.concatenate([x[:2]] * (TILE // 2), axis=0)
     grad_in_ref[...] = complex_rows(grad, weights_ref[...], 1, 1.0)
 
 
@@ -286,6 +285,11 @@
     return exchange(x.reshape(n, 2, LANES), axis).reshape(2 * n, LANES)
 
 
+def exchange_tiles(x, axis):
+    n = x.shape[0] // TILE
+    return exchange(x.reshape(n, TILE, LANES), axis).reshape(TILE * n, LANES)
+
+
 def twice_diag(x):
     zero = jnp.zeros_like(x)
     return jnp.concatenate(
@@ -312,11 +316,12 @@
     modal, table = call(
         modal_kernel,
         "modal",
-        [((2 * count, width), F32), ((2 * count, rows), BF16)],
+        [((2 * count, width), BF16), ((2 * count, rows), BF16)],
         [HBM, HBM],
         [
             pltpu.SMEM(mode_blocks.shape, jnp.int32),
             pltpu.VMEM((rows, width), BF16),
+            pltpu.VMEM((2 * count, width), F32),
             pltpu.SemaphoreType.DMA,
             pltpu.SemaphoreType.DMA,
         ],
@@ -351,14 +356,14 @@
     output, parts = call(
         functools.partial(cells_kernel, 256),
         "cells",
-        [((rows, width), BF16, HBM), ((PARTS * grid, width), BF16)],
+        [((rows, width), BF16, HBM), ((TILE * grid, width), BF16)],
         [VMEM] * 12,
         [
             pltpu.VMEM((2 * count, width), F32),
             pltpu.VMEM((rows, 2 * hid), BF16),
             pltpu.VMEM((rows, 2 * hid), BF16),
             pltpu.VMEM((rows, width), BF16),
-            pltpu.VMEM((PARTS * grid, width), F32),
+            pltpu.VMEM((TILE * grid, width), F32),
             pltpu.SemaphoreType.DMA((rows // 256,)),
         ],
     )(
@@ -377,7 +382,7 @@
     )
     share, grad_in = call(
         share_kernel, "share", [((2 * TILE * dp, width), F32), ((TILE, width), F32)], [VMEM] * 3
-    )(exchange_pairs(parts, "grid"), modal_sum, back_weights)
+    )(exchange_tiles(parts, "grid"), modal_sum, back_weights)
     shares = exchange(share, "dp")
     (own,) = call(
         functools.partial(total_kernel, inv_cols), "total", [((TILE * grid, width), BF16)], [VMEM] * 2

time: 114 us -> 112 us (0.982)
  waiting for transfers between devices: 12.2 us -> 10 us
    all_to_all x1, waiting for transfers between devices: 12.2 us -> 10 us  [exchange(): return lax.all_to_all(x, axis, 0, 0, tiled=True)]
where the time goes in v5:
time: 112 us; the launch traced here: 111 us
  blocking collectives  73.4 us (66%)
  starting transfers between devices  18.2 us (16%)
  waiting for transfers between devices  10 us (9%)
  Pallas kernels  5.9 us (5%)
  local copies, waits for them, and re-layouts  2.78 us (2%)
    all_to_all x4, blocking collectives, exchange(): return lax.all_to_all(x, axis, 0, 0, tiled=True)  73.4 us
    all_to_all x1, starting transfers between devices, exchange(): return lax.all_to_all(x, axis, 0, 0, tiled=True)  18.2 us
    all_to_all x1, waiting for transfers between devices, exchange(): return lax.all_to_all(x, axis, 0, 0, tiled=True)  10 us
    pallas_call x1, Pallas kernels, local(): call(functools.partial(cells_kernel, 256), 'cells', [((rows, width), BF16...  2.68 us
    unnamed x17, local copies, waits for them, and re-layouts  2.52 us
  transfers between devices with their start and end apart: 1, of which 1 were waited for; matrix products, arithmetic and copies ran while one was open for 1% of the time, Pallas kernels for 0%

profile of v5, /device:TPU:1, one launch (start us, length us, event | category | flops | bytes accessed | tf_op | source)
XLA Modules:
  0.0 111.3 jit_solution(8986736233100252588)
XLA Ops:
  0.6 1.8 %modal.1 = (bf16[128,128]{1,0:T(8,128)(2,1)}, bf16[128,1024]{1,0:T(8,128)(2,1)S(1)}) custom-call(s32[8]{0:T(128)} %blocks_hbm.1, bf16[1024,128]{1,0:T(8,128)(2,1)} %field_ref.1), custom_call_target="tpu_custom_call" | custom-call | tf_op jit(solution)/shard_map/modal/pallas_call | solution.py:316
  2.5 0.0 copy-start.4
  2.5 18.2 %all-to-all-start = ((bf16[64,2,128]{2,1,0:T(2,128)(2,1)}), bf16[64,2,128]{2,1,0:T(2,128)(2,1)S(1)}, u32[]{:S(2)}, u32[]{:S(2)}) async-start(bf16[64,2,128]{2,1,0:T(2,128)(2,1)} %bitcast), calls=%async_computation | async-start | bytes 65536 | tf_op jit(solution)/shard_map/all_to_all | solution.py:280
  20.6 0.0 copy-done.4
  20.7 0.1 fusion.12
  20.8 0.0 copy-start.5
  20.8 0.0 copy-start.2
  20.8 0.6 copy-done.5
  21.5 0.1 copy-done.2
  21.5 0.0 copy-start.3
  21.5 0.1 copy.17
  21.7 0.6 copy-done.3
  22.3 0.1 copy.18
  22.4 0.0 copy-start
  22.5 0.0 copy-start.6
  22.5 0.1 fusion.10
  22.6 0.6 copy-done.6
  23.2 0.1 maximum_bitcast_fusion.bout_ref
  23.2 0.2 copy-done
  23.4 0.1 copy.16
  23.6 0.2 copy.15
  23.7 0.0 copy-start.1
  23.8 10.0 %all-to-all-done = bf16[64,2,128]{2,1,0:T(2,128)(2,1)S(1)} async-done(((bf16[64,2,128]{2,1,0:T(2,128)(2,1)}), bf16[64,2,128]{2,1,0:T(2,128)(2,1)S(1)}, u32[]{:S(2)}, u32[]{:S(2)}) %all-to-all-start) | async-done | bytes 32800 | tf_op jit(solution)/shard_map/all_to_all | solution.py:280
  33.8 0.2 mix.1
  34.0 17.2 %all_to_all.37 = bf16[64,2,128]{2,1,0:T(2,128)(2,1)S(1)} all-to-all(bf16[64,2,128]{2,1,0:T(2,128)(2,1)S(1)} %bitcast.37), channel_id=1, replica_groups=mesh['grid'=64,'dp'=8] {'grid'}, dimensions={0} | all-to-all | bytes 65536 | tf_op jit(solution)/shard_map/all_to_all | solution.py:280
  51.2 0.0 copy-done.1
  51.2 2.7 %cells.1 = (bf16[1024,128]{1,0:T(8,128)(2,1)}, bf16[512,128]{1,0:T(8,128)(2,1)S(1)}) custom-call(bf16[128,128]{1,0:T(8,128)(2,1)S(1)} %bitcast.33, bf16[128,1024]{1,0:T(8,128)(2,1)S(1)} %get-tuple-element.33.table_ref, bf16[1024,256]{1,0:T(8,128)(2,1)S(1)} %pad_maximum_fusion.table_tt_ref, bf16[1024,128]{1,0:T(8,128)(2,1)S(1)} %copy-done.1, ...), custom_call_target="tpu_custom_call" | custom-call | tf_op jit(solution)/shard_map/cells/pallas_call | solution.py:356
  53.9 21.0 %all_to_all.38 = bf16[64,8,128]{2,1,0:T(8,128)(2,1)S(1)} all-to-all(bf16[64,8,128]{2,1,0:T(8,128)(2,1)S(1)} %bitcast.35), channel_id=1, replica_groups=mesh['grid'=64,'dp'=8] {'grid'}, dimensions={0} | all-to-all | bytes 262144 | tf_op jit(solution)/shard_map/all_to_all | solution.py:280
  74.9 0.2 share.1
  75.1 12.8 %all_to_all.39 = f32[8,16,128]{2,1,0:T(8,128)S(1)} all-to-all(f32[8,16,128]{2,1,0:T(8,128)S(1)} %bitcast.36), channel_id=1, replica_groups=mesh['grid'=64,'dp'=8] {'dp'}, dimensions={0} | all-to-all | bytes 131072 | tf_op jit(solution)/shard_map/all_to_all | solution.py:280
  88.0 22.3 %all_to_all.40 = bf16[64,8,128]{2,1,0:T(8,128)(2,1)S(1)} all-to-all(bf16[64,8,128]{2,1,0:T(8,128)(2,1)S(1)} %bitcast.32), channel_id=1, replica_groups=mesh['grid'=64,'dp'=8] {'grid'}, dimensions={0} | all-to-all | bytes 262144 | tf_op jit(solution)/shard_map/all_to_all | solution.py:280
  110.3 1.0 final.1
  (7 shorter events, 0.1 us)
Async XLA Ops:
  2.5 18.2 %copy-start.4 = (bf16[2,1,64,64]{3,2,1,0:T(8,128)(2,1)S(1)}, bf16[2,1,64,64]{3,2,1,0:T(8,128)(2,1)}, u32[]{:S(2)}) copy-start(bf16[2,1,64,64]{3,2,1,0:T(8,128)(2,1)} %param.11) | copy-start | bytes 49156
  2.5 31.4 %all-to-all-start = ((bf16[64,2,128]{2,1,0:T(2,128)(2,1)}), bf16[64,2,128]{2,1,0:T(2,128)(2,1)S(1)}, u32[]{:S(2)}, u32[]{:S(2)}) async-start(bf16[64,2,128]{2,1,0:T(2,128)(2,1)} %bitcast), calls=%async_computation | async-start | bytes 65536 | tf_op jit(solution)/shard_map/all_to_all | solution.py:280
  20.8 0.7 copy-start.5
  20.8 0.8 copy-start.2
  21.5 0.8 copy-start.3
  22.4 1.0 copy-start
  22.5 0.7 copy-start.6
  23.7 27.4 %copy-start.1 = (bf16[1024,128]{1,0:T(8,128)(2,1)S(1)}, bf16[1024,128]{1,0:T(8,128)(2,1)}, u32[]{:S(2)}) copy-start(bf16[1024,128]{1,0:T(8,128)(2,1)} %field_ref.1) | copy-start | bytes 786436

commit v6 on v5

--- a/solution.py
+++ b/solution.py
@@ -89,6 +89,78 @@
     wide_ref[pl.ds(0, count, stride=2), :] = modal[:count]
     wide_ref[pl.ds(1, count, stride=2), :] = modal[count:]
     modal_ref[...] = wide_ref[...].astype(BF16)
+
+
+def prepare_kernel(
+    spectral_hbm,
+    win_hbm,
+    wout_hbm,
+    bin_hbm,
+    bout_hbm,
+    cot_hbm,
+    field_hbm,
+    table_ref,
+    mix_ref,
+    back_ref,
+    win_two_ref,
+    win_back_ref,
+    bin_two_ref,
+    wout_two_ref,
+    wout_back_ref,
+    bout_two_ref,
+    table_tt_ref,
+    cot_ref,
+    cot_t_ref,
+    field_ref,
+    s_ref,
+    win_ref,
+    wout_ref,
+    bin_ref,
+    bout_ref,
+    sems,
+):
+    pairs = (
+        (spectral_hbm, s_ref),
+        (win_hbm, win_ref),
+        (wout_hbm, wout_ref),
+        (bin_hbm, bin_ref),
+        (bout_hbm, bout_ref),
+        (cot_hbm, cot_ref),
+        (field_hbm, field_ref),
+    )
+    copies = [pltpu.make_async_copy(a, b, sems.at[i]) for i, (a, b) in enumerate(pairs)]
+    for copy in copies:
+        copy.start()
+    rows = cot_ref.shape[0]
+    width = 2 * table_ref.shape[0]
+    for a in range(rows // LANES):
+        span = pl.ds(a * LANES, LANES)
+        flipped = table_ref[:, span].astype(F32).T.astype(BF16)
+        table_tt_ref[span, : width // 2] = flipped
+        table_tt_ref[span, width // 2 :] = flipped
+    for copy in copies:
+        copy.wait()
+    s_re, s_im = twice_diag(s_ref[0]), twice_diag(s_ref[1])
+    mix_ref[...] = jnp.concatenate([s_re, s_im], axis=1)
+    back_ref[...] = jnp.concatenate([s_re, s_im], axis=0)
+    put_twice_diag(win_two_ref, win_back_ref, win_ref[...])
+    put_twice_diag(wout_back_ref, wout_two_ref, wout_ref[...])
+    bin_two_ref[...] = jnp.concatenate([bin_ref[...]] * 2, axis=1)
+    bout_two_ref[...] = jnp.concatenate([bout_ref[...]] * 2, axis=1)
+    for a in range(rows // LANES):
+        span = pl.ds(a * LANES, LANES)
+        cot_t_ref[:, span] = cot_ref[span, :].astype(F32).T.astype(BF16)
+
+
+def put_twice_diag(wide_ref, tall_ref, x):
+    chans, hid = x.shape
+    wide_ref[...] = jnp.zeros_like(wide_ref)
+    wide_ref[:chans, :hid] = x
+    wide_ref[chans:, hid:] = x
+    flipped = x.astype(F32).T.astype(BF16)
+    zero = jnp.zeros_like(flipped)
+    tall_ref[:hid, :] = jnp.concatenate([flipped, zero], axis=1)
+    tall_ref[hid:, :] = jnp.concatenate([zero, flipped], axis=1)
 
 
 def complex_rows(x, weights, axis, sign):
@@ -305,13 +377,6 @@
     dp = lax.axis_size("dp")
     inv_cols = 1.0 / (ncol * dp)
     count = mode_blocks.shape[0] * BLK
-    s_re, s_im = spectral[0, 0], spectral[1, 0]
-    mix_weights = jnp.concatenate([twice_diag(s_re), twice_diag(s_im)], axis=1)
-    back_weights = jnp.concatenate([twice_diag(s_re), twice_diag(s_im)], axis=0)
-    w_in_two, w_out_two = twice_diag(w_in), twice_diag(w_out)
-    w_in_back, w_out_back = twice_diag(w_in.T), twice_diag(w_out.T)
-    b_in_two = jnp.concatenate([b_in, b_in]).reshape(1, 2 * hid)
-    b_out_two = jnp.concatenate([b_out, b_out]).reshape(1, width)
 
     modal, table = call(
         modal_kernel,
@@ -329,25 +394,50 @@
         pltpu.with_memory_space_constraint(mode_blocks, pltpu.HBM),
         pltpu.with_memory_space_constraint(field, pltpu.HBM),
     )
-    recv, ready = lax.optimization_barrier(
-        (
-            exchange_pairs(modal, "grid"),
-            (
-                jnp.concatenate([table.T, table.T], axis=1),
-                cotangent.T,
-                mix_weights,
-                back_weights,
-                w_in_two,
-                w_in_back,
-                b_in_two,
-                w_out_two,
-                w_out_back,
-                b_out_two,
-            ),
-        )
-    )
-    table_tt, cotangent_t, mix_weights, back_weights = ready[:4]
-    w_in_two, w_in_back, b_in_two, w_out_two, w_out_back, b_out_two = ready[4:]
+    recv = exchange_pairs(modal, "grid")
+    sources = (
+        spectral.reshape(2, chans, chans),
+        w_in,
+        w_out.T,
+        b_in.reshape(1, hid),
+        b_out.reshape(1, chans),
+        cotangent,
+        field,
+    )
+    (
+        mix_weights,
+        back_weights,
+        w_in_two,
+        w_in_back,
+        b_in_two,
+        w_out_two,
+        w_out_back,
+        b_out_two,
+        table_tt,
+        cotangent_here,
+        cotangent_t,
+        field_here,
+    ) = call(
+        prepare_kernel,
+        "prepare",
+        [
+            ((width, 2 * width), BF16),
+            ((2 * width, width), BF16),
+            ((width, 2 * hid), BF16),
+            ((2 * hid, width), BF16),
+            ((1, 2 * hid), F32),
+            ((2 * hid, width), BF16),
+            ((width, 2 * hid), BF16),
+            ((1, width), F32),
+            ((rows, 4 * count), BF16),
+            ((rows, width), BF16),
+            ((width, rows), BF16),
+            ((rows, width), BF16),
+        ],
+        [HBM] * len(sources) + [VMEM],
+        [pltpu.VMEM(a.shape, a.dtype) for a in sources[:5]]
+        + [pltpu.SemaphoreType.DMA((len(sources),))],
+    )(*(pltpu.with_memory_space_constraint(a, pltpu.HBM) for a in sources), table)
     mixed, modal_sum = call(
         mix_kernel, "mix", [((2 * grid, width), BF16), ((TILE, width), F32)], [VMEM] * 2
     )(recv, mix_weights)
@@ -370,8 +460,8 @@
         piece,
         table,
         table_tt,
-        field,
-        cotangent,
+        field_here,
+        cotangent_here,
         cotangent_t,
         w_in_two,
         w_in_back,
@@ -400,7 +490,7 @@
         ],
         [VMEM] * 4,
         [pltpu.VMEM((TILE * grid, width), F32)],
-    )(exchange(own, "grid"), shares, table_tt, cotangent)
+    )(exchange(own, "grid"), shares, table_tt, cotangent_here)
     return (
         output,
         field_grad,

time: 112 us -> 112 us (level)
  local copies, waits for them, and re-layouts: 2.78 us -> 0 us
  waiting for transfers between devices: 10 us -> 11.7 us
  Pallas kernels: 5.9 us -> 7.37 us
    unnamed x17 -> x0, local copies, waits for them, and re-layouts: 2.52 us -> none
    all_to_all x1, waiting for transfers between devices: 10 us -> 11.7 us  [exchange(): return lax.all_to_all(x, axis, 0, 0, tiled=True)]
    pallas_call x0 -> x1, Pallas kernels: none -> 1.47 us  [local(): call(prepare_kernel, 'prepare', [((width, 2 * width), BF16), ((2 * width,...]
  transfers between devices with their start and end apart: 1 -> 1, of which waited for: 1 -> 1; matrix products, arithmetic and copies ran while one was open for 1% -> 0% of each run, Pallas kernels for 0% -> 1%
where the time goes in v6:
time: 112 us; the launch traced here: 111 us
  blocking collectives  73.4 us (66%)
  starting transfers between devices  18.2 us (16%)
  waiting for transfers between devices  11.7 us (10%)
  Pallas kernels  7.37 us (7%)
    all_to_all x4, blocking collectives, exchange(): return lax.all_to_all(x, axis, 0, 0, tiled=True)  73.4 us
    all_to_all x1, starting transfers between devices, exchange(): return lax.all_to_all(x, axis, 0, 0, tiled=True)  18.2 us
    all_to_all x1, waiting for transfers between devices, exchange(): return lax.all_to_all(x, axis, 0, 0, tiled=True)  11.7 us
    pallas_call x1, Pallas kernels, local(): call(functools.partial(cells_kernel, 256), 'cells', [((rows, width), BF16...  2.67 us
  transfers between devices with their start and end apart: 1, of which 1 were waited for; matrix products, arithmetic and copies ran while one was open for 0% of the time, Pallas kernels for 1%

profile of v6, /device:TPU:1, one launch (start us, length us, event | category | flops | bytes accessed | tf_op | source)
XLA Modules:
  0.0 111.3 jit_solution(12024687504614034028)
XLA Ops:
  0.6 1.8 %modal.1 = (bf16[128,128]{1,0:T(8,128)(2,1)}, bf16[128,1024]{1,0:T(8,128)(2,1)S(1)}) custom-call(s32[8]{0:T(128)} %blocks_hbm.1, bf16[1024,128]{1,0:T(8,128)(2,1)} %field_hbm.3), custom_call_target="tpu_custom_call" | custom-call | tf_op jit(solution)/shard_map/modal/pallas_call | solution.py:381
  2.5 18.2 %all-to-all-start = ((bf16[64,2,128]{2,1,0:T(2,128)(2,1)}), bf16[64,2,128]{2,1,0:T(2,128)(2,1)S(1)}, u32[]{:S(2)}, u32[]{:S(2)}) async-start(bf16[64,2,128]{2,1,0:T(2,128)(2,1)} %bitcast), calls=%async_computation | async-start | bytes 65536 | tf_op jit(solution)/shard_map/all_to_all | solution.py:352
  20.6 1.5 %prepare.1 = (bf16[128,256]{1,0:T(8,128)(2,1)S(1)}, bf16[256,128]{1,0:T(8,128)(2,1)S(1)}, bf16[128,512]{1,0:T(8,128)(2,1)S(1)}, bf16[512,128]{1,0:T(8,128)(2,1)S...) custom-call(bf16[2,64,64]{2,1,0:T(8,128)(2,1)} %bitcast.30, ...), custom_call_target="tpu_custom_call" | custom-call | tf_op jit(solution)/shard_map/prepare/pallas_call | solution.py:420
  22.1 11.7 %all-to-all-done = bf16[64,2,128]{2,1,0:T(2,128)(2,1)S(1)} async-done(((bf16[64,2,128]{2,1,0:T(2,128)(2,1)}), bf16[64,2,128]{2,1,0:T(2,128)(2,1)S(1)}, u32[]{:S(2)}, u32[]{:S(2)}) %all-to-all-start) | async-done | bytes 32800 | tf_op jit(solution)/shard_map/all_to_all | solution.py:352
  33.8 0.2 mix.1
  34.0 17.2 %all_to_all.37 = bf16[64,2,128]{2,1,0:T(2,128)(2,1)S(1)} all-to-all(bf16[64,2,128]{2,1,0:T(2,128)(2,1)S(1)} %bitcast.29), channel_id=1, replica_groups=mesh['grid'=64,'dp'=8] {'grid'}, dimensions={0} | all-to-all | bytes 65536 | tf_op jit(solution)/shard_map/all_to_all | solution.py:352
  51.2 2.7 %cells.1 = (bf16[1024,128]{1,0:T(8,128)(2,1)}, bf16[512,128]{1,0:T(8,128)(2,1)S(1)}) custom-call(bf16[128,128]{1,0:T(8,128)(2,1)S(1)} %bitcast.25, bf16[128,1024]{1,0:T(8,128)(2,1)S(1)} %get-tuple-element.34.table_ref, bf16[1024,256]{1,0:T(8,128)(2,1)S(1)} %get-tuple-element.37.table_tt_ref, bf16[1024,128]{1,0:T(8,128)(2,1)S(1)} %get-tuple-element.38.field_ref, ...), custom_call_target="tpu_custom_call" | custom-call | tf_op jit(solution)/shard_map/cells/pallas_call | solution.py:446
  53.8 21.1 %all_to_all.38 = bf16[64,8,128]{2,1,0:T(8,128)(2,1)S(1)} all-to-all(bf16[64,8,128]{2,1,0:T(8,128)(2,1)S(1)} %bitcast.27), channel_id=1, replica_groups=mesh['grid'=64,'dp'=8] {'grid'}, dimensions={0} | all-to-all | bytes 262144 | tf_op jit(solution)/shard_map/all_to_all | solution.py:352
  74.9 0.2 share.1
  75.1 12.8 %all_to_all.39 = f32[8,16,128]{2,1,0:T(8,128)S(1)} all-to-all(f32[8,16,128]{2,1,0:T(8,128)S(1)} %bitcast.28), channel_id=1, replica_groups=mesh['grid'=64,'dp'=8] {'dp'}, dimensions={0} | all-to-all | bytes 131072 | tf_op jit(solution)/shard_map/all_to_all | solution.py:352
  88.0 22.3 %all_to_all.40 = bf16[64,8,128]{2,1,0:T(8,128)(2,1)S(1)} all-to-all(bf16[64,8,128]{2,1,0:T(8,128)(2,1)S(1)} %bitcast.24), channel_id=1, replica_groups=mesh['grid'=64,'dp'=8] {'grid'}, dimensions={0} | all-to-all | bytes 262144 | tf_op jit(solution)/shard_map/all_to_all | solution.py:352
  110.3 1.0 final.1
  (1 shorter events, 0.0 us)
Async XLA Ops:
  2.5 31.4 %all-to-all-start = ((bf16[64,2,128]{2,1,0:T(2,128)(2,1)}), bf16[64,2,128]{2,1,0:T(2,128)(2,1)S(1)}, u32[]{:S(2)}, u32[]{:S(2)}) async-start(bf16[64,2,128]{2,1,0:T(2,128)(2,1)} %bitcast), calls=%async_computation | async-start | bytes 65536 | tf_op jit(solution)/shard_map/all_to_all | solution.py:352

commit v7 on v6

--- a/solution.py
+++ b/solution.py
@@ -16,6 +16,7 @@
 BF16 = jnp.bfloat16
 VMEM = pl.BlockSpec(memory_space=pltpu.VMEM)
 HBM = pl.BlockSpec(memory_space=pltpu.HBM)
+OWN = 6
 
 
 def call(kernel, name, outs, specs, scratch=()):
@@ -92,6 +93,7 @@
 
 
 def prepare_kernel(
+    blocks_hbm,
     spectral_hbm,
     win_hbm,
     wout_hbm,
@@ -112,6 +114,9 @@
     cot_ref,
     cot_t_ref,
     field_ref,
+    zero_row_ref,
+    zero_own_ref,
+    blocks_ref,
     s_ref,
     win_ref,
     wout_ref,
@@ -120,6 +125,7 @@
     sems,
 ):
     pairs = (
+        (blocks_hbm, blocks_ref),
         (spectral_hbm, s_ref),
         (win_hbm, win_ref),
         (wout_hbm, wout_ref),
@@ -140,6 +146,14 @@
         table_tt_ref[span, width // 2 :] = flipped
     for copy in copies:
         copy.wait()
+    count = zero_row_ref.shape[0]
+    row = row_id((count, LANES))
+    at = jnp.int32(0)
+    for b in range(blocks_ref.shape[0]):
+        at = jnp.where(blocks_ref[b] == 0, b * BLK, at)
+    zero_row_ref[...] = jnp.where(row == at, 1.0, 0.0)
+    own = jnp.full((TILE, LANES), lax.axis_index("grid"), jnp.int32)
+    zero_own_ref[...] = jnp.where(own == at, 1.0, 0.0)
     s_re, s_im = twice_diag(s_ref[0]), twice_diag(s_ref[1])
     mix_ref[...] = jnp.concatenate([s_re, s_im], axis=1)
     back_ref[...] = jnp.concatenate([s_re, s_im], axis=0)
@@ -211,6 +225,7 @@
     wout_ref,
     wout_t_ref,
     bout_ref,
+    zero_row_ref,
     out_hbm,
     parts_ref,
     wide_ref,
@@ -252,22 +267,17 @@
     g_in = by_in[:chans, :hid] + by_in[chans:, hid:]
     g_out = by_out[:chans, :hid] + by_out[chans:, hid:]
     b_in = b_in[:, :hid] + b_in[:, hid:]
-    b_out = (sums_out + pltpu.roll(sums_out, chans, 1))[:1]
-    row = row_id((count, LANES))
-    bias = jnp.where(
-        row == 0,
-        b_in[:, :LANES],
-        jnp.where(row == 1, b_in[:, LANES:], jnp.where(row == 2, b_out, 0.0)),
-    )
+    b_out = halves((sums_out + pltpu.roll(sums_out, chans, 1))[:1])
     for r, block in enumerate(
         (
             grad_modal[:count],
-            grad_modal[count:],
+            jnp.where(zero_row_ref[...] > 0.0, b_out, grad_modal[count:]),
             g_in[:, :LANES],
             g_in[:, LANES:],
             g_out[:, :LANES],
             g_out[:, LANES:],
-            *split(bias),
+            jnp.broadcast_to(b_in[:, :LANES], (count, LANES)),
+            jnp.broadcast_to(b_in[:, LANES:], (count, LANES)),
         )
     ):
         sums_ref[pl.ds(r, count, stride=TILE), :] = block
@@ -281,24 +291,38 @@
     return jnp.concatenate([high, low], axis=0).astype(BF16)
 
 
+def halves(x):
+    high, low = split(x)
+    lane = lax.broadcasted_iota(jnp.int32, x.shape, 1)
+    return jnp.where(lane < LANES // 2, high, low)
+
+
 def split(x):
     high = x.astype(BF16).astype(F32)
     return high, x - high
 
 
-def share_kernel(recv_ref, modal_ref, weights_ref, share_ref, grad_in_ref):
+def share_kernel(recv_ref, modal_ref, weights_ref, zero_own_ref, share_ref, grad_in_ref):
     x = jnp.sum(recv_ref[...].astype(F32).reshape(-1, TILE, LANES), axis=0)
-    x = jnp.where(row_id(x.shape) == 6, x + pltpu.roll(x, TILE - 1, 0), x)
-    both = jnp.concatenate([x, modal_ref[...]], axis=0)
+    row = row_id(x.shape)
+    owner = zero_own_ref[...] > 0.0
+    extra = jnp.where(owner & (row == 2), pltpu.roll(x, 1, 0), 0.0)
+    x = jnp.where(owner & (row == 1), 0.0, x)
+    both = jnp.concatenate([x, jnp.where(row < 2, modal_ref[...], extra)], axis=0)
     share_ref[...] = jnp.concatenate([both] * (share_ref.shape[0] // (2 * TILE)), axis=0)
     grad = jnp.concatenate([x[:2]] * (TILE // 2), axis=0)
     grad_in_ref[...] = complex_rows(grad, weights_ref[...], 1, 1.0)
 
 
-def total_kernel(scale, shares_ref, grad_in_ref, out_ref):
-    x = jnp.sum(shares_ref[...].reshape(-1, 2 * TILE, LANES), axis=0)[:TILE]
-    own = jnp.where(row_id((TILE, LANES)) < 2, grad_in_ref[...], x * scale)
-    out_ref[...] = jnp.concatenate([own] * (out_ref.shape[0] // TILE), axis=0).astype(BF16)
+def total_kernel(scale, shares_ref, grad_in_ref, zero_own_ref, out_ref):
+    x = jnp.sum(shares_ref[...].reshape(-1, 2 * TILE, LANES), axis=0) * scale
+    bias = x[TILE + 2 : TILE + 3]
+    bias = halves(bias + pltpu.roll(bias, LANES // 2, 1))
+    row = row_id((TILE, LANES))
+    own = jnp.where(row < 2, grad_in_ref[...], x[:TILE])
+    own = jnp.where((zero_own_ref[...] > 0.0) & (row == 1), bias, own)
+    group = jnp.concatenate([own[:OWN]] * 4, axis=0)
+    out_ref[...] = jnp.concatenate([group] * (out_ref.shape[0] // (4 * OWN)), axis=0).astype(BF16)
 
 
 def final_kernel(
@@ -307,6 +331,7 @@
     shares_ref,
     table_tt_ref,
     cot_ref,
+    zero_row_ref,
     fgrad_ref,
     spectral_ref,
     win_ref,
@@ -317,7 +342,7 @@
 ):
     count = table_tt_ref.shape[1] // 4
     wide_ref[...] = recv_ref[...].astype(F32)
-    rows = [every(wide_ref, r, count, TILE) for r in range(TILE - 1)]
+    rows = [every(wide_ref, r, count, OWN) for r in range(OWN)]
     grad_in = jnp.concatenate(rows[:2], axis=0).astype(BF16)
     back = dot(table_tt_ref[:, : 2 * count], grad_in)
     fgrad_ref[...] = (cot_ref[...].astype(F32) + back).astype(BF16)
@@ -325,9 +350,12 @@
     win_ref[:, LANES:] = rows[3]
     wout_ref[:, :LANES] = rows[4]
     wout_ref[:, LANES:] = rows[5]
-    bin_ref[:, :LANES] = rows[6][0:1]
-    bin_ref[:, LANES:] = rows[6][1:2]
-    bout_ref[...] = rows[6][2:3, : bout_ref.shape[1]]
+    n = shares_ref.shape[0] // (2 * TILE)
+    for r in range(2):
+        b_in = jnp.sum(every(shares_ref, OWN + r, n, 2 * TILE), axis=0, keepdims=True)
+        bin_ref[:, r * LANES : (r + 1) * LANES] = b_in * scale
+    b_out = jnp.sum(jnp.where(zero_row_ref[...] > 0.0, rows[1], 0.0), axis=0, keepdims=True)
+    bout_ref[...] = (b_out + pltpu.roll(b_out, LANES // 2, 1))[:, : bout_ref.shape[1]]
     spectral_sums(scale, shares_ref, spectral_ref)
 
 
@@ -396,6 +424,7 @@
     )
     recv = exchange_pairs(modal, "grid")
     sources = (
+        mode_blocks,
         spectral.reshape(2, chans, chans),
         w_in,
         w_out.T,
@@ -417,6 +446,8 @@
         cotangent_here,
         cotangent_t,
         field_here,
+        zero_row,
+        zero_own,
     ) = call(
         prepare_kernel,
         "prepare",
@@ -433,9 +464,12 @@
             ((rows, width), BF16),
             ((width, rows), BF16),
             ((rows, width), BF16),
+            ((count, width), F32),
+            ((TILE, width), F32),
         ],
         [HBM] * len(sources) + [VMEM],
-        [pltpu.VMEM(a.shape, a.dtype) for a in sources[:5]]
+        [pltpu.SMEM(mode_blocks.shape, jnp.int32)]
+        + [pltpu.VMEM(a.shape, a.dtype) for a in sources[1:6]]
         + [pltpu.SemaphoreType.DMA((len(sources),))],
     )(*(pltpu.with_memory_space_constraint(a, pltpu.HBM) for a in sources), table)
     mixed, modal_sum = call(
@@ -447,7 +481,7 @@
         functools.partial(cells_kernel, 256),
         "cells",
         [((rows, width), BF16, HBM), ((TILE * grid, width), BF16)],
-        [VMEM] * 12,
+        [VMEM] * 13,
         [
             pltpu.VMEM((2 * count, width), F32),
             pltpu.VMEM((rows, 2 * hid), BF16),
@@ -469,14 +503,15 @@
         w_out_two,
         w_out_back,
         b_out_two,
+        zero_row,
     )
     share, grad_in = call(
-        share_kernel, "share", [((2 * TILE * dp, width), F32), ((TILE, width), F32)], [VMEM] * 3
-    )(exchange_tiles(parts, "grid"), modal_sum, back_weights)
+        share_kernel, "share", [((2 * TILE * dp, width), F32), ((TILE, width), F32)], [VMEM] * 4
+    )(exchange_tiles(parts, "grid"), modal_sum, back_weights, zero_own)
     shares = exchange(share, "dp")
     (own,) = call(
-        functools.partial(total_kernel, inv_cols), "total", [((TILE * grid, width), BF16)], [VMEM] * 2
-    )(shares, grad_in)
+        functools.partial(total_kernel, inv_cols), "total", [((OWN * grid, width), BF16)], [VMEM] * 3
+    )(shares, grad_in, zero_own)
     field_grad, spectral_grad, w_in_grad, w_out_grad, b_in_grad, b_out_grad = call(
         functools.partial(final_kernel, inv_cols),
         "final",
@@ -488,9 +523,9 @@
             ((1, hid), F32),
             ((1, chans), F32),
         ],
-        [VMEM] * 4,
-        [pltpu.VMEM((TILE * grid, width), F32)],
-    )(exchange(own, "grid"), shares, table_tt, cotangent_here)
+        [VMEM] * 5,
+        [pltpu.VMEM((OWN * grid, width), F32)],
+    )(exchange_pairs(own, "grid"), shares, table_tt, cotangent_here, zero_row)
     return (
         output,
         field_grad,

time: 112 us -> 110 us (0.982)
  blocking collectives: 73.4 us -> 72.1 us
    all_to_all x4, blocking collectives: 73.4 us -> 72.1 us  [exchange(): return lax.all_to_all(x, axis, 0, 0, tiled=True)]
where the time goes in v7:
time: 110 us
  blocking collectives  72.1 us (66%)
  starting transfers between devices  18.2 us (17%)
  waiting for transfers between devices  11.7 us (11%)
  Pallas kernels  7.45 us (7%)
    all_to_all x4, blocking collectives, exchange(): return lax.all_to_all(x, axis, 0, 0, tiled=True)  72.1 us
    all_to_all x1, starting transfers between devices, exchange(): return lax.all_to_all(x, axis, 0, 0, tiled=True)  18.2 us
    all_to_all x1, waiting for transfers between devices, exchange(): return lax.all_to_all(x, axis, 0, 0, tiled=True)  11.7 us
    pallas_call x1, Pallas kernels, local(): call(functools.partial(cells_kernel, 256), 'cells', [((rows, width), BF16...  2.68 us
  transfers between devices with their start and end apart: 1, of which 1 were waited for; matrix products, arithmetic and copies ran while one was open for 0% of the time, Pallas kernels for 1%

profile of v7, /device:TPU:1, one launch (start us, length us, event | category | flops | bytes accessed | tf_op | source)
XLA Modules:
  0.0 110.1 jit_solution(9770271866947500283)
XLA Ops:
  0.6 1.8 %modal.1 = (bf16[128,128]{1,0:T(8,128)(2,1)}, bf16[128,1024]{1,0:T(8,128)(2,1)S(1)}) custom-call(s32[8]{0:T(128)} %blocks_hbm.3, bf16[1024,128]{1,0:T(8,128)(2,1)} %field_hbm.3), custom_call_target="tpu_custom_call" | custom-call | tf_op jit(solution)/shard_map/modal/pallas_call | solution.py:409
  2.5 18.2 %all-to-all-start = ((bf16[64,2,128]{2,1,0:T(2,128)(2,1)}), bf16[64,2,128]{2,1,0:T(2,128)(2,1)S(1)}, u32[]{:S(2)}, u32[]{:S(2)}) async-start(bf16[64,2,128]{2,1,0:T(2,128)(2,1)} %bitcast), calls=%async_computation | async-start | bytes 65536 | tf_op jit(solution)/shard_map/all_to_all | solution.py:380
  20.6 1.5 %prepare.1 = (bf16[128,256]{1,0:T(8,128)(2,1)S(1)}, bf16[256,128]{1,0:T(8,128)(2,1)S(1)}, bf16[128,512]{1,0:T(8,128)(2,1)S(1)}, bf16[512,128]{1,0:T(8,128)(2,1)S...) custom-call(s32[8]{0:T(128)} %blocks_hbm.3, ...), custom_call_target="tpu_custom_call" | custom-call | tf_op jit(solution)/shard_map/prepare/pallas_call | solution.py:451
  22.1 11.7 %all-to-all-done = bf16[64,2,128]{2,1,0:T(2,128)(2,1)S(1)} async-done(((bf16[64,2,128]{2,1,0:T(2,128)(2,1)}), bf16[64,2,128]{2,1,0:T(2,128)(2,1)S(1)}, u32[]{:S(2)}, u32[]{:S(2)}) %all-to-all-start) | async-done | bytes 32800 | tf_op jit(solution)/shard_map/all_to_all | solution.py:380
  33.8 0.2 mix.1
  34.0 17.2 %all_to_all.31 = bf16[64,2,128]{2,1,0:T(2,128)(2,1)S(1)} all-to-all(bf16[64,2,128]{2,1,0:T(2,128)(2,1)S(1)} %bitcast.29), channel_id=1, replica_groups=mesh['grid'=64,'dp'=8] {'grid'}, dimensions={0} | all-to-all | bytes 65536 | tf_op jit(solution)/shard_map/all_to_all | solution.py:380
  51.2 2.7 %cells.1 = (bf16[1024,128]{1,0:T(8,128)(2,1)}, bf16[512,128]{1,0:T(8,128)(2,1)S(1)}) custom-call(bf16[128,128]{1,0:T(8,128)(2,1)S(1)} %bitcast.25, bf16[128,1024]{1,0:T(8,128)(2,1)S(1)} %get-tuple-element.36.table_ref, bf16[1024,256]{1,0:T(8,128)(2,1)S(1)} %get-tuple-element.39.table_tt_ref, bf16[1024,128]{1,0:T(8,128)(2,1)S(1)} %get-tuple-element.40.field_ref, ...), custom_call_target="tpu_custom_call" | custom-call | tf_op jit(solution)/shard_map/cells/pallas_call | solution.py:480
  53.9 21.1 %all_to_all.32 = bf16[64,8,128]{2,1,0:T(8,128)(2,1)S(1)} all-to-all(bf16[64,8,128]{2,1,0:T(8,128)(2,1)S(1)} %bitcast.27), channel_id=1, replica_groups=mesh['grid'=64,'dp'=8] {'grid'}, dimensions={0} | all-to-all | bytes 262144 | tf_op jit(solution)/shard_map/all_to_all | solution.py:380
  74.9 0.2 share.1
  75.1 12.8 %all_to_all.33 = f32[8,16,128]{2,1,0:T(8,128)S(1)} all-to-all(f32[8,16,128]{2,1,0:T(8,128)S(1)} %bitcast.28), channel_id=1, replica_groups=mesh['grid'=64,'dp'=8] {'dp'}, dimensions={0} | all-to-all | bytes 131072 | tf_op jit(solution)/shard_map/all_to_all | solution.py:380
  88.0 0.1 total.1
  88.1 21.0 %all_to_all.34 = bf16[192,2,128]{2,1,0:T(2,128)(2,1)S(1)} all-to-all(bf16[192,2,128]{2,1,0:T(2,128)(2,1)S(1)} %bitcast.23), channel_id=1, replica_groups=mesh['grid'=64,'dp'=8] {'grid'}, dimensions={0} | all-to-all | bytes 196608 | tf_op jit(solution)/shard_map/all_to_all | solution.py:380
  109.1 1.0 final.1
Async XLA Ops:
  2.5 31.4 %all-to-all-start = ((bf16[64,2,128]{2,1,0:T(2,128)(2,1)}), bf16[64,2,128]{2,1,0:T(2,128)(2,1)S(1)}, u32[]{:S(2)}, u32[]{:S(2)}) async-start(bf16[64,2,128]{2,1,0:T(2,128)(2,1)} %bitcast), calls=%async_computation | async-start | bytes 65536 | tf_op jit(solution)/shard_map/all_to_all | solution.py:380

commit v8 on v7

--- a/solution.py
+++ b/solution.py
@@ -35,6 +35,10 @@
     return jnp.dot(a, b, preferred_element_type=F32)
 
 
+def dot_on(a, b, over_a, over_b):
+    return lax.dot_general(a, b, (((over_a,), (over_b,)), ((), ())), preferred_element_type=F32)
+
+
 def row_id(shape):
     return lax.broadcasted_iota(jnp.int32, shape, 0)
 
@@ -58,62 +62,32 @@
     return jnp.where(((quad + 1) & 2) != 0, -c, c), jnp.where((quad & 2) != 0, -s, s)
 
 
-def modal_kernel(
-    blocks_hbm, field_hbm, modal_ref, table_ref, blocks_ref, field_ref, wide_ref, blocks_sem, field_sem
-):
-    blocks_copy = pltpu.make_async_copy(blocks_hbm, blocks_ref, blocks_sem)
-    blocks_copy.start()
-    field_copy = pltpu.make_async_copy(field_hbm, field_ref, field_sem)
-    field_copy.start()
-    blocks_copy.wait()
-    kblocks = blocks_ref.shape[0]
-    count = kblocks * BLK
-    rows = field_ref.shape[0]
-    first = lax.axis_index("grid") * rows
-    base = jnp.concatenate(
-        [jnp.full((BLK, LANES), blocks_ref[b] * BLK, jnp.int32) for b in range(kblocks)], axis=0
-    )
-    modes = base + row_id((count, LANES)) % BLK
-    lane = lax.broadcasted_iota(jnp.int32, (count, LANES), 1)
-    scale = 1.0 / math.sqrt(NX)
-    near_c, near_s = cos_sin((modes * lane) & (NX - 1))
-    near_c, near_s = near_c * scale, near_s * scale
-    far_c, far_s = cos_sin((modes * (first + lane * LANES)) & (NX - 1))
-    for a in range(rows // LANES):
-        ca = jnp.broadcast_to(far_c[:, a : a + 1], (count, LANES))
-        sa = jnp.broadcast_to(far_s[:, a : a + 1], (count, LANES))
-        span = pl.ds(a * LANES, LANES)
-        table_ref[:count, span] = (near_c * ca - near_s * sa).astype(BF16)
-        table_ref[count:, span] = (-(near_s * ca + near_c * sa)).astype(BF16)
-    field_copy.wait()
-    modal = dot(table_ref[...], field_ref[...])
-    wide_ref[pl.ds(0, count, stride=2), :] = modal[:count]
-    wide_ref[pl.ds(1, count, stride=2), :] = modal[count:]
-    modal_ref[...] = wide_ref[...].astype(BF16)
-
-
-def prepare_kernel(
+def twice_diag(x):
+    zero = jnp.zeros_like(x)
+    return jnp.concatenate(
+        [jnp.concatenate([x, zero], axis=1), jnp.concatenate([zero, x], axis=1)], axis=0
+    )
+
+
+def first_kernel(
     blocks_hbm,
+    field_hbm,
     spectral_hbm,
     win_hbm,
     wout_hbm,
     bin_hbm,
     bout_hbm,
     cot_hbm,
-    field_hbm,
+    modal_ref,
     table_ref,
+    field_ref,
+    cot_ref,
     mix_ref,
     back_ref,
     win_two_ref,
-    win_back_ref,
+    wout_two_ref,
     bin_two_ref,
-    wout_two_ref,
-    wout_back_ref,
     bout_two_ref,
-    table_tt_ref,
-    cot_ref,
-    cot_t_ref,
-    field_ref,
     zero_row_ref,
     zero_own_ref,
     blocks_ref,
@@ -122,59 +96,66 @@
     wout_ref,
     bin_ref,
     bout_ref,
+    wide_ref,
     sems,
 ):
     pairs = (
         (blocks_hbm, blocks_ref),
+        (field_hbm, field_ref),
         (spectral_hbm, s_ref),
         (win_hbm, win_ref),
         (wout_hbm, wout_ref),
         (bin_hbm, bin_ref),
         (bout_hbm, bout_ref),
         (cot_hbm, cot_ref),
-        (field_hbm, field_ref),
     )
     copies = [pltpu.make_async_copy(a, b, sems.at[i]) for i, (a, b) in enumerate(pairs)]
     for copy in copies:
         copy.start()
-    rows = cot_ref.shape[0]
-    width = 2 * table_ref.shape[0]
+    win_two_ref[...] = jnp.zeros_like(win_two_ref)
+    wout_two_ref[...] = jnp.zeros_like(wout_two_ref)
+    copies[0].wait()
+    kblocks = blocks_ref.shape[0]
+    count = kblocks * BLK
+    rows = field_ref.shape[0]
+    index = lax.axis_index("grid")
+    base = jnp.concatenate(
+        [jnp.full((BLK, LANES), blocks_ref[b] * BLK, jnp.int32) for b in range(kblocks)], axis=0
+    )
+    modes = base + row_id((count, LANES)) % BLK
+    lane = lax.broadcasted_iota(jnp.int32, (count, LANES), 1)
+    scale = 1.0 / math.sqrt(NX)
+    near_c, near_s = cos_sin((modes * lane) & (NX - 1))
+    near_c, near_s = near_c * scale, near_s * scale
+    far_c, far_s = cos_sin((modes * (index * rows + lane * LANES)) & (NX - 1))
     for a in range(rows // LANES):
+        ca = jnp.broadcast_to(far_c[:, a : a + 1], (count, LANES))
+        sa = jnp.broadcast_to(far_s[:, a : a + 1], (count, LANES))
         span = pl.ds(a * LANES, LANES)
-        flipped = table_ref[:, span].astype(F32).T.astype(BF16)
-        table_tt_ref[span, : width // 2] = flipped
-        table_tt_ref[span, width // 2 :] = flipped
-    for copy in copies:
+        table_ref[:count, span] = (near_c * ca - near_s * sa).astype(BF16)
+        table_ref[count:, span] = (-(near_s * ca + near_c * sa)).astype(BF16)
+    copies[1].wait()
+    modal = dot(table_ref[...], field_ref[...])
+    wide_ref[pl.ds(0, count, stride=2), :] = modal[:count]
+    wide_ref[pl.ds(1, count, stride=2), :] = modal[count:]
+    modal_ref[...] = wide_ref[...].astype(BF16)
+    zero_row_ref[...] = jnp.where(modes == 0, 1.0, 0.0)
+    at = jnp.int32(0)
+    for b in range(kblocks):
+        at = jnp.where(blocks_ref[b] == 0, b * BLK, at)
+    own = jnp.full((TILE, LANES), index, jnp.int32)
+    zero_own_ref[...] = jnp.where(own == at, 1.0, 0.0)
+    for copy in copies[2:]:
         copy.wait()
-    count = zero_row_ref.shape[0]
-    row = row_id((count, LANES))
-    at = jnp.int32(0)
-    for b in range(blocks_ref.shape[0]):
-        at = jnp.where(blocks_ref[b] == 0, b * BLK, at)
-    zero_row_ref[...] = jnp.where(row == at, 1.0, 0.0)
-    own = jnp.full((TILE, LANES), lax.axis_index("grid"), jnp.int32)
-    zero_own_ref[...] = jnp.where(own == at, 1.0, 0.0)
     s_re, s_im = twice_diag(s_ref[0]), twice_diag(s_ref[1])
     mix_ref[...] = jnp.concatenate([s_re, s_im], axis=1)
     back_ref[...] = jnp.concatenate([s_re, s_im], axis=0)
-    put_twice_diag(win_two_ref, win_back_ref, win_ref[...])
-    put_twice_diag(wout_back_ref, wout_two_ref, wout_ref[...])
+    chans, hid = win_ref.shape
+    for two_ref, one_ref in ((win_two_ref, win_ref), (wout_two_ref, wout_ref)):
+        two_ref[:chans, :hid] = one_ref[...]
+        two_ref[chans:, hid:] = one_ref[...]
     bin_two_ref[...] = jnp.concatenate([bin_ref[...]] * 2, axis=1)
     bout_two_ref[...] = jnp.concatenate([bout_ref[...]] * 2, axis=1)
-    for a in range(rows // LANES):
-        span = pl.ds(a * LANES, LANES)
-        cot_t_ref[:, span] = cot_ref[span, :].astype(F32).T.astype(BF16)
-
-
-def put_twice_diag(wide_ref, tall_ref, x):
-    chans, hid = x.shape
-    wide_ref[...] = jnp.zeros_like(wide_ref)
-    wide_ref[:chans, :hid] = x
-    wide_ref[chans:, hid:] = x
-    flipped = x.astype(F32).T.astype(BF16)
-    zero = jnp.zeros_like(flipped)
-    tall_ref[:hid, :] = jnp.concatenate([flipped, zero], axis=1)
-    tall_ref[hid:, :] = jnp.concatenate([zero, flipped], axis=1)
 
 
 def complex_rows(x, weights, axis, sign):
@@ -215,14 +196,10 @@
     chunk,
     piece_ref,
     table_ref,
-    table_tt_ref,
     field_ref,
     cot_ref,
-    cot_t_ref,
     win_ref,
-    win_t_ref,
     bin_ref,
-    wout_ref,
     wout_t_ref,
     bout_ref,
     zero_row_ref,
@@ -245,22 +222,23 @@
     copies = []
     for i in range(rows // chunk):
         span = pl.ds(i * chunk, chunk)
-        pre = dot(table_tt_ref[span, :], right) + bin_ref[...]
+        table = table_ref[:, span]
+        pre = dot_on(jnp.concatenate([table, table], axis=0), right, 0, 0) + bin_ref[...]
         gate, slope = gelu_pair(pre)
         hidden = gate.astype(BF16)
         hidden_ref[span, :] = hidden
         gpre_ref[span, :] = (dot(cot_ref[span, :], wout_t_ref[...]) * slope).astype(BF16)
-        out = dot(hidden, wout_ref[...]) + bout_ref[...]
+        out = dot_on(hidden, wout_t_ref[...], 1, 1) + bout_ref[...]
         out_ref[span, :] = (field_ref[span, :].astype(F32) + out).astype(BF16)
         copies.append(pltpu.make_async_copy(out_ref.at[span], out_hbm.at[span], out_sems.at[i]))
         copies[-1].start()
     ones = jnp.ones((2 * TILE, rows), BF16)
     t = dot(jnp.concatenate([table_ref[...], ones], axis=0), gpre_ref[...])
-    by_out = dot(cot_t_ref[...], hidden_ref[...])
+    by_out = dot_on(cot_ref[...], hidden_ref[...], 0, 0)
     sums_out = dot(ones, cot_ref[...])
     b_in = t[2 * count : 2 * count + 1]
     t_parts = stack_parts(t[: 2 * count])
-    grad_modal = dot(t_parts, win_t_ref[...])
+    grad_modal = dot_on(t_parts, win_ref[...], 1, 1)
     grad_modal = 2.0 * (grad_modal[: 2 * count] + grad_modal[2 * count :])
     mixed_t = mixed.T.astype(BF16)
     by_in = dot(jnp.concatenate([mixed_t, mixed_t], axis=1), t_parts)
@@ -329,7 +307,7 @@
     scale,
     recv_ref,
     shares_ref,
-    table_tt_ref,
+    table_ref,
     cot_ref,
     zero_row_ref,
     fgrad_ref,
@@ -340,11 +318,11 @@
     bout_ref,
     wide_ref,
 ):
-    count = table_tt_ref.shape[1] // 4
+    count = table_ref.shape[0] // 2
     wide_ref[...] = recv_ref[...].astype(F32)
     rows = [every(wide_ref, r, count, OWN) for r in range(OWN)]
     grad_in = jnp.concatenate(rows[:2], axis=0).astype(BF16)
-    back = dot(table_tt_ref[:, : 2 * count], grad_in)
+    back = dot_on(table_ref[...], grad_in, 0, 0)
     fgrad_ref[...] = (cot_ref[...].astype(F32) + back).astype(BF16)
     win_ref[:, :LANES] = rows[2]
     win_ref[:, LANES:] = rows[3]
@@ -390,13 +368,6 @@
     return exchange(x.reshape(n, TILE, LANES), axis).reshape(TILE * n, LANES)
 
 
-def twice_diag(x):
-    zero = jnp.zeros_like(x)
-    return jnp.concatenate(
-        [jnp.concatenate([x, zero], axis=1), jnp.concatenate([zero, x], axis=1)], axis=0
-    )
-
-
 def local(field, cotangent, mode_blocks, spectral, w_in, b_in, w_out, b_out):
     rows, width = field.shape
     chans, hid = w_in.shape
@@ -406,82 +377,61 @@
     inv_cols = 1.0 / (ncol * dp)
     count = mode_blocks.shape[0] * BLK
 
-    modal, table = call(
-        modal_kernel,
-        "modal",
-        [((2 * count, width), BF16), ((2 * count, rows), BF16)],
-        [HBM, HBM],
-        [
-            pltpu.SMEM(mode_blocks.shape, jnp.int32),
-            pltpu.VMEM((rows, width), BF16),
-            pltpu.VMEM((2 * count, width), F32),
-            pltpu.SemaphoreType.DMA,
-            pltpu.SemaphoreType.DMA,
-        ],
-    )(
-        pltpu.with_memory_space_constraint(mode_blocks, pltpu.HBM),
-        pltpu.with_memory_space_constraint(field, pltpu.HBM),
-    )
-    recv = exchange_pairs(modal, "grid")
     sources = (
         mode_blocks,
+        field,
         spectral.reshape(2, chans, chans),
         w_in,
         w_out.T,
         b_in.reshape(1, hid),
         b_out.reshape(1, chans),
         cotangent,
-        field,
     )
     (
+        modal,
+        table,
+        field_here,
+        cotangent_here,
         mix_weights,
         back_weights,
         w_in_two,
-        w_in_back,
+        w_out_two,
         b_in_two,
-        w_out_two,
-        w_out_back,
         b_out_two,
-        table_tt,
-        cotangent_here,
-        cotangent_t,
-        field_here,
         zero_row,
         zero_own,
     ) = call(
-        prepare_kernel,
-        "prepare",
+        first_kernel,
+        "first",
         [
+            ((2 * count, width), BF16),
+            ((2 * count, rows), BF16),
+            ((rows, width), BF16),
+            ((rows, width), BF16),
             ((width, 2 * width), BF16),
             ((2 * width, width), BF16),
             ((width, 2 * hid), BF16),
-            ((2 * hid, width), BF16),
+            ((width, 2 * hid), BF16),
             ((1, 2 * hid), F32),
-            ((2 * hid, width), BF16),
-            ((width, 2 * hid), BF16),
             ((1, width), F32),
-            ((rows, 4 * count), BF16),
-            ((rows, width), BF16),
-            ((width, rows), BF16),
-            ((rows, width), BF16),
             ((count, width), F32),
             ((TILE, width), F32),
         ],
-        [HBM] * len(sources) + [VMEM],
+        [HBM] * len(sources),
         [pltpu.SMEM(mode_blocks.shape, jnp.int32)]
-        + [pltpu.VMEM(a.shape, a.dtype) for a in sources[1:6]]
-        + [pltpu.SemaphoreType.DMA((len(sources),))],
-    )(*(pltpu.with_memory_space_constraint(a, pltpu.HBM) for a in sources), table)
+        + [pltpu.VMEM(a.shape, a.dtype) for a in sources[2:7]]
+        + [pltpu.VMEM((2 * count, width), F32), pltpu.SemaphoreType.DMA((len(sources),))],
+    )(*(pltpu.with_memory_space_constraint(a, pltpu.HBM) for a in sources))
     mixed, modal_sum = call(
         mix_kernel, "mix", [((2 * grid, width), BF16), ((TILE, width), F32)], [VMEM] * 2
-    )(recv, mix_weights)
+    )(exchange_pairs(modal, "grid"), mix_weights)
     piece = exchange_pairs(mixed, "grid")
 
     output, parts = call(
         functools.partial(cells_kernel, 256),
         "cells",
         [((rows, width), BF16, HBM), ((TILE * grid, width), BF16)],
-        [VMEM] * 13,
+        [VMEM] * 9,
         [
             pltpu.VMEM((2 * count, width), F32),
             pltpu.VMEM((rows, 2 * hid), BF16),
@@ -493,15 +443,11 @@
     )(
         piece,
         table,
-        table_tt,
         field_here,
         cotangent_here,
-        cotangent_t,
         w_in_two,
-        w_in_back,
         b_in_two,
         w_out_two,
-        w_out_back,
         b_out_two,
         zero_row,
     )
@@ -525,7 +471,7 @@
         ],
         [VMEM] * 5,
         [pltpu.VMEM((OWN * grid, width), F32)],
-    )(exchange_pairs(own, "grid"), shares, table_tt, cotangent_here, zero_row)
+    )(exchange_pairs(own, "grid"), shares, table, cotangent_here, zero_row)
     return (
         output,
         field_grad,

time: 110 us -> 110 us (level)
  blocking collectives: 72.1 us -> 103 us
  starting transfers between devices: 18.2 us -> 0 us
  waiting for transfers between devices: 11.7 us -> 0 us
  Pallas kernels: 7.45 us -> 5.61 us
    all_to_all x4 -> x5, blocking collectives: 72.1 us -> 103 us  [exchange(): return lax.all_to_all(x, axis, 0, 0, tiled=True)]
    all_to_all x1 -> x0, starting transfers between devices: 18.2 us -> none  [exchange(): return lax.all_to_all(x, axis, 0, 0, tiled=True)]
    all_to_all x1 -> x0, waiting for transfers between devices: 11.7 us -> none  [exchange(): return lax.all_to_all(x, axis, 0, 0, tiled=True)]
    pallas_call x2 -> x1, Pallas kernels: 3.3 us -> 1.36 us  [local(): call(first_kernel, 'first', [((2 * count, width), BF16), ((2 * count, row...]
  transfers between devices with their start and end apart: 1 -> 0, of which waited for: 1 -> 0; matrix products, arithmetic and copies ran while one was open for 0% -> 0% of each run, Pallas kernels for 1% -> 0%
where the time goes in v8:
time: 110 us
  blocking collectives  103 us (94%)
  Pallas kernels  5.61 us (5%)
    all_to_all x5, blocking collectives, exchange(): return lax.all_to_all(x, axis, 0, 0, tiled=True)  103 us
    pallas_call x1, Pallas kernels, local(): call(functools.partial(cells_kernel, 256), 'cells', [((rows, width), BF16...  2.74 us

profile of v8, /device:TPU:1, one launch (start us, length us, event | category | flops | bytes accessed | tf_op | source)
XLA Modules:
  0.0 109.6 jit_solution(14903972682292531911)
XLA Ops:
  0.6 1.4 %first.1 = (bf16[128,128]{1,0:T(8,128)(2,1)S(1)}, bf16[128,1024]{1,0:T(8,128)(2,1)S(1)}, bf16[1024,128]{1,0:T(8,128)(2,1)S(1)}, bf16[1024,128]{1,0:T(8,128)(2,1)...) custom-call(s32[8]{0:T(128)} %blocks_hbm.1, ...), custom_call_target="tpu_custom_call" | custom-call | tf_op jit(solution)/shard_map/first/pallas_call | solution.py:403
  2.0 31.2 %all_to_all.31 = bf16[64,2,128]{2,1,0:T(2,128)(2,1)S(1)} all-to-all(bf16[64,2,128]{2,1,0:T(2,128)(2,1)S(1)} %bitcast.29), channel_id=1, replica_groups=mesh['grid'=64,'dp'=8] {'grid'}, dimensions={0} | all-to-all | bytes 65536 | tf_op jit(solution)/shard_map/all_to_all | solution.py:358
  33.2 0.2 mix.1
  33.4 17.2 %all_to_all.32 = bf16[64,2,128]{2,1,0:T(2,128)(2,1)S(1)} all-to-all(bf16[64,2,128]{2,1,0:T(2,128)(2,1)S(1)} %bitcast.30), channel_id=1, replica_groups=mesh['grid'=64,'dp'=8] {'grid'}, dimensions={0} | all-to-all | bytes 65536 | tf_op jit(solution)/shard_map/all_to_all | solution.py:358
  50.6 2.7 %cells.1 = (bf16[1024,128]{1,0:T(8,128)(2,1)}, bf16[512,128]{1,0:T(8,128)(2,1)S(1)}) custom-call(bf16[128,128]{1,0:T(8,128)(2,1)S(1)} %bitcast.25, bf16[128,1024]{1,0:T(8,128)(2,1)S(1)} %get-tuple-element.34.table_ref, bf16[1024,128]{1,0:T(8,128)(2,1)S(1)} %get-tuple-element.35.field_ref, bf16[1024,128]{1,0:T(8,128)(2,1)S(1)} %get-tuple-element.36.cot_ref, ...), custom_call_target="tpu_custom_call" | custom-call | tf_op jit(solution)/shard_map/cells/pallas_call | solution.py:430
  53.3 21.1 %all_to_all.33 = bf16[64,8,128]{2,1,0:T(8,128)(2,1)S(1)} all-to-all(bf16[64,8,128]{2,1,0:T(8,128)(2,1)S(1)} %bitcast.27), channel_id=1, replica_groups=mesh['grid'=64,'dp'=8] {'grid'}, dimensions={0} | all-to-all | bytes 262144 | tf_op jit(solution)/shard_map/all_to_all | solution.py:358
  74.4 0.2 share.1
  74.6 12.8 %all_to_all.34 = f32[8,16,128]{2,1,0:T(8,128)S(1)} all-to-all(f32[8,16,128]{2,1,0:T(8,128)S(1)} %bitcast.28), channel_id=1, replica_groups=mesh['grid'=64,'dp'=8] {'dp'}, dimensions={0} | all-to-all | bytes 131072 | tf_op jit(solution)/shard_map/all_to_all | solution.py:358
  87.4 0.1 total.1
  87.5 21.0 %all_to_all.35 = bf16[192,2,128]{2,1,0:T(2,128)(2,1)S(1)} all-to-all(bf16[192,2,128]{2,1,0:T(2,128)(2,1)S(1)} %bitcast.23), channel_id=1, replica_groups=mesh['grid'=64,'dp'=8] {'grid'}, dimensions={0} | all-to-all | bytes 196608 | tf_op jit(solution)/shard_map/all_to_all | solution.py:358
  108.5 1.0 final.1

commit v9 on v8

--- a/solution.py
+++ b/solution.py
@@ -185,11 +185,10 @@
 
 def gelu_pair(pre):
     k = math.sqrt(2.0 / math.pi)
-    sq = pre * pre
-    t = jnp.tanh(pre * (k + (0.044715 * k) * sq))
-    half = 0.5 * pre
-    up = 1.0 + t
-    return half * up, up * (0.5 + half * (1.0 - t) * (k + (3 * 0.044715 * k) * sq))
+    inner = k + (0.044715 * k) * (pre * pre)
+    share = 0.5 * jnp.tanh(pre * inner) + 0.5
+    gate = pre * share
+    return gate, share + gate * (1.0 - share) * (6.0 * inner - 4.0 * k)
 
 
 def cells_kernel(

time: 110 us -> 110 us (level)
  no operation moved by 1% of the time
where the time goes in v9:
time: 110 us; the launch traced here: 109 us
  blocking collectives  103 us (94%)
  Pallas kernels  5.41 us (5%)
    all_to_all x5, blocking collectives, exchange(): return lax.all_to_all(x, axis, 0, 0, tiled=True)  103 us
    pallas_call x1, Pallas kernels, local(): call(functools.partial(cells_kernel, 256), 'cells', [((rows, width), BF16...  2.54 us

profile of v9, /device:TPU:1, one launch (start us, length us, event | category | flops | bytes accessed | tf_op | source)
XLA Modules:
  0.0 109.4 jit_solution(11100568219815442013)
XLA Ops:
  0.6 1.4 %first.1 = (bf16[128,128]{1,0:T(8,128)(2,1)S(1)}, bf16[128,1024]{1,0:T(8,128)(2,1)S(1)}, bf16[1024,128]{1,0:T(8,128)(2,1)S(1)}, bf16[1024,128]{1,0:T(8,128)(2,1)...) custom-call(s32[8]{0:T(128)} %blocks_hbm.1, ...), custom_call_target="tpu_custom_call" | custom-call | tf_op jit(solution)/shard_map/first/pallas_call | solution.py:402
  2.0 31.2 %all_to_all.31 = bf16[64,2,128]{2,1,0:T(2,128)(2,1)S(1)} all-to-all(bf16[64,2,128]{2,1,0:T(2,128)(2,1)S(1)} %bitcast.29), channel_id=1, replica_groups=mesh['grid'=64,'dp'=8] {'grid'}, dimensions={0} | all-to-all | bytes 65536 | tf_op jit(solution)/shard_map/all_to_all | solution.py:357
  33.2 0.2 mix.1
  33.4 17.2 %all_to_all.32 = bf16[64,2,128]{2,1,0:T(2,128)(2,1)S(1)} all-to-all(bf16[64,2,128]{2,1,0:T(2,128)(2,1)S(1)} %bitcast.30), channel_id=1, replica_groups=mesh['grid'=64,'dp'=8] {'grid'}, dimensions={0} | all-to-all | bytes 65536 | tf_op jit(solution)/shard_map/all_to_all | solution.py:357
  50.6 2.5 %cells.1 = (bf16[1024,128]{1,0:T(8,128)(2,1)}, bf16[512,128]{1,0:T(8,128)(2,1)S(1)}) custom-call(bf16[128,128]{1,0:T(8,128)(2,1)S(1)} %bitcast.25, bf16[128,1024]{1,0:T(8,128)(2,1)S(1)} %get-tuple-element.34.table_ref, bf16[1024,128]{1,0:T(8,128)(2,1)S(1)} %get-tuple-element.35.field_ref, bf16[1024,128]{1,0:T(8,128)(2,1)S(1)} %get-tuple-element.36.cot_ref, ...), custom_call_target="tpu_custom_call" | custom-call | tf_op jit(solution)/shard_map/cells/pallas_call | solution.py:429
  53.1 21.0 %all_to_all.33 = bf16[64,8,128]{2,1,0:T(8,128)(2,1)S(1)} all-to-all(bf16[64,8,128]{2,1,0:T(8,128)(2,1)S(1)} %bitcast.27), channel_id=1, replica_groups=mesh['grid'=64,'dp'=8] {'grid'}, dimensions={0} | all-to-all | bytes 262144 | tf_op jit(solution)/shard_map/all_to_all | solution.py:357
  74.2 0.2 share.1
  74.4 12.8 %all_to_all.34 = f32[8,16,128]{2,1,0:T(8,128)S(1)} all-to-all(f32[8,16,128]{2,1,0:T(8,128)S(1)} %bitcast.28), channel_id=1, replica_groups=mesh['grid'=64,'dp'=8] {'dp'}, dimensions={0} | all-to-all | bytes 131072 | tf_op jit(solution)/shard_map/all_to_all | solution.py:357
  87.2 0.1 total.1
  87.3 21.0 %all_to_all.35 = bf16[192,2,128]{2,1,0:T(2,128)(2,1)S(1)} all-to-all(bf16[192,2,128]{2,1,0:T(2,128)(2,1)S(1)} %bitcast.23), channel_id=1, replica_groups=mesh['grid'=64,'dp'=8] {'grid'}, dimensions={0} | all-to-all | bytes 196608 | tf_op jit(solution)/shard_map/all_to_all | solution.py:357
  108.3 1.0 final.1

commit v10 on v9

--- a/solution.py
+++ b/solution.py
@@ -138,7 +138,7 @@
     modal = dot(table_ref[...], field_ref[...])
     wide_ref[pl.ds(0, count, stride=2), :] = modal[:count]
     wide_ref[pl.ds(1, count, stride=2), :] = modal[count:]
-    modal_ref[...] = wide_ref[...].astype(BF16)
+    modal_ref[...] = wide_ref[...]
     zero_row_ref[...] = jnp.where(modes == 0, 1.0, 0.0)
     at = jnp.int32(0)
     for b in range(kblocks):
@@ -258,7 +258,7 @@
         )
     ):
         sums_ref[pl.ds(r, count, stride=TILE), :] = block
-    parts_ref[...] = sums_ref[...].astype(BF16)
+    parts_ref[...] = sums_ref[...]
     for copy in copies:
         copy.wait()
 
@@ -403,7 +403,7 @@
         first_kernel,
         "first",
         [
-            ((2 * count, width), BF16),
+            ((2 * count, width), F32),
             ((2 * count, rows), BF16),
             ((rows, width), BF16),
             ((rows, width), BF16),
@@ -429,7 +429,7 @@
     output, parts = call(
         functools.partial(cells_kernel, 256),
         "cells",
-        [((rows, width), BF16, HBM), ((TILE * grid, width), BF16)],
+        [((rows, width), BF16, HBM), ((TILE * grid, width), F32)],
         [VMEM] * 9,
         [
             pltpu.VMEM((2 * count, width), F32),

time: 110 us -> 116 us (1.055)
  blocking collectives: 103 us -> 110 us
    all_to_all x5, blocking collectives: 103 us -> 110 us  [exchange(): return lax.all_to_all(x, axis, 0, 0, tiled=True)]
where the time goes in v10:
time: 116 us
  blocking collectives  110 us (95%)
  Pallas kernels  5.34 us (5%)
    all_to_all x5, blocking collectives, exchange(): return lax.all_to_all(x, axis, 0, 0, tiled=True)  110 us
    pallas_call x1, Pallas kernels, local(): call(functools.partial(cells_kernel, 256), 'cells', [((rows, width), BF16...  2.49 us

profile of v10, /device:TPU:1, one launch (start us, length us, event | category | flops | bytes accessed | tf_op | source)
XLA Modules:
  0.0 115.7 jit_solution(4153597399695160946)
XLA Ops:
  0.6 1.4 %first.1 = (f32[128,128]{1,0:T(8,128)S(1)}, bf16[128,1024]{1,0:T(8,128)(2,1)S(1)}, bf16[1024,128]{1,0:T(8,128)(2,1)S(1)}, bf16[1024,128]{1,0:T(8,128)(2,1)S(1)},...) custom-call(s32[8]{0:T(128)} %blocks_hbm.1, ...), custom_call_target="tpu_custom_call" | custom-call | tf_op jit(solution)/shard_map/first/pallas_call | solution.py:402
  2.0 32.6 %all_to_all.31 = f32[64,2,128]{2,1,0:T(2,128)S(1)} all-to-all(f32[64,2,128]{2,1,0:T(2,128)S(1)} %bitcast.28), channel_id=1, replica_groups=mesh['grid'=64,'dp'=8] {'grid'}, dimensions={0} | all-to-all | bytes 131072 | tf_op jit(solution)/shard_map/all_to_all | solution.py:357
  34.6 0.2 mix.1
  34.7 17.0 %all_to_all.32 = bf16[64,2,128]{2,1,0:T(2,128)(2,1)S(1)} all-to-all(bf16[64,2,128]{2,1,0:T(2,128)(2,1)S(1)} %bitcast.30), channel_id=1, replica_groups=mesh['grid'=64,'dp'=8] {'grid'}, dimensions={0} | all-to-all | bytes 65536 | tf_op jit(solution)/shard_map/all_to_all | solution.py:357
  51.7 2.5 %cells.1 = (bf16[1024,128]{1,0:T(8,128)(2,1)}, f32[512,128]{1,0:T(8,128)S(1)}) custom-call(bf16[128,128]{1,0:T(8,128)(2,1)S(1)} %bitcast.27, bf16[128,1024]{1,0:T(8,128)(2,1)S(1)} %get-tuple-element.34.table_ref, bf16[1024,128]{1,0:T(8,128)(2,1)S(1)} %get-tuple-element.35.field_ref, bf16[1024,128]{1,0:T(8,128)(2,1)S(1)} %get-tuple-element.36.cot_ref, ...), custom_call_target="tpu_custom_call" | custom-call | tf_op jit(solution)/shard_map/cells/pallas_call | solution.py:429
  54.2 26.2 %all_to_all.33 = f32[64,8,128]{2,1,0:T(8,128)S(1)} all-to-all(f32[64,8,128]{2,1,0:T(8,128)S(1)} %bitcast.25), channel_id=1, replica_groups=mesh['grid'=64,'dp'=8] {'grid'}, dimensions={0} | all-to-all | bytes 524288 | tf_op jit(solution)/shard_map/all_to_all | solution.py:357
  80.4 0.2 share.1
  80.6 12.9 %all_to_all.34 = f32[8,16,128]{2,1,0:T(8,128)S(1)} all-to-all(f32[8,16,128]{2,1,0:T(8,128)S(1)} %bitcast.29), channel_id=1, replica_groups=mesh['grid'=64,'dp'=8] {'dp'}, dimensions={0} | all-to-all | bytes 131072 | tf_op jit(solution)/shard_map/all_to_all | solution.py:357
  93.4 0.1 total.1
  93.5 21.1 %all_to_all.35 = bf16[192,2,128]{2,1,0:T(2,128)(2,1)S(1)} all-to-all(bf16[192,2,128]{2,1,0:T(2,128)(2,1)S(1)} %bitcast.23), channel_id=1, replica_groups=mesh['grid'=64,'dp'=8] {'grid'}, dimensions={0} | all-to-all | bytes 196608 | tf_op jit(solution)/shard_map/all_to_all | solution.py:357
  114.6 1.0 final.1

commit v11 on v9

--- a/solution.py
+++ b/solution.py
@@ -309,31 +309,55 @@
     table_ref,
     cot_ref,
     zero_row_ref,
+    fgrad_hbm,
+    spectral_hbm,
+    win_hbm,
+    wout_hbm,
+    bin_hbm,
+    bout_hbm,
+    wide_ref,
     fgrad_ref,
     spectral_ref,
     win_ref,
     wout_ref,
     bin_ref,
     bout_ref,
-    wide_ref,
+    sems,
 ):
     count = table_ref.shape[0] // 2
+    half = table_ref.shape[1] // 2
+    copies = []
+
+    def send(source, target):
+        copies.append(pltpu.make_async_copy(source, target, sems.at[len(copies)]))
+        copies[-1].start()
+
     wide_ref[...] = recv_ref[...].astype(F32)
     rows = [every(wide_ref, r, count, OWN) for r in range(OWN)]
     grad_in = jnp.concatenate(rows[:2], axis=0).astype(BF16)
-    back = dot_on(table_ref[...], grad_in, 0, 0)
-    fgrad_ref[...] = (cot_ref[...].astype(F32) + back).astype(BF16)
+    for i in range(2):
+        span = pl.ds(i * half, half)
+        back = dot_on(table_ref[:, span], grad_in, 0, 0)
+        fgrad_ref[span, :] = (cot_ref[span, :].astype(F32) + back).astype(BF16)
+        send(fgrad_ref.at[span], fgrad_hbm.at[span])
     win_ref[:, :LANES] = rows[2]
     win_ref[:, LANES:] = rows[3]
+    send(win_ref, win_hbm)
     wout_ref[:, :LANES] = rows[4]
     wout_ref[:, LANES:] = rows[5]
+    send(wout_ref, wout_hbm)
+    spectral_sums(scale, shares_ref, spectral_ref)
+    send(spectral_ref, spectral_hbm)
     n = shares_ref.shape[0] // (2 * TILE)
     for r in range(2):
         b_in = jnp.sum(every(shares_ref, OWN + r, n, 2 * TILE), axis=0, keepdims=True)
         bin_ref[:, r * LANES : (r + 1) * LANES] = b_in * scale
+    send(bin_ref, bin_hbm)
     b_out = jnp.sum(jnp.where(zero_row_ref[...] > 0.0, rows[1], 0.0), axis=0, keepdims=True)
     bout_ref[...] = (b_out + pltpu.roll(b_out, LANES // 2, 1))[:, : bout_ref.shape[1]]
-    spectral_sums(scale, shares_ref, spectral_ref)
+    send(bout_ref, bout_hbm)
+    for copy in copies:
+        copy.wait()
 
 
 def spectral_sums(scale, shares_ref, out_ref):
@@ -457,19 +481,22 @@
     (own,) = call(
         functools.partial(total_kernel, inv_cols), "total", [((OWN * grid, width), BF16)], [VMEM] * 3
     )(shares, grad_in, zero_own)
+    results = [
+        ((rows, width), BF16),
+        ((2, chans, chans), F32),
+        ((chans, hid), F32),
+        ((chans, hid), F32),
+        ((1, hid), F32),
+        ((1, chans), F32),
+    ]
     field_grad, spectral_grad, w_in_grad, w_out_grad, b_in_grad, b_out_grad = call(
         functools.partial(final_kernel, inv_cols),
         "final",
-        [
-            ((rows, width), BF16),
-            ((2, chans, chans), F32),
-            ((chans, hid), F32),
-            ((chans, hid), F32),
-            ((1, hid), F32),
-            ((1, chans), F32),
-        ],
+        [(shape, dtype, HBM) for shape, dtype in results],
         [VMEM] * 5,
-        [pltpu.VMEM((OWN * grid, width), F32)],
+        [pltpu.VMEM((OWN * grid, width), F32)]
+        + [pltpu.VMEM(shape, dtype) for shape, dtype in results]
+        + [pltpu.SemaphoreType.DMA((len(results) + 1,))],
     )(exchange_pairs(own, "grid"), shares, table, cotangent_here, zero_row)
     return (
         output,

time: 110 us -> 110 us (level)
  no operation moved by 1% of the time
where the time goes in v11:
time: 110 us; the launch traced here: 109 us
  blocking collectives  103 us (94%)
  Pallas kernels  5.44 us (5%)
    all_to_all x5, blocking collectives, exchange(): return lax.all_to_all(x, axis, 0, 0, tiled=True)  103 us
    pallas_call x1, Pallas kernels, local(): call(functools.partial(cells_kernel, 256), 'cells', [((rows, width), BF16...  2.54 us

profile of v11, /device:TPU:1, one launch (start us, length us, event | category | flops | bytes accessed | tf_op | source)
XLA Modules:
  0.0 109.4 jit_solution(14458932613094494272)
XLA Ops:
  0.6 1.4 %first.1 = (bf16[128,128]{1,0:T(8,128)(2,1)S(1)}, bf16[128,1024]{1,0:T(8,128)(2,1)S(1)}, bf16[1024,128]{1,0:T(8,128)(2,1)S(1)}, bf16[1024,128]{1,0:T(8,128)(2,1)...) custom-call(s32[8]{0:T(128)} %blocks_hbm.1, ...), custom_call_target="tpu_custom_call" | custom-call | tf_op jit(solution)/shard_map/first/pallas_call | solution.py:426
  2.0 31.2 %all_to_all.31 = bf16[64,2,128]{2,1,0:T(2,128)(2,1)S(1)} all-to-all(bf16[64,2,128]{2,1,0:T(2,128)(2,1)S(1)} %bitcast.29), channel_id=1, replica_groups=mesh['grid'=64,'dp'=8] {'grid'}, dimensions={0} | all-to-all | bytes 65536 | tf_op jit(solution)/shard_map/all_to_all | solution.py:381
  33.2 0.2 mix.1
  33.4 17.2 %all_to_all.32 = bf16[64,2,128]{2,1,0:T(2,128)(2,1)S(1)} all-to-all(bf16[64,2,128]{2,1,0:T(2,128)(2,1)S(1)} %bitcast.30), channel_id=1, replica_groups=mesh['grid'=64,'dp'=8] {'grid'}, dimensions={0} | all-to-all | bytes 65536 | tf_op jit(solution)/shard_map/all_to_all | solution.py:381
  50.6 2.5 %cells.1 = (bf16[1024,128]{1,0:T(8,128)(2,1)}, bf16[512,128]{1,0:T(8,128)(2,1)S(1)}) custom-call(bf16[128,128]{1,0:T(8,128)(2,1)S(1)} %bitcast.25, bf16[128,1024]{1,0:T(8,128)(2,1)S(1)} %get-tuple-element.34.table_ref, bf16[1024,128]{1,0:T(8,128)(2,1)S(1)} %get-tuple-element.35.field_ref, bf16[1024,128]{1,0:T(8,128)(2,1)S(1)} %get-tuple-element.36.cot_ref, ...), custom_call_target="tpu_custom_call" | custom-call | tf_op jit(solution)/shard_map/cells/pallas_call | solution.py:453
  53.1 21.0 %all_to_all.33 = bf16[64,8,128]{2,1,0:T(8,128)(2,1)S(1)} all-to-all(bf16[64,8,128]{2,1,0:T(8,128)(2,1)S(1)} %bitcast.27), channel_id=1, replica_groups=mesh['grid'=64,'dp'=8] {'grid'}, dimensions={0} | all-to-all | bytes 262144 | tf_op jit(solution)/shard_map/all_to_all | solution.py:381
  74.2 0.2 share.1
  74.4 12.8 %all_to_all.34 = f32[8,16,128]{2,1,0:T(8,128)S(1)} all-to-all(f32[8,16,128]{2,1,0:T(8,128)S(1)} %bitcast.28), channel_id=1, replica_groups=mesh['grid'=64,'dp'=8] {'dp'}, dimensions={0} | all-to-all | bytes 131072 | tf_op jit(solution)/shard_map/all_to_all | solution.py:381
  87.2 0.1 total.1
  87.3 21.0 %all_to_all.35 = bf16[192,2,128]{2,1,0:T(2,128)(2,1)S(1)} all-to-all(bf16[192,2,128]{2,1,0:T(2,128)(2,1)S(1)} %bitcast.23), channel_id=1, replica_groups=mesh['grid'=64,'dp'=8] {'grid'}, dimensions={0} | all-to-all | bytes 196608 | tf_op jit(solution)/shard_map/all_to_all | solution.py:381
  108.3 1.1 final.1

commit v12 on v9

--- a/solution.py
+++ b/solution.py
@@ -77,11 +77,9 @@
     wout_hbm,
     bin_hbm,
     bout_hbm,
-    cot_hbm,
     modal_ref,
     table_ref,
     field_ref,
-    cot_ref,
     mix_ref,
     back_ref,
     win_two_ref,
@@ -107,7 +105,6 @@
         (wout_hbm, wout_ref),
         (bin_hbm, bin_ref),
         (bout_hbm, bout_ref),
-        (cot_hbm, cot_ref),
     )
     copies = [pltpu.make_async_copy(a, b, sems.at[i]) for i, (a, b) in enumerate(pairs)]
     for copy in copies:
@@ -384,13 +381,11 @@
         w_out.T,
         b_in.reshape(1, hid),
         b_out.reshape(1, chans),
-        cotangent,
     )
     (
         modal,
         table,
         field_here,
-        cotangent_here,
         mix_weights,
         back_weights,
         w_in_two,
@@ -405,7 +400,6 @@
         [
             ((2 * count, width), BF16),
             ((2 * count, rows), BF16),
-            ((rows, width), BF16),
             ((rows, width), BF16),
             ((width, 2 * width), BF16),
             ((2 * width, width), BF16),
@@ -443,7 +437,7 @@
         piece,
         table,
         field_here,
-        cotangent_here,
+        cotangent,
         w_in_two,
         b_in_two,
         w_out_two,
@@ -470,7 +464,7 @@
         ],
         [VMEM] * 5,
         [pltpu.VMEM((OWN * grid, width), F32)],
-    )(exchange_pairs(own, "grid"), shares, table, cotangent_here, zero_row)
+    )(exchange_pairs(own, "grid"), shares, table, cotangent, zero_row)
     return (
         output,
         field_grad,

time: 110 us -> 110 us (level)
  no operation moved by 1% of the time
where the time goes in v12:
time: 110 us; the launch traced here: 109 us
  blocking collectives  103 us (94%)
  Pallas kernels  5.47 us (5%)
    all_to_all x5, blocking collectives, exchange(): return lax.all_to_all(x, axis, 0, 0, tiled=True)  103 us
    pallas_call x1, Pallas kernels, local(): call(functools.partial(cells_kernel, 256), 'cells', [((rows, width), BF16...  2.49 us

profile of v12, /device:TPU:1, one launch (start us, length us, event | category | flops | bytes accessed | tf_op | source)
XLA Modules:
  0.0 109.4 jit_solution(3544420154681780577)
XLA Ops:
  0.6 0.0 copy-start
  0.6 1.5 %first.1 = (bf16[128,128]{1,0:T(8,128)(2,1)S(1)}, bf16[128,1024]{1,0:T(8,128)(2,1)S(1)}, bf16[1024,128]{1,0:T(8,128)(2,1)S(1)}, bf16[128,256]{1,0:T(8,128)(2,1)S...) custom-call(s32[8]{0:T(128)} %blocks_hbm.1, ...), custom_call_target="tpu_custom_call" | custom-call | tf_op jit(solution)/shard_map/first/pallas_call | solution.py:397
  2.1 31.2 %all_to_all.31 = bf16[64,2,128]{2,1,0:T(2,128)(2,1)S(1)} all-to-all(bf16[64,2,128]{2,1,0:T(2,128)(2,1)S(1)} %bitcast.29), channel_id=1, replica_groups=mesh['grid'=64,'dp'=8] {'grid'}, dimensions={0} | all-to-all | bytes 65536 | tf_op jit(solution)/shard_map/all_to_all | solution.py:354
  33.4 0.2 mix.1
  33.5 17.2 %all_to_all.32 = bf16[64,2,128]{2,1,0:T(2,128)(2,1)S(1)} all-to-all(bf16[64,2,128]{2,1,0:T(2,128)(2,1)S(1)} %bitcast.30), channel_id=1, replica_groups=mesh['grid'=64,'dp'=8] {'grid'}, dimensions={0} | all-to-all | bytes 65536 | tf_op jit(solution)/shard_map/all_to_all | solution.py:354
  50.7 0.0 copy-done
  50.7 2.5 %cells.1 = (bf16[1024,128]{1,0:T(8,128)(2,1)}, bf16[512,128]{1,0:T(8,128)(2,1)S(1)}) custom-call(bf16[128,128]{1,0:T(8,128)(2,1)S(1)} %bitcast.25, bf16[128,1024]{1,0:T(8,128)(2,1)S(1)} %get-tuple-element.33.table_ref, bf16[1024,128]{1,0:T(8,128)(2,1)S(1)} %get-tuple-element.34.field_ref, bf16[1024,128]{1,0:T(8,128)(2,1)S(1)} %copy-done, ...), custom_call_target="tpu_custom_call" | custom-call | tf_op jit(solution)/shard_map/cells/pallas_call | solution.py:423
  53.2 21.1 %all_to_all.33 = bf16[64,8,128]{2,1,0:T(8,128)(2,1)S(1)} all-to-all(bf16[64,8,128]{2,1,0:T(8,128)(2,1)S(1)} %bitcast.27), channel_id=1, replica_groups=mesh['grid'=64,'dp'=8] {'grid'}, dimensions={0} | all-to-all | bytes 262144 | tf_op jit(solution)/shard_map/all_to_all | solution.py:354
  74.3 0.2 share.1
  74.5 12.8 %all_to_all.34 = f32[8,16,128]{2,1,0:T(8,128)S(1)} all-to-all(f32[8,16,128]{2,1,0:T(8,128)S(1)} %bitcast.28), channel_id=1, replica_groups=mesh['grid'=64,'dp'=8] {'dp'}, dimensions={0} | all-to-all | bytes 131072 | tf_op jit(solution)/shard_map/all_to_all | solution.py:354
  87.3 0.1 total.1
  87.4 21.0 %all_to_all.35 = bf16[192,2,128]{2,1,0:T(2,128)(2,1)S(1)} all-to-all(bf16[192,2,128]{2,1,0:T(2,128)(2,1)S(1)} %bitcast.23), channel_id=1, replica_groups=mesh['grid'=64,'dp'=8] {'grid'}, dimensions={0} | all-to-all | bytes 196608 | tf_op jit(solution)/shard_map/all_to_all | solution.py:354
  108.4 1.0 final.1
Async XLA Ops:
  0.6 50.1 %copy-start = (bf16[1024,128]{1,0:T(8,128)(2,1)S(1)}, bf16[1024,128]{1,0:T(8,128)(2,1)}, u32[]{:S(2)}) copy-start(bf16[1024,128]{1,0:T(8,128)(2,1)} %cot_ref.3) | copy-start | bytes 786436

commit v13 on v9

--- a/solution.py
+++ b/solution.py
@@ -427,7 +427,7 @@
     piece = exchange_pairs(mixed, "grid")
 
     output, parts = call(
-        functools.partial(cells_kernel, 256),
+        functools.partial(cells_kernel, 1024),
         "cells",
         [((rows, width), BF16, HBM), ((TILE * grid, width), BF16)],
         [VMEM] * 9,
@@ -437,7 +437,7 @@
             pltpu.VMEM((rows, 2 * hid), BF16),
             pltpu.VMEM((rows, width), BF16),
             pltpu.VMEM((TILE * grid, width), F32),
-            pltpu.SemaphoreType.DMA((rows // 256,)),
+            pltpu.SemaphoreType.DMA((rows // 1024,)),
         ],
     )(
         piece,

time: 110 us -> 110 us (level)
  no operation moved by 1% of the time
where the time goes in v13:
time: 110 us
  blocking collectives  103 us (94%)
  Pallas kernels  5.64 us (5%)
    all_to_all x5, blocking collectives, exchange(): return lax.all_to_all(x, axis, 0, 0, tiled=True)  103 us
    pallas_call x1, Pallas kernels, local(): call(functools.partial(cells_kernel, 1024), 'cells', [((rows, width), BF1...  2.77 us

profile of v13, /device:TPU:1, one launch (start us, length us, event | category | flops | bytes accessed | tf_op | source)
XLA Modules:
  0.0 109.6 jit_solution(17122629899515312658)
XLA Ops:
  0.6 1.4 %first.1 = (bf16[128,128]{1,0:T(8,128)(2,1)S(1)}, bf16[128,1024]{1,0:T(8,128)(2,1)S(1)}, bf16[1024,128]{1,0:T(8,128)(2,1)S(1)}, bf16[1024,128]{1,0:T(8,128)(2,1)...) custom-call(s32[8]{0:T(128)} %blocks_hbm.1, ...), custom_call_target="tpu_custom_call" | custom-call | tf_op jit(solution)/shard_map/first/pallas_call | solution.py:402
  2.0 31.2 %all_to_all.31 = bf16[64,2,128]{2,1,0:T(2,128)(2,1)S(1)} all-to-all(bf16[64,2,128]{2,1,0:T(2,128)(2,1)S(1)} %bitcast.29), channel_id=1, replica_groups=mesh['grid'=64,'dp'=8] {'grid'}, dimensions={0} | all-to-all | bytes 65536 | tf_op jit(solution)/shard_map/all_to_all | solution.py:357
  33.2 0.2 mix.1
  33.4 17.2 %all_to_all.32 = bf16[64,2,128]{2,1,0:T(2,128)(2,1)S(1)} all-to-all(bf16[64,2,128]{2,1,0:T(2,128)(2,1)S(1)} %bitcast.30), channel_id=1, replica_groups=mesh['grid'=64,'dp'=8] {'grid'}, dimensions={0} | all-to-all | bytes 65536 | tf_op jit(solution)/shard_map/all_to_all | solution.py:357
  50.6 2.8 %cells.1 = (bf16[1024,128]{1,0:T(8,128)(2,1)}, bf16[512,128]{1,0:T(8,128)(2,1)S(1)}) custom-call(bf16[128,128]{1,0:T(8,128)(2,1)S(1)} %bitcast.25, bf16[128,1024]{1,0:T(8,128)(2,1)S(1)} %get-tuple-element.34.table_ref, bf16[1024,128]{1,0:T(8,128)(2,1)S(1)} %get-tuple-element.35.field_ref, bf16[1024,128]{1,0:T(8,128)(2,1)S(1)} %get-tuple-element.36.cot_ref, ...), custom_call_target="tpu_custom_call" | custom-call | tf_op jit(solution)/shard_map/cells/pallas_call | solution.py:429
  53.4 21.0 %all_to_all.33 = bf16[64,8,128]{2,1,0:T(8,128)(2,1)S(1)} all-to-all(bf16[64,8,128]{2,1,0:T(8,128)(2,1)S(1)} %bitcast.27), channel_id=1, replica_groups=mesh['grid'=64,'dp'=8] {'grid'}, dimensions={0} | all-to-all | bytes 262144 | tf_op jit(solution)/shard_map/all_to_all | solution.py:357
  74.4 0.2 share.1
  74.6 12.8 %all_to_all.34 = f32[8,16,128]{2,1,0:T(8,128)S(1)} all-to-all(f32[8,16,128]{2,1,0:T(8,128)S(1)} %bitcast.28), channel_id=1, replica_groups=mesh['grid'=64,'dp'=8] {'dp'}, dimensions={0} | all-to-all | bytes 131072 | tf_op jit(solution)/shard_map/all_to_all | solution.py:357
  87.5 0.1 total.1
  87.6 21.0 %all_to_all.35 = bf16[192,2,128]{2,1,0:T(2,128)(2,1)S(1)} all-to-all(bf16[192,2,128]{2,1,0:T(2,128)(2,1)S(1)} %bitcast.23), channel_id=1, replica_groups=mesh['grid'=64,'dp'=8] {'grid'}, dimensions={0} | all-to-all | bytes 196608 | tf_op jit(solution)/shard_map/all_to_all | solution.py:357
  108.6 1.0 final.1
